TPU v7x, 32 devices: a whole 2x2x4 slice. The times are simulated.
32 devices in a mesh: grow: 8 (over z, y), lat: 4 (over x, core).
Axes of the slice: x: 2, y: 2, z: 4, core: 2. Of those that a mesh axis runs over, the one named last changes fastest.
Arguments:
- labels: int32 [128, 128, 128], P('grow', 'lat'), may hold values from 0 to 3
- roughness: float32 [4, 128, 128, 128], P(None, 'grow', 'lat'), may hold values from 0.1 to 1
- potential: float32 [2, 128, 128, 128], P(None, 'grow', 'lat'), may hold values from -3 to 3
- grad_coef: float32 [4, 3], replicated, may hold values from 0.2 to 1
- composition: float32 [4, 2], replicated, may hold values from -2 to 2
- latent: float32 [4], replicated, may hold values from 0.5 to 2
- diffusivity: float32 [2], replicated, may hold values from 0.5 to 2
- melt_table: float32 [16, 2], replicated, may hold values from -1 to 1
- melt_index: int32 [4, 8, 128, 128], P(None, None, 'lat'), may hold values from 0 to 15
Outputs:
- phases: float32 [4, 128, 128, 128], P(None, 'grow', 'lat')
- potentials: float32 [2, 128, 128, 128], P(None, 'grow', 'lat')
All inputs are finite; a program needn't handle non-finite values.
Results may differ from a plain program's by a relative error of at most 0.00025.
Values sent between devices are 32-bit elements; how exact they have to be, the bound alone decides.
No kernel may reach another device: no remote copies, remote signals or barrier semaphores. Data moves between devices by JAX's collectives and lax.ppermute only.
A program may use at most 64 MiB of HBM per device.

v0:
```python
import jax
import jax.numpy as jnp
from jax import lax
from jax.sharding import PartitionSpec as P

STEPS = 4
ROUNDS = 4
SHIFT = 8


def with_halo(array, sides, width):
    for axis, dim in sides:
        peers, length = (lax.axis_size(axis), array.shape[dim])
        up = [(i, (i + 1) % peers) for i in range(peers)]
        down = [(j, i) for i, j in up]
        last = lax.slice_in_dim(array, length - width, length, axis=dim)
        leading = lax.slice_in_dim(array, 0, width, axis=dim)
        before = lax.ppermute(last, axis, up)
        after = lax.ppermute(leading, axis, down)
        array = jnp.concatenate([before, array, after], axis=dim)
    return array


def passed_along(block, axis, distance):
    devices = range(lax.axis_size(axis))
    route = [(i - distance, i) for i in devices if i - distance in devices]
    return lax.ppermute(block, axis, route)


def advance(padded, grad_coef, composition, latent, diffusivity, first, total):
    center = padded[:, 1:-1, 1:-1]
    gsum = padded[:, 2:, 1:-1] + padded[:, :-2, 1:-1] - 2.0 * center
    xsum = padded[:, 1:-1, 2:] + padded[:, 1:-1, :-2] - 2.0 * center
    ysum = jnp.roll(center, 1, 3) + jnp.roll(center, -1, 3) - 2.0 * center
    fracs = center[:4]
    chem = center[4:]
    lap_phi = (
        grad_coef[:, 0][:, None, None, None] * gsum[:4]
        + grad_coef[:, 1][:, None, None, None] * xsum[:4]
        + grad_coef[:, 2][:, None, None, None] * ysum[:4]
    )
    lap_mu = gsum[4:] + xsum[4:] + ysum[4:]
    rows = center.shape[1]
    theta = ((jnp.arange(rows, dtype=jnp.int32) + first).astype(jnp.float32) - 0.5 * total) / total
    psi = (
        composition[:, 0][:, None, None, None] * chem[0]
        + composition[:, 1][:, None, None, None] * chem[1]
        + latent[:, None, None, None] * theta[None, :, None, None]
    )
    summed = jnp.sum(fracs, axis=0)
    rhs = lap_phi - 1.0 * (summed[None] - fracs) - psi
    rhs = rhs - jnp.mean(rhs, axis=0)[None]
    trial = fracs + 0.04 * rhs
    clipped = jnp.clip(trial, 0.0, 1.0)
    newphi = clipped / jnp.sum(clipped, axis=0)[None]
    change = newphi - fracs
    release = jnp.stack(
        [
            jnp.sum(composition[:, 0][:, None, None, None] * change, axis=0),
            jnp.sum(composition[:, 1][:, None, None, None] * change, axis=0),
        ]
    )
    newmu = chem + 0.04 * diffusivity[:, None, None, None] * lap_mu - release
    return jnp.concatenate([newphi, newmu], axis=0)


def settle(padded, margin, block):
    place = lax.axis_index("grow")
    final = lax.axis_size("grow") - 1
    rows = lax.broadcasted_iota(jnp.int32, (1, padded.shape[1], 1, 1), 1)
    lower = padded[:, margin : margin + 1]
    upper = padded[:, margin + block - 1 : margin + block]
    out = jnp.where((place == 0) & (rows < margin), lower, padded)
    return jnp.where((place == final) & (rows >= margin + block), upper, out)


def melt_planes(melt_table, melt_index, turn):
    rowsmelt = melt_table.shape[0]
    table_cols = jnp.transpose(melt_table)
    chosen = lax.dynamic_index_in_dim(melt_index, turn, 0, keepdims=False)
    entries = jnp.arange(rowsmelt, dtype=jnp.int32)[:, None, None, None]
    picks = (chosen[None] == entries).astype(jnp.float32)
    melt_mu = jnp.tensordot(table_cols, picks, axes=1, precision=lax.Precision.HIGHEST)
    zeros = jnp.zeros(chosen.shape, jnp.float32)
    return jnp.concatenate([jnp.stack([zeros, zeros, zeros, zeros + 1.0]), melt_mu], axis=0)


def on_device(
    labels,
    roughness,
    potential,
    grad_coef,
    composition,
    latent,
    diffusivity,
    melt_table,
    melt_index,
):
    block = labels.shape[0]
    total = float(block * lax.axis_size("grow"))
    place = lax.axis_index("grow")
    final = lax.axis_size("grow") - 1
    kinds = jnp.arange(4, dtype=jnp.int32)[:, None, None, None]
    onehot = (labels[None] == kinds).astype(jnp.float32)
    fracs = (3.0 * onehot + roughness) / (3.0 + jnp.sum(roughness, axis=0))[None]
    start = jnp.concatenate([fracs, potential], axis=0)

    def one_round(turn, state):
        base = place * block + SHIFT * turn
        fresh = melt_planes(melt_table, melt_index, turn)
        for step in range(STEPS):
            padded = with_halo(state, (("grow", 1), ("lat", 2)), 1)
            padded = settle(padded, 1, block)
            state = advance(padded, grad_coef, composition, latent, diffusivity, base, total)
        incoming = passed_along(state[:, :SHIFT], "grow", -1)
        incoming = jnp.where(place == final, fresh, incoming)
        return jnp.concatenate([state[:, SHIFT:], incoming], axis=1)

    state = lax.fori_loop(0, ROUNDS, one_round, start)
    return (state[:4], state[4:])


def solution(mesh):
    placed = (
        P("grow", "lat", None),
        P(None, "grow", "lat", None),
        P(None, "grow", "lat", None),
        P(),
        P(),
        P(),
        P(),
        P(),
        P(None, None, "lat", None),
    )
    return jax.shard_map(
        on_device,
        mesh=mesh,
        in_specs=placed,
        out_specs=(P(None, "grow", "lat", None), P(None, "grow", "lat", None)),
        check_vma=False,
    )
```

profile of v0, /device:TPU:17, one launch (start us, length us, event | category | flops | bytes accessed | tf_op | source)
XLA Modules:
  0.0 493.8 jit_solution(17111343043257326900)
XLA Ops:
  5.6 485.7 %while.15 = (s32[]{:T(128)}, f32[6,16,32,128]{3,0,2,1:T(8,128)S(1)}, f32[4,3]{0,1:T(4,128)S(1)}, f32[4,2]{0,1:T(2,128)S(1)}, f32[4]{0:T(128)S(1)}, /*index=5*/s3...) while((s32[]{:T(128)}, ...), condition=%wide.region_22.23_spmd, body=%wide.region_1.22_spmd.sunk | while | flops 79381744 | bytes 223798240 | solution.py:119
  8.4 2.8 collective-permute-done
  11.4 3.7 collective-permute-done.1
  34.3 2.9 collective-permute-done.5
  61.2 3.5 collective-permute-start.10
  81.6 2.8 collective-permute-done.12
  102.8 4.6 collective-permute-start.16
  109.1 14.2 %collective-permute-done.16 = f32[6,8,32,128]{3,2,1,0:T(8,128)S(1)} collective-permute-done((f32[6,8,32,128]{3,2,1,0:T(8,128)S(1)}, f32[6,8,32,128]{3,2,1,0:T(8,128)S(1)}, u32[]{:S(2)}, u32[]{:S(2)}) %collective-permute-start.16) | collective-permute-done | bytes 786464 | tf_op jit(solution)/shard_map/while/body/eval_jaxpr/ppermute | solution.py:27
  130.3 3.2 collective-permute-done.1
  135.8 2.8 collective-permute-done.2
  151.7 4.3 collective-permute-done.4
  173.2 3.1 collective-permute-start.8
  181.1 3.1 collective-permute-start.10
  204.4 3.2 collective-permute-done.13
  225.3 4.2 collective-permute-start.16
  231.2 14.1 %collective-permute-done.16 = f32[6,8,32,128]{3,2,1,0:T(8,128)S(1)} collective-permute-done((f32[6,8,32,128]{3,2,1,0:T(8,128)S(1)}, f32[6,8,32,128]{3,2,1,0:T(8,128)S(1)}, u32[]{:S(2)}, u32[]{:S(2)}) %collective-permute-start.16) | collective-permute-done | bytes 786464 | tf_op jit(solution)/shard_map/while/body/eval_jaxpr/ppermute | solution.py:27
  252.2 3.9 collective-permute-start.2
  277.2 3.0 collective-permute-done.5
  283.3 2.8 collective-permute-done.6
  299.4 6.0 %collective-permute-done.8 = f32[6,1,32,128]{3,0,2,1:T(8,128)S(1)} collective-permute-done((f32[6,1,32,128]{3,0,2,1:T(8,128)S(1)}, f32[6,1,32,128]{3,0,2,1:T(8,128)S(1)}, u32[]{:S(2)}, u32[]{:S(2)}) %collective-permute-start.8) | collective-permute-done | bytes 98336 | tf_op jit(solution)/shard_map/while/body/eval_jaxpr/ppermute | solution.py:19
  325.1 3.1 collective-permute-done.13
  328.2 3.1 collective-permute-start.14
  345.9 4.6 collective-permute-start.16
  352.2 13.5 %collective-permute-done.16 = f32[6,8,32,128]{3,2,1,0:T(8,128)S(1)} collective-permute-done((f32[6,8,32,128]{3,2,1,0:T(8,128)S(1)}, f32[6,8,32,128]{3,2,1,0:T(8,128)S(1)}, u32[]{:S(2)}, u32[]{:S(2)}) %collective-permute-start.16) | collective-permute-done | bytes 786464 | tf_op jit(solution)/shard_map/while/body/eval_jaxpr/ppermute | solution.py:27
  372.5 3.0 collective-permute-done.1
  377.3 3.3 collective-permute-start.3
  399.1 3.3 collective-permute-done.5
  421.1 4.2 collective-permute-done.8
  447.4 2.9 collective-permute-done.13
  450.4 2.9 collective-permute-start.14
  468.8 4.2 collective-permute-start.16
  474.7 14.4 %collective-permute-done.16 = f32[6,8,32,128]{3,2,1,0:T(8,128)S(1)} collective-permute-done((f32[6,8,32,128]{3,2,1,0:T(8,128)S(1)}, f32[6,8,32,128]{3,2,1,0:T(8,128)S(1)}, u32[]{:S(2)}, u32[]{:S(2)}) %collective-permute-start.16) | collective-permute-done | bytes 786464 | tf_op jit(solution)/shard_map/while/body/eval_jaxpr/ppermute | solution.py:27
  (412 shorter events, 337.9 us)
Async XLA Ops:
  5.9 5.3 %collective-permute-start = (f32[6,1,32,128]{3,0,2,1:T(8,128)S(1)}, f32[6,1,32,128]{3,0,2,1:T(8,128)S(1)}, u32[]{:S(2)}, u32[]{:S(2)}) collective-permute-start(f32[6,1,32,128]{3,0,2,1:T(8,128)S(1)} %get-tuple-element.513), channel_id=1, source_target_pairs={{0,4},{4,8},{8,12},{12,16},{16,20},{20,24},{24,28},{28,0},{1,5},{5... | collective-permute-start | bytes 294920 | tf_op jit(solution)/shard_map/while/body/eval_jaxpr/ppermute | solution.py:18
  7.2 7.9 %collective-permute-start.1 = (f32[6,1,32,128]{3,0,2,1:T(8,128)S(1)}, f32[6,1,32,128]{3,0,2,1:T(8,128)S(1)}, u32[]{:S(2)}, u32[]{:S(2)}) collective-permute-start(f32[6,1,32,128]{3,0,2,1:T(8,128)S(1)} %get-tuple-element.514), channel_id=1, source_target_pairs={{4,0},{8,4},{12,8},{16,12},{20,16},{24,20},{28,24},{0,28},{5,1},{9... | collective-permute-start | bytes 294920 | tf_op jit(solution)/shard_map/while/body/eval_jaxpr/ppermute | solution.py:19
  31.8 5.4 %collective-permute-start.5 = (f32[6,1,32,128]{3,0,2,1:T(8,128)S(1)}, f32[6,1,32,128]{3,0,2,1:T(8,128)S(1)}, u32[]{:S(2)}, u32[]{:S(2)}) collective-permute-start(f32[6,1,32,128]{3,0,2,1:T(8,128)S(1)} %get-tuple-element.540), channel_id=1, source_target_pairs={{0,4},{4,8},{8,12},{12,16},{16,20},{20,24},{24,28},{28,0},{1,5},{5... | collective-permute-start | bytes 294920 | tf_op jit(solution)/shard_map/while/body/eval_jaxpr/ppermute | solution.py:18
  37.2 6.2 %collective-permute-start.6 = (f32[6,18,1,128]{3,0,2,1:T(8,128)S(1)}, f32[6,18,1,128]{3,0,2,1:T(8,128)S(1)}, u32[]{:S(2)}, u32[]{:S(2)}) collective-permute-start(f32[6,18,1,128]{3,0,2,1:T(8,128)S(1)} %get-tuple-element.541), channel_id=1, source_target_pairs={{1,0},{2,1},{3,2},{0,3},{5,4},{6,5},{7,6},{4,7},{9,8},{10,9},{11,1... | collective-permute-start | bytes 165896 | tf_op jit(solution)/shard_map/while/body/eval_jaxpr/ppermute | solution.py:19
  61.2 6.9 %collective-permute-start.10 = (f32[6,18,1,128]{3,0,2,1:T(8,128)S(1)}, f32[6,18,1,128]{3,0,2,1:T(8,128)S(1)}, u32[]{:S(2)}, u32[]{:S(2)}) collective-permute-start(f32[6,18,1,128]{3,0,2,1:T(8,128)S(1)} %get-tuple-element.561), channel_id=1, source_target_pairs={{1,0},{2,1},{3,2},{0,3},{5,4},{6,5},{7,6},{4,7},{9,8},{10,9},{11,1... | collective-permute-start | bytes 165896 | tf_op jit(solution)/shard_map/while/body/eval_jaxpr/ppermute | solution.py:19
  81.4 5.4 %collective-permute-start.13 = (f32[6,1,32,128]{3,0,2,1:T(8,128)S(1)}, f32[6,1,32,128]{3,0,2,1:T(8,128)S(1)}, u32[]{:S(2)}, u32[]{:S(2)}) collective-permute-start(f32[6,1,32,128]{3,0,2,1:T(8,128)S(1)} %get-tuple-element.580), channel_id=1, source_target_pairs={{0,4},{4,8},{8,12},{12,16},{16,20},{20,24},{24,28},{28,0},{1,5},{5... | collective-permute-start | bytes 294920 | tf_op jit(solution)/shard_map/while/body/eval_jaxpr/ppermute | solution.py:18
  102.8 20.5 %collective-permute-start.16 = (f32[6,8,32,128]{3,2,1,0:T(8,128)S(1)}, f32[6,8,32,128]{3,2,1,0:T(8,128)S(1)}, u32[]{:S(2)}, u32[]{:S(2)}) collective-permute-start(f32[6,8,32,128]{3,2,1,0:T(8,128)S(1)} %copy.31), channel_id=1, source_target_pairs={{4,0},{8,4},{12,8},{16,12},{20,16},{24,20},{28,24},{5,1},{9,5},{13... | collective-permute-start | bytes 2359304 | tf_op jit(solution)/shard_map/while/body/eval_jaxpr/ppermute | solution.py:27
  124.6 5.6 %collective-permute-start = (f32[6,1,32,128]{3,0,2,1:T(8,128)S(1)}, f32[6,1,32,128]{3,0,2,1:T(8,128)S(1)}, u32[]{:S(2)}, u32[]{:S(2)}) collective-permute-start(f32[6,1,32,128]{3,0,2,1:T(8,128)S(1)} %get-tuple-element.513), channel_id=1, source_target_pairs={{0,4},{4,8},{8,12},{12,16},{16,20},{20,24},{24,28},{28,0},{1,5},{5... | collective-permute-start | bytes 294920 | tf_op jit(solution)/shard_map/while/body/eval_jaxpr/ppermute | solution.py:18
  126.1 7.4 %collective-permute-start.1 = (f32[6,1,32,128]{3,0,2,1:T(8,128)S(1)}, f32[6,1,32,128]{3,0,2,1:T(8,128)S(1)}, u32[]{:S(2)}, u32[]{:S(2)}) collective-permute-start(f32[6,1,32,128]{3,0,2,1:T(8,128)S(1)} %get-tuple-element.514), channel_id=1, source_target_pairs={{4,0},{8,4},{12,8},{16,12},{20,16},{24,20},{28,24},{0,28},{5,1},{9... | collective-permute-start | bytes 294920 | tf_op jit(solution)/shard_map/while/body/eval_jaxpr/ppermute | solution.py:19
  150.1 5.9 %collective-permute-start.4 = (f32[6,1,32,128]{3,0,2,1:T(8,128)S(1)}, f32[6,1,32,128]{3,0,2,1:T(8,128)S(1)}, u32[]{:S(2)}, u32[]{:S(2)}) collective-permute-start(f32[6,1,32,128]{3,0,2,1:T(8,128)S(1)} %get-tuple-element.539), channel_id=1, source_target_pairs={{4,0},{8,4},{12,8},{16,12},{20,16},{24,20},{28,24},{0,28},{5,1},{9... | collective-permute-start | bytes 294920 | tf_op jit(solution)/shard_map/while/body/eval_jaxpr/ppermute | solution.py:19
  150.6 6.3 %collective-permute-start.5 = (f32[6,1,32,128]{3,0,2,1:T(8,128)S(1)}, f32[6,1,32,128]{3,0,2,1:T(8,128)S(1)}, u32[]{:S(2)}, u32[]{:S(2)}) collective-permute-start(f32[6,1,32,128]{3,0,2,1:T(8,128)S(1)} %get-tuple-element.540), channel_id=1, source_target_pairs={{0,4},{4,8},{8,12},{12,16},{16,20},{20,24},{24,28},{28,0},{1,5},{5... | collective-permute-start | bytes 294920 | tf_op jit(solution)/shard_map/while/body/eval_jaxpr/ppermute | solution.py:18
  181.1 7.0 %collective-permute-start.10 = (f32[6,18,1,128]{3,0,2,1:T(8,128)S(1)}, f32[6,18,1,128]{3,0,2,1:T(8,128)S(1)}, u32[]{:S(2)}, u32[]{:S(2)}) collective-permute-start(f32[6,18,1,128]{3,0,2,1:T(8,128)S(1)} %get-tuple-element.561), channel_id=1, source_target_pairs={{1,0},{2,1},{3,2},{0,3},{5,4},{6,5},{7,6},{4,7},{9,8},{10,9},{11,1... | collective-permute-start | bytes 165896 | tf_op jit(solution)/shard_map/while/body/eval_jaxpr/ppermute | solution.py:19
  202.3 5.2 %collective-permute-start.13 = (f32[6,1,32,128]{3,0,2,1:T(8,128)S(1)}, f32[6,1,32,128]{3,0,2,1:T(8,128)S(1)}, u32[]{:S(2)}, u32[]{:S(2)}) collective-permute-start(f32[6,1,32,128]{3,0,2,1:T(8,128)S(1)} %get-tuple-element.580), channel_id=1, source_target_pairs={{0,4},{4,8},{8,12},{12,16},{16,20},{20,24},{24,28},{28,0},{1,5},{5... | collective-permute-start | bytes 294920 | tf_op jit(solution)/shard_map/while/body/eval_jaxpr/ppermute | solution.py:18
  207.5 6.1 %collective-permute-start.14 = (f32[6,18,1,128]{3,0,2,1:T(8,128)S(1)}, f32[6,18,1,128]{3,0,2,1:T(8,128)S(1)}, u32[]{:S(2)}, u32[]{:S(2)}) collective-permute-start(f32[6,18,1,128]{3,0,2,1:T(8,128)S(1)} %get-tuple-element.581), channel_id=1, source_target_pairs={{1,0},{2,1},{3,2},{0,3},{5,4},{6,5},{7,6},{4,7},{9,8},{10,9},{11,1... | collective-permute-start | bytes 165896 | tf_op jit(solution)/shard_map/while/body/eval_jaxpr/ppermute | solution.py:19
  225.3 20.1 %collective-permute-start.16 = (f32[6,8,32,128]{3,2,1,0:T(8,128)S(1)}, f32[6,8,32,128]{3,2,1,0:T(8,128)S(1)}, u32[]{:S(2)}, u32[]{:S(2)}) collective-permute-start(f32[6,8,32,128]{3,2,1,0:T(8,128)S(1)} %copy.31), channel_id=1, source_target_pairs={{4,0},{8,4},{12,8},{16,12},{20,16},{24,20},{28,24},{5,1},{9,5},{13... | collective-permute-start | bytes 2359304 | tf_op jit(solution)/shard_map/while/body/eval_jaxpr/ppermute | solution.py:27
  246.9 5.2 %collective-permute-start.1 = (f32[6,1,32,128]{3,0,2,1:T(8,128)S(1)}, f32[6,1,32,128]{3,0,2,1:T(8,128)S(1)}, u32[]{:S(2)}, u32[]{:S(2)}) collective-permute-start(f32[6,1,32,128]{3,0,2,1:T(8,128)S(1)} %get-tuple-element.514), channel_id=1, source_target_pairs={{4,0},{8,4},{12,8},{16,12},{20,16},{24,20},{28,24},{0,28},{5,1},{9... | collective-permute-start | bytes 294920 | tf_op jit(solution)/shard_map/while/body/eval_jaxpr/ppermute | solution.py:19
  252.2 8.9 %collective-permute-start.2 = (f32[6,18,1,128]{3,0,2,1:T(8,128)S(1)}, f32[6,18,1,128]{3,0,2,1:T(8,128)S(1)}, u32[]{:S(2)}, u32[]{:S(2)}) collective-permute-start(f32[6,18,1,128]{3,0,2,1:T(8,128)S(1)} %get-tuple-element.515), channel_id=1, source_target_pairs={{1,0},{2,1},{3,2},{0,3},{5,4},{6,5},{7,6},{4,7},{9,8},{10,9},{11,1... | collective-permute-start | bytes 165896 | tf_op jit(solution)/shard_map/while/body/eval_jaxpr/ppermute | solution.py:19
  274.7 5.5 %collective-permute-start.5 = (f32[6,1,32,128]{3,0,2,1:T(8,128)S(1)}, f32[6,1,32,128]{3,0,2,1:T(8,128)S(1)}, u32[]{:S(2)}, u32[]{:S(2)}) collective-permute-start(f32[6,1,32,128]{3,0,2,1:T(8,128)S(1)} %get-tuple-element.540), channel_id=1, source_target_pairs={{0,4},{4,8},{8,12},{12,16},{16,20},{20,24},{24,28},{28,0},{1,5},{5... | collective-permute-start | bytes 294920 | tf_op jit(solution)/shard_map/while/body/eval_jaxpr/ppermute | solution.py:18
  280.2 5.8 %collective-permute-start.6 = (f32[6,18,1,128]{3,0,2,1:T(8,128)S(1)}, f32[6,18,1,128]{3,0,2,1:T(8,128)S(1)}, u32[]{:S(2)}, u32[]{:S(2)}) collective-permute-start(f32[6,18,1,128]{3,0,2,1:T(8,128)S(1)} %get-tuple-element.541), channel_id=1, source_target_pairs={{1,0},{2,1},{3,2},{0,3},{5,4},{6,5},{7,6},{4,7},{9,8},{10,9},{11,1... | collective-permute-start | bytes 165896 | tf_op jit(solution)/shard_map/while/body/eval_jaxpr/ppermute | solution.py:19
  297.8 7.5 %collective-permute-start.8 = (f32[6,1,32,128]{3,0,2,1:T(8,128)S(1)}, f32[6,1,32,128]{3,0,2,1:T(8,128)S(1)}, u32[]{:S(2)}, u32[]{:S(2)}) collective-permute-start(f32[6,1,32,128]{3,0,2,1:T(8,128)S(1)} %get-tuple-element.559), channel_id=1, source_target_pairs={{4,0},{8,4},{12,8},{16,12},{20,16},{24,20},{28,24},{0,28},{5,1},{9... | collective-permute-start | bytes 294920 | tf_op jit(solution)/shard_map/while/body/eval_jaxpr/ppermute | solution.py:19
  297.9 7.4 %collective-permute-start.9 = (f32[6,1,32,128]{3,0,2,1:T(8,128)S(1)}, f32[6,1,32,128]{3,0,2,1:T(8,128)S(1)}, u32[]{:S(2)}, u32[]{:S(2)}) collective-permute-start(f32[6,1,32,128]{3,0,2,1:T(8,128)S(1)} %get-tuple-element.560), channel_id=1, source_target_pairs={{0,4},{4,8},{8,12},{12,16},{16,20},{20,24},{24,28},{28,0},{1,5},{5... | collective-permute-start | bytes 294920 | tf_op jit(solution)/shard_map/while/body/eval_jaxpr/ppermute | solution.py:18
  328.2 6.1 %collective-permute-start.14 = (f32[6,18,1,128]{3,0,2,1:T(8,128)S(1)}, f32[6,18,1,128]{3,0,2,1:T(8,128)S(1)}, u32[]{:S(2)}, u32[]{:S(2)}) collective-permute-start(f32[6,18,1,128]{3,0,2,1:T(8,128)S(1)} %get-tuple-element.581), channel_id=1, source_target_pairs={{1,0},{2,1},{3,2},{0,3},{5,4},{6,5},{7,6},{4,7},{9,8},{10,9},{11,1... | collective-permute-start | bytes 165896 | tf_op jit(solution)/shard_map/while/body/eval_jaxpr/ppermute | solution.py:19
  345.9 19.9 %collective-permute-start.16 = (f32[6,8,32,128]{3,2,1,0:T(8,128)S(1)}, f32[6,8,32,128]{3,2,1,0:T(8,128)S(1)}, u32[]{:S(2)}, u32[]{:S(2)}) collective-permute-start(f32[6,8,32,128]{3,2,1,0:T(8,128)S(1)} %copy.31), channel_id=1, source_target_pairs={{4,0},{8,4},{12,8},{16,12},{20,16},{24,20},{28,24},{5,1},{9,5},{13... | collective-permute-start | bytes 2359304 | tf_op jit(solution)/shard_map/while/body/eval_jaxpr/ppermute | solution.py:27
  366.8 5.5 %collective-permute-start = (f32[6,1,32,128]{3,0,2,1:T(8,128)S(1)}, f32[6,1,32,128]{3,0,2,1:T(8,128)S(1)}, u32[]{:S(2)}, u32[]{:S(2)}) collective-permute-start(f32[6,1,32,128]{3,0,2,1:T(8,128)S(1)} %get-tuple-element.513), channel_id=1, source_target_pairs={{0,4},{4,8},{8,12},{12,16},{16,20},{20,24},{24,28},{28,0},{1,5},{5... | collective-permute-start | bytes 294920 | tf_op jit(solution)/shard_map/while/body/eval_jaxpr/ppermute | solution.py:18
  368.8 6.6 %collective-permute-start.1 = (f32[6,1,32,128]{3,0,2,1:T(8,128)S(1)}, f32[6,1,32,128]{3,0,2,1:T(8,128)S(1)}, u32[]{:S(2)}, u32[]{:S(2)}) collective-permute-start(f32[6,1,32,128]{3,0,2,1:T(8,128)S(1)} %get-tuple-element.514), channel_id=1, source_target_pairs={{4,0},{8,4},{12,8},{16,12},{20,16},{24,20},{28,24},{0,28},{5,1},{9... | collective-permute-start | bytes 294920 | tf_op jit(solution)/shard_map/while/body/eval_jaxpr/ppermute | solution.py:19
  375.5 7.0 %collective-permute-start.2 = (f32[6,18,1,128]{3,0,2,1:T(8,128)S(1)}, f32[6,18,1,128]{3,0,2,1:T(8,128)S(1)}, u32[]{:S(2)}, u32[]{:S(2)}) collective-permute-start(f32[6,18,1,128]{3,0,2,1:T(8,128)S(1)} %get-tuple-element.515), channel_id=1, source_target_pairs={{1,0},{2,1},{3,2},{0,3},{5,4},{6,5},{7,6},{4,7},{9,8},{10,9},{11,1... | collective-permute-start | bytes 165896 | tf_op jit(solution)/shard_map/while/body/eval_jaxpr/ppermute | solution.py:19
  377.3 5.2 %collective-permute-start.3 = (f32[6,18,1,128]{3,0,2,1:T(8,128)S(1)}, f32[6,18,1,128]{3,0,2,1:T(8,128)S(1)}, u32[]{:S(2)}, u32[]{:S(2)}) collective-permute-start(f32[6,18,1,128]{3,0,2,1:T(8,128)S(1)} %get-tuple-element.516), channel_id=1, source_target_pairs={{0,1},{1,2},{2,3},{3,0},{4,5},{5,6},{6,7},{7,4},{8,9},{9,10},{10,1... | collective-permute-start | bytes 165896 | tf_op jit(solution)/shard_map/while/body/eval_jaxpr/ppermute | solution.py:18
  396.7 5.7 %collective-permute-start.5 = (f32[6,1,32,128]{3,0,2,1:T(8,128)S(1)}, f32[6,1,32,128]{3,0,2,1:T(8,128)S(1)}, u32[]{:S(2)}, u32[]{:S(2)}) collective-permute-start(f32[6,1,32,128]{3,0,2,1:T(8,128)S(1)} %get-tuple-element.540), channel_id=1, source_target_pairs={{0,4},{4,8},{8,12},{12,16},{16,20},{20,24},{24,28},{28,0},{1,5},{5... | collective-permute-start | bytes 294920 | tf_op jit(solution)/shard_map/while/body/eval_jaxpr/ppermute | solution.py:18
  419.2 6.2 %collective-permute-start.8 = (f32[6,1,32,128]{3,0,2,1:T(8,128)S(1)}, f32[6,1,32,128]{3,0,2,1:T(8,128)S(1)}, u32[]{:S(2)}, u32[]{:S(2)}) collective-permute-start(f32[6,1,32,128]{3,0,2,1:T(8,128)S(1)} %get-tuple-element.559), channel_id=1, source_target_pairs={{4,0},{8,4},{12,8},{16,12},{20,16},{24,20},{28,24},{0,28},{5,1},{9... | collective-permute-start | bytes 294920 | tf_op jit(solution)/shard_map/while/body/eval_jaxpr/ppermute | solution.py:19
  419.9 6.4 %collective-permute-start.9 = (f32[6,1,32,128]{3,0,2,1:T(8,128)S(1)}, f32[6,1,32,128]{3,0,2,1:T(8,128)S(1)}, u32[]{:S(2)}, u32[]{:S(2)}) collective-permute-start(f32[6,1,32,128]{3,0,2,1:T(8,128)S(1)} %get-tuple-element.560), channel_id=1, source_target_pairs={{0,4},{4,8},{8,12},{12,16},{16,20},{20,24},{24,28},{28,0},{1,5},{5... | collective-permute-start | bytes 294920 | tf_op jit(solution)/shard_map/while/body/eval_jaxpr/ppermute | solution.py:18
  450.4 6.8 %collective-permute-start.14 = (f32[6,18,1,128]{3,0,2,1:T(8,128)S(1)}, f32[6,18,1,128]{3,0,2,1:T(8,128)S(1)}, u32[]{:S(2)}, u32[]{:S(2)}) collective-permute-start(f32[6,18,1,128]{3,0,2,1:T(8,128)S(1)} %get-tuple-element.581), channel_id=1, source_target_pairs={{1,0},{2,1},{3,2},{0,3},{5,4},{6,5},{7,6},{4,7},{9,8},{10,9},{11,1... | collective-permute-start | bytes 165896 | tf_op jit(solution)/shard_map/while/body/eval_jaxpr/ppermute | solution.py:19
  468.8 20.3 %collective-permute-start.16 = (f32[6,8,32,128]{3,2,1,0:T(8,128)S(1)}, f32[6,8,32,128]{3,2,1,0:T(8,128)S(1)}, u32[]{:S(2)}, u32[]{:S(2)}) collective-permute-start(f32[6,8,32,128]{3,2,1,0:T(8,128)S(1)} %copy.31), channel_id=1, source_target_pairs={{4,0},{8,4},{12,8},{16,12},{20,16},{24,20},{28,24},{5,1},{9,5},{13... | collective-permute-start | bytes 2359304 | tf_op jit(solution)/shard_map/while/body/eval_jaxpr/ppermute | solution.py:27
  (43 other events, 156.1 us)
where the time goes:
time: 504 us; the launch traced here: 494 us
  waiting for transfers between devices  173 us (34%)
  other arithmetic  160 us (32%)
  starting transfers between devices  112 us (22%)
  local copies, waits for them, and re-layouts  40.7 us (8%)
    ppermute x32, waiting for transfers between devices, with_halo(): after = lax.ppermute(leading, axis, down)  79.4 us
    ppermute x32, starting transfers between devices, with_halo(): after = lax.ppermute(leading, axis, down)  62.1 us
    ppermute x4, waiting for transfers between devices, passed_along(): return lax.ppermute(block, axis, route)  56.2 us
    ppermute x32, waiting for transfers between devices, with_halo(): before = lax.ppermute(last, axis, up)  37.2 us
    sub x16, other arithmetic, advance(): rhs = lap_phi - 1.0 * (summed[None] - fracs) - psi  34.8 us
    ppermute x32, starting transfers between devices, with_halo(): before = lax.ppermute(last, axis, up)  32.3 us
    sub x16, other arithmetic, advance(): gsum = padded[:, 2:, 1:-1] + padded[:, :-2, 1:-1] - 2.0 * center  30.1 us
    reduce_sum x12, other arithmetic, advance(): jnp.sum(composition[:, 0][:, None, None, None] * change, axis=0)  23.4 us
  transfers between devices with their start and end apart: 68, of which 51 were waited for; matrix products, arithmetic and copies ran while one was open for 2% of the time, Pallas kernels for 0%

commit v1 on v0

v1 whole, which is shorter than its diff:
```python
import functools

import jax
import jax.numpy as jnp
from jax import lax
from jax.experimental import pallas as pl
from jax.experimental.pallas import tpu as pltpu
from jax.sharding import PartitionSpec as P

STEPS = 4
ROUNDS = 4
SHIFT = 8
JUMPS = (12, 8, 4, 8)
SENT = 5
PAD = 8
DT = 0.04
AXES = ("grow", "lat")
GRAD, CENTER, COUPLE, LATENT, RELEASE, SPREAD, STAY, MELT = 0, 12, 16, 24, 28, 36, 38, 40


def scalar_table(grad_coef, composition, latent, diffusivity, melt_table):
    scaled = DT * grad_coef
    return jnp.concatenate(
        [
            scaled.reshape(-1),
            1.0 + DT - 2.0 * jnp.sum(scaled, axis=1),
            (DT * composition).reshape(-1),
            DT * latent,
            composition.reshape(-1),
            DT * diffusivity,
            1.0 - 6.0 * DT * diffusivity,
            melt_table.reshape(-1),
        ]
    )


def round_kernel(
    turn, place_of, base, keeps, last, sizes, table, own, above, left, right, index, *rest
):
    outs, (even, odd) = rest[:-2], rest[-2:]
    ng, block, rows = sizes
    kept, total = own.shape[1], float(ng * block)
    height = block + 2 * STEPS
    place = place_of()
    start = place * block + base - STEPS
    lowest = SHIFT * turn - start
    top = ng * block + SHIFT * turn - 1 - start

    def fill(source, e_from, e_to):
        fields = [source[f, e_from] for f in range(SENT)]
        for f, value in zip((0, 1, 2, 4, 5), fields):
            even[f, e_to, PAD : PAD + rows] = value
        even[3, e_to, PAD : PAD + rows] = 1.0 - fields[0] - fields[1] - fields[2]
        for side, at in ((left, PAD - STEPS), (right, PAD + rows)):
            fields = [side[f, e_to] for f in range(SENT)]
            for f, value in zip((0, 1, 2, 4, 5), fields):
                even[f, e_to, at : at + STEPS] = value
            even[3, e_to, at : at + STEPS] = 1.0 - fields[0] - fields[1] - fields[2]

    @pl.loop(0, kept)
    def _(e):
        fill(own, e, e)

    @pl.loop(0, height - kept)
    def _(e):
        fill(above, e, e + kept)

    def advance(src, e, at):
        window = pl.ds(at, 8)
        up, down = jnp.minimum(e + 1, top), jnp.maximum(e - 1, lowest)
        theta = ((e + start).astype(jnp.float32) - 0.5 * total) / total
        mid = [src[f, e, window] for f in range(6)]
        gsum = [src[f, up, window] + src[f, down, window] for f in range(6)]
        xsum = [src[f, e, pl.ds(at + 1, 8)] + src[f, e, pl.ds(at - 1, 8)] for f in range(6)]
        ysum = [pltpu.roll(v, 1, 1) + pltpu.roll(v, v.shape[1] - 1, 1) for v in mid]
        m0, m1 = mid[4], mid[5]
        guess = []
        for a in range(4):
            guess.append(
                table[GRAD + 3 * a] * gsum[a]
                + table[GRAD + 3 * a + 1] * xsum[a]
                + table[GRAD + 3 * a + 2] * ysum[a]
                + table[CENTER + a] * mid[a]
                - table[COUPLE + 2 * a] * m0
                - table[COUPLE + 2 * a + 1] * m1
                - table[LATENT + a] * theta
            )
        phase_sum = mid[0] + mid[1] + mid[2] + mid[3]
        mean = 0.25 * (guess[0] + guess[1] + guess[2] + guess[3] - phase_sum)
        clipped = [jnp.clip(g - mean, 0.0, 1.0) for g in guess]
        inverse = 1.0 / (clipped[0] + clipped[1] + clipped[2] + clipped[3])
        new = [c * inverse for c in clipped]
        change = [n - v for n, v in zip(new, mid)]
        for k in range(2):
            release = table[RELEASE + k] * change[0]
            for a in range(1, 4):
                release = release + table[RELEASE + 2 * a + k] * change[a]
            sides = gsum[4 + k] + xsum[4 + k] + ysum[4 + k]
            new.append(table[SPREAD + k] * sides + table[STAY + k] * mid[4 + k] - release)
        return new

    buffers = (even, odd)
    for step in range(1, STEPS):
        src, dst = buffers[(step - 1) % 2], buffers[step % 2]

        @pl.loop(step, height - step)
        def _(e, src=src, dst=dst):
            for t in range(rows // 8 + 1):
                at = PAD - STEPS + 8 * t
                for f, value in enumerate(advance(src, e, at)):
                    dst[f, e, pl.ds(at, 8)] = value

    src = buffers[(STEPS - 1) % 2]
    if last:
        phases, potentials = outs

        def put(o, here, new):
            for a in range(4):
                phases[a, o, here] = new[a]
            for k in range(2):
                potentials[k, o, here] = new[4 + k]

    else:
        climbing, staying = outs

        def put(o, here, new):
            sent = [new[f] for f in (0, 1, 2, 4, 5)]

            @pl.when(o < climbing.shape[1])
            def _():
                for f in range(SENT):
                    climbing[f, o, here] = sent[f]

            @pl.when(o >= keeps)
            def _():
                for f in range(SENT):
                    staying[f, o - keeps, here] = sent[f]

    @pl.loop(0, block)
    def _(o):
        for t in range(rows // 8):
            put(o, pl.ds(8 * t, 8), advance(src, o + STEPS, PAD + 8 * t))

    fresh = ng * block + SHIFT * turn - (ng - 1) * block - base

    @pl.when(place == ng - 1)
    def _():
        @pl.loop(0, SHIFT)
        def _(j):
            for t in range(rows // 8):
                here = pl.ds(8 * t, 8)
                row = index[j, here]
                mu = [jnp.zeros(row.shape, jnp.float32)] * 2
                for m in range((table.shape[0] - MELT) // 2):
                    mu = [jnp.where(row == m, table[MELT + 2 * m + k], mu[k]) for k in range(2)]
                none = jnp.zeros(row.shape, jnp.float32)
                put(fresh + j, here, [none, none, none, none + 1.0] + mu)


def prepare_kernel(labels, roughness, potential, climbing, staying):
    skipped = labels.shape[0] - staying.shape[1]

    @pl.loop(0, labels.shape[0])
    def _(o):
        kind = labels[o]
        rough = [roughness[a, o] for a in range(4)]
        inverse = 1.0 / (3.0 + rough[0] + rough[1] + rough[2] + rough[3])
        new = [(jnp.where(kind == a, 3.0, 0.0) + rough[a]) * inverse for a in range(3)]
        new += [potential[0, o], potential[1, o]]
        for f in range(SENT):
            climbing[f, o] = new[f]

        @pl.when(o >= skipped)
        def _():
            for f in range(SENT):
                staying[f, o - skipped] = new[f]


def on_device(ng, nl, labels, roughness, potential, grad_coef, composition, latent, diffusivity, melt_table, melt_index):
    block, rows, lanes = labels.shape
    height = block + 2 * STEPS
    vmem = pl.BlockSpec(memory_space=pltpu.VMEM)
    smem = pl.BlockSpec(memory_space=pltpu.SMEM)
    f32 = jnp.float32
    table = scalar_table(grad_coef, composition, latent, diffusivity, melt_table)

    def home(g, l):
        return g * nl + l

    def away(g, l):
        return (g // 2 * 2 + (l % 2 ^ (l // 2 % 2))) * nl + l // 2 * 2 + g % 2

    def home_place():
        return lax.axis_index("grow")

    def away_place():
        return lax.axis_index("grow") // 2 * 2 + lax.axis_index("lat") % 2

    blocks = [(g, l) for g in range(ng) for l in range(nl)]

    def moved(array, before, after, climb):
        route = [(before(g + climb, l), after(g, l)) for g, l in blocks if g + climb < ng]
        return lax.ppermute(array, AXES, route)

    def sides(own, above, where):
        first = jnp.concatenate([own[:, :, :STEPS], above[:, :, :STEPS]], axis=1)
        final = jnp.concatenate([own[:, :, rows - STEPS :], above[:, :, rows - STEPS :]], axis=1)
        left = lax.ppermute(final, AXES, [(where(g, l), where(g, (l + 1) % nl)) for g, l in blocks])
        right = lax.ppermute(first, AXES, [(where(g, (l + 1) % nl), where(g, l)) for g, l in blocks])
        return left, right

    def sizes_of(jump):
        return jump + STEPS, block - jump + STEPS

    def piece(planes):
        return jax.ShapeDtypeStruct((SENT, planes, rows, lanes), f32)

    climbing, staying = pl.pallas_call(
        prepare_kernel,
        out_shape=[piece(n) for n in sizes_of(JUMPS[0])],
        in_specs=[vmem] * 3,
        out_specs=[vmem] * 2,
        name="prepare",
    )(labels, roughness, potential)

    away_index = lax.ppermute(
        melt_index[: ROUNDS - 1],
        AXES,
        [(home(ng - 1, l), away(ng - 1, l)) for l in range(nl)],
    )

    base = 0
    for turn in range(ROUNDS):
        before = home if turn == 0 else away
        after = home if turn == ROUNDS - 1 else away
        above = moved(climbing, before, after, 1)
        own = staying if before is after else moved(staying, before, after, 0)
        left, right = sides(own, above, after)
        base += JUMPS[turn]
        last = turn == ROUNDS - 1
        if last:
            shapes = [jax.ShapeDtypeStruct((n, block, rows, lanes), f32) for n in (4, 2)]
            keeps = 0
        else:
            shapes = [piece(n) for n in sizes_of(JUMPS[turn + 1])]
            keeps = block - shapes[1].shape[1]
        outs = pl.pallas_call(
            functools.partial(
                round_kernel,
                turn,
                home_place if last else away_place,
                base,
                keeps,
                last,
                (ng, block, rows),
            ),
            out_shape=shapes,
            in_specs=[smem] + [vmem] * 5,
            out_specs=[vmem] * 2,
            scratch_shapes=[pltpu.VMEM((6, height, rows + 2 * PAD, lanes), f32)] * 2,
            compiler_params=pltpu.CompilerParams(vmem_limit_bytes=40 << 20),
            name="advance",
        )(table, own, above, left, right, melt_index[turn] if last else away_index[turn])
        climbing, staying = outs
    return outs[0], outs[1]


def solution(mesh):
    ng, nl = mesh.shape["grow"], mesh.shape["lat"]
    placed = (
        P("grow", "lat", None),
        P(None, "grow", "lat", None),
        P(None, "grow", "lat", None),
        P(),
        P(),
        P(),
        P(),
        P(),
        P(None, None, "lat", None),
    )
    return jax.shard_map(
        functools.partial(on_device, ng, nl),
        mesh=mesh,
        in_specs=placed,
        out_specs=(P(None, "grow", "lat", None), P(None, "grow", "lat", None)),
        check_vma=False,
    )
```

time: 504 us -> 187 us (0.37); the launches traced: 494 us -> 187 us
  other arithmetic: 160 us -> 1.96 us
  starting transfers between devices: 112 us -> 22.3 us
  waiting for transfers between devices: 173 us -> 93.1 us
  Pallas kernels: 0 us -> 66.4 us
  local copies, waits for them, and re-layouts: 40.7 us -> 1.88 us
    ppermute x68 -> x15, starting transfers between devices: 112 us -> 22.3 us  [the longest x6 14.8 us: moved(): return lax.ppermute(array, AXES, route)]
    sub x48 -> x2, other arithmetic: 86.6 us -> 0.01 us  [the longest x1 0.01 us: scalar_table(): 1.0 + DT - 2.0 * jnp.sum(scaled, axis=1)]
    ppermute x68 -> x15, waiting for transfers between devices: 173 us -> 93.1 us  [the longest x6 69.6 us: moved(): return lax.ppermute(array, AXES, route)]
    pallas_call x0 -> x5, Pallas kernels: none -> 66.4 us  [the longest x4 63.3 us: on_device(): pl.pallas_call(functools.partial(round_kernel, turn, home_place if last e...]
    reduce_sum x25 -> x1, other arithmetic: 37.7 us -> 0.12 us  [scalar_table(): jnp.sum(scaled, axis=1)]
    slice x62 -> x9, local copies, waits for them, and re-layouts: 35 us -> 1.13 us  [the longest x1 0.77 us: on_device(): melt_index[:ROUNDS - 1]]
    select_n x20 -> x0, other arithmetic: 12.7 us -> none  [the longest x16 10.3 us: settle(): return jnp.where((place == final) & (rows >= margin + block), upper, out)]
    div x25 -> x0, other arithmetic: 11.9 us -> none  [the longest x4 9.43 us: advance(): newphi = clipped / jnp.sum(clipped, axis=0)[None]]
  transfers between devices with their start and end apart: 68 -> 15, of which waited for: 51 -> 13; matrix products, arithmetic and copies ran while one was open for 2% -> 2% of each run, Pallas kernels for 0% -> 0%
where the time goes in v1:
time: 187 us
  waiting for transfers between devices  93.1 us (50%)
  Pallas kernels  66.4 us (36%)
  starting transfers between devices  22.3 us (12%)
  other arithmetic  1.96 us (1%)
  local copies, waits for them, and re-layouts  1.88 us (1%)
    ppermute x6, waiting for transfers between devices, moved(): return lax.ppermute(array, AXES, route)  69.6 us
    pallas_call x4, Pallas kernels, on_device(): pl.pallas_call(functools.partial(round_kernel, turn, home_place if last e...  63.3 us
    ppermute x4, waiting for transfers between devices, sides(): lax.ppermute(first, AXES, [(where(g, (l + 1) % nl), where(g, l)) for g, l...  21.1 us
    ppermute x6, starting transfers between devices, moved(): return lax.ppermute(array, AXES, route)  14.8 us
    ppermute x4, starting transfers between devices, sides(): lax.ppermute(final, AXES, [(where(g, l), where(g, (l + 1) % nl)) for g, l...  6.17 us
  transfers between devices with their start and end apart: 15, of which 13 were waited for; matrix products, arithmetic and copies ran while one was open for 2% of the time, Pallas kernels for 0%

profile of v1, /device:TPU:17, one launch (start us, length us, event | category | flops | bytes accessed | tf_op | source)
XLA Modules:
  0.0 186.7 jit_solution(14032661225562258626)
XLA Ops:
  0.7 3.1 %prepare.1 = (f32[5,16,32,128]{3,2,1,0:T(8,128)}, f32[5,8,32,128]{3,2,1,0:T(8,128)}) custom-call(s32[16,32,128]{2,1,0:T(8,128)} %labels.1, f32[4,16,32,128]{3,2,1,0:T(8,128)} %roughness.1, f32[2,16,32,128]{3,2,1,0:T(8,128)} %potential.1), custom_call_target="tpu_custom_call" | custom-call | tf_op jit(solution)/shard_map/prepare/pallas_call | solution.py:218
  3.8 3.0 %collective-permute-start.1 = (f32[5,16,32,128]{3,2,1,0:T(8,128)}, f32[5,16,32,128]{3,2,1,0:T(8,128)S(1)}, u32[]{:S(2)}, u32[]{:S(2)}) collective-permute-start(f32[5,16,32,128]{3,2,1,0:T(8,128)} %get-tuple-element.11), channel_id=1, source_target_pairs={{4,0},{5,4},{6,6},{7,2},{8,1},{9,5},{10,7},{11,3},{12,8},{13,12},{... | collective-permute-start | bytes 3932168 | tf_op jit(solution)/shard_map/ppermute | solution.py:203
  6.8 3.1 %collective-permute-start = (f32[5,8,32,128]{3,2,1,0:T(8,128)}, f32[5,8,32,128]{3,2,1,0:T(8,128)S(1)}, u32[]{:S(2)}, u32[]{:S(2)}) collective-permute-start(f32[5,8,32,128]{3,2,1,0:T(8,128)} %get-tuple-element.10), channel_id=1, source_target_pairs={{0,0},{1,4},{2,6},{3,2},{4,1},{5,5},{6,7},{7,3},{8,8},{9,12},{10,1... | collective-permute-start | bytes 1966088 | tf_op jit(solution)/shard_map/ppermute | solution.py:203
  9.9 0.8 slice.67
  10.7 0.7 collective-permute-start.4
  11.6 18.9 %collective-permute-done.own = f32[5,8,32,128]{3,2,1,0:T(8,128)S(1)} collective-permute-done((f32[5,8,32,128]{3,2,1,0:T(8,128)}, f32[5,8,32,128]{3,2,1,0:T(8,128)S(1)}, u32[]{:S(2)}, u32[]{:S(2)}) %collective-permute-start) | collective-permute-done | bytes 655392 | tf_op jit(solution)/shard_map/ppermute | solution.py:203
  30.5 6.3 %collective-permute-done.1.above = f32[5,16,32,128]{3,2,1,0:T(8,128)S(1)} collective-permute-done((f32[5,16,32,128]{3,2,1,0:T(8,128)}, f32[5,16,32,128]{3,2,1,0:T(8,128)S(1)}, u32[]{:S(2)}, u32[]{:S(2)}) %collective-permute-start.1) | collective-permute-done | bytes 1310752 | tf_op jit(solution)/shard_map/ppermute | solution.py:203
  36.9 0.7 pad_maximum_fusion.1
  37.6 0.8 pad_maximum_fusion
  38.4 1.5 collective-permute-start.2
  40.6 4.4 %collective-permute-done.3.right = f32[5,24,4,128]{3,2,1,0:T(4,128)S(1)} collective-permute-done((f32[5,24,4,128]{3,2,1,0:T(4,128)}, f32[5,24,4,128]{3,2,1,0:T(4,128)S(1)}, u32[]{:S(2)}, u32[]{:S(2)}) %collective-permute-start.3) | collective-permute-done | bytes 245792 | tf_op jit(solution)/shard_map/ppermute | solution.py:209
  45.0 1.6 collective-permute-done.2.left
  46.6 16.7 %advance.4 = (f32[5,12,32,128]{3,2,1,0:T(8,128)S(1)}, f32[5,12,32,128]{3,2,1,0:T(8,128)S(1)}) custom-call(f32[72]{0:T(128)S(1)} %concatenate.27.table, f32[5,8,32,128]{3,2,1,0:T(8,128)S(1)} %collective-permute-done.own, f32[5,16,32,128]{3,2,1,0:T(8,128)S(1)} %collective-permute-done.1.above, f32[5,24,4,128]{3,2,1,0:T(4,128)S(1)} %collective-permute-done.2.left, ...), custom_call_target="tpu_custom_call" | custom-call | tf_op jit(solution)/shard_map/advance/pallas_call | solution.py:247
  63.3 2.3 %collective-permute-start.5 = (f32[5,12,32,128]{3,2,1,0:T(8,128)S(1)}, f32[5,12,32,128]{3,2,1,0:T(8,128)S(1)}, u32[]{:S(2)}, u32[]{:S(2)}) collective-permute-start(f32[5,12,32,128]{3,2,1,0:T(8,128)S(1)} %get-tuple-element.13), channel_id=1, source_target_pairs={{1,0},{5,4},{7,6},{3,2},{8,1},{12,5},{14,7},{10,3},{9,8},{13,12},{... | collective-permute-start | bytes 2949128 | tf_op jit(solution)/shard_map/ppermute | solution.py:203
  65.7 13.1 %collective-permute-done.5.above = f32[5,12,32,128]{3,2,1,0:T(8,128)S(1)} collective-permute-done((f32[5,12,32,128]{3,2,1,0:T(8,128)S(1)}, f32[5,12,32,128]{3,2,1,0:T(8,128)S(1)}, u32[]{:S(2)}, u32[]{:S(2)}) %collective-permute-start.5) | collective-permute-done | bytes 983072 | tf_op jit(solution)/shard_map/ppermute | solution.py:203
  78.9 1.5 collective-permute-start.6
  80.4 5.3 %collective-permute-done.7.right = f32[5,24,4,128]{3,2,1,0:T(4,128)S(1)} collective-permute-done((f32[5,24,4,128]{3,2,1,0:T(4,128)S(1)}, f32[5,24,4,128]{3,2,1,0:T(4,128)S(1)}, u32[]{:S(2)}, u32[]{:S(2)}) %collective-permute-start.7) | collective-permute-done | bytes 245792 | tf_op jit(solution)/shard_map/ppermute | solution.py:209
  85.9 16.7 %advance.5 = (f32[5,8,32,128]{3,2,1,0:T(8,128)S(1)}, f32[5,16,32,128]{3,2,1,0:T(8,128)S(1)}) custom-call(f32[72]{0:T(128)S(1)} %concatenate.27.table, f32[5,12,32,128]{3,2,1,0:T(8,128)S(1)} %get-tuple-element.12.own, f32[5,12,32,128]{3,2,1,0:T(8,128)S(1)} %collective-permute-done.5.above, f32[5,24,4,128]{3,2,1,0:T(4,128)S(1)} %collective-permute-done.6.left, ...), custom_call_target="tpu_custom_call" | custom-call | tf_op jit(solution)/shard_map/advance/pallas_call | solution.py:247
  102.6 1.9 %collective-permute-start.8 = (f32[5,8,32,128]{3,2,1,0:T(8,128)S(1)}, f32[5,8,32,128]{3,2,1,0:T(8,128)S(1)}, u32[]{:S(2)}, u32[]{:S(2)}) collective-permute-start(f32[5,8,32,128]{3,2,1,0:T(8,128)S(1)} %get-tuple-element.15), channel_id=1, source_target_pairs={{1,0},{5,4},{7,6},{3,2},{8,1},{12,5},{14,7},{10,3},{9,8},{13,12},{... | collective-permute-start | bytes 1966088 | tf_op jit(solution)/shard_map/ppermute | solution.py:203
  104.6 9.9 %collective-permute-done.8.above = f32[5,8,32,128]{3,2,1,0:T(8,128)S(1)} collective-permute-done((f32[5,8,32,128]{3,2,1,0:T(8,128)S(1)}, f32[5,8,32,128]{3,2,1,0:T(8,128)S(1)}, u32[]{:S(2)}, u32[]{:S(2)}) %collective-permute-start.8) | collective-permute-done | bytes 655392 | tf_op jit(solution)/shard_map/ppermute | solution.py:203
  114.6 0.6 collective-permute-start.10
  115.2 1.3 collective-permute-start.9
  116.5 4.8 %collective-permute-done.10.right = f32[5,24,4,128]{3,2,1,0:T(4,128)S(1)} collective-permute-done((f32[5,24,4,128]{3,2,1,0:T(4,128)S(1)}, f32[5,24,4,128]{3,2,1,0:T(4,128)S(1)}, u32[]{:S(2)}, u32[]{:S(2)}) %collective-permute-start.10) | collective-permute-done | bytes 245792 | tf_op jit(solution)/shard_map/ppermute | solution.py:209
  121.3 0.7 collective-permute-done.9.left
  122.0 16.7 %advance.6 = (f32[5,12,32,128]{3,2,1,0:T(8,128)S(1)}, f32[5,12,32,128]{3,2,1,0:T(8,128)S(1)}) custom-call(f32[72]{0:T(128)S(1)} %concatenate.27.table, f32[5,16,32,128]{3,2,1,0:T(8,128)S(1)} %get-tuple-element.14.own, f32[5,8,32,128]{3,2,1,0:T(8,128)S(1)} %collective-permute-done.8.above, f32[5,24,4,128]{3,2,1,0:T(4,128)S(1)} %collective-permute-done.9.left, ...), custom_call_target="tpu_custom_call" | custom-call | tf_op jit(solution)/shard_map/advance/pallas_call | solution.py:247
  138.7 2.6 %collective-permute-start.11 = (f32[5,12,32,128]{3,2,1,0:T(8,128)S(1)}, f32[5,12,32,128]{3,2,1,0:T(8,128)S(1)}, u32[]{:S(2)}, u32[]{:S(2)}) collective-permute-start(f32[5,12,32,128]{3,2,1,0:T(8,128)S(1)} %get-tuple-element.16), channel_id=1, source_target_pairs={{0,0},{4,1},{6,2},{2,3},{1,4},{5,5},{7,6},{3,7},{8,8},{12,9},{14,1... | collective-permute-start | bytes 2949128 | tf_op jit(solution)/shard_map/ppermute | solution.py:203
  141.3 1.9 %collective-permute-start.12 = (f32[5,12,32,128]{3,2,1,0:T(8,128)S(1)}, f32[5,12,32,128]{3,2,1,0:T(8,128)S(1)}, u32[]{:S(2)}, u32[]{:S(2)}) collective-permute-start(f32[5,12,32,128]{3,2,1,0:T(8,128)S(1)} %get-tuple-element.17), channel_id=1, source_target_pairs={{1,0},{5,1},{7,2},{3,3},{8,4},{12,5},{14,6},{10,7},{9,8},{13,9},{1... | collective-permute-start | bytes 2949128 | tf_op jit(solution)/shard_map/ppermute | solution.py:203
  143.2 19.6 %collective-permute-done.11.own = f32[5,12,32,128]{3,2,1,0:T(8,128)S(1)} collective-permute-done((f32[5,12,32,128]{3,2,1,0:T(8,128)S(1)}, f32[5,12,32,128]{3,2,1,0:T(8,128)S(1)}, u32[]{:S(2)}, u32[]{:S(2)}) %collective-permute-start.11) | collective-permute-done | bytes 983072 | tf_op jit(solution)/shard_map/ppermute | solution.py:203
  162.9 1.8 collective-permute-done.12.above
  164.9 1.9 %collective-permute-start.13 = (f32[5,24,4,128]{3,2,1,0:T(4,128)S(1)}, f32[5,24,4,128]{3,2,1,0:T(4,128)S(1)}, u32[]{:S(2)}, u32[]{:S(2)}) collective-permute-start(f32[5,24,4,128]{3,2,1,0:T(4,128)S(1)} %pad_maximum_fusion.6), channel_id=1, source_target_pairs={{0,1},{1,2},{2,3},{3,0},{4,5},{5,6},{6,7},{7,4},{8,9},{9,10},{10,1... | collective-permute-start | bytes 737288 | tf_op jit(solution)/shard_map/ppermute | solution.py:208
  166.8 6.6 %collective-permute-done.14.right = f32[5,24,4,128]{3,2,1,0:T(4,128)S(1)} collective-permute-done((f32[5,24,4,128]{3,2,1,0:T(4,128)S(1)}, f32[5,24,4,128]{3,2,1,0:T(4,128)S(1)}, u32[]{:S(2)}, u32[]{:S(2)}) %collective-permute-start.14) | collective-permute-done | bytes 245792 | tf_op jit(solution)/shard_map/ppermute | solution.py:209
  173.4 13.3 %advance.7 = (f32[4,16,32,128]{3,2,1,0:T(8,128)}, f32[2,16,32,128]{3,2,1,0:T(8,128)}) custom-call(f32[72]{0:T(128)S(1)} %concatenate.27.table, f32[5,12,32,128]{3,2,1,0:T(8,128)S(1)} %collective-permute-done.11.own, f32[5,12,32,128]{3,2,1,0:T(8,128)S(1)} %collective-permute-done.12.above, f32[5,24,4,128]{3,2,1,0:T(4,128)S(1)} %collective-permute-done.13.left, ...), custom_call_target="tpu_custom_call" | custom-call | tf_op jit(solution)/shard_map/advance/pallas_call | solution.py:247
  (46 shorter events, 1.8 us)
Async XLA Ops:
  0.6 9.3 %copy-start = (s32[4,8,32,128]{3,2,1,0:T(8,128)S(1)}, s32[4,8,32,128]{3,2,1,0:T(8,128)}, u32[]{:S(2)}) copy-start(s32[4,8,32,128]{3,2,1,0:T(8,128)} %param.17) | copy-start | bytes 1572868
  0.6 10.8 %copy-start.1 = (f32[4,2]{0,1:T(2,128)S(1)}, f32[4,2]{0,1:T(2,128)}, u32[]{:S(2)}) copy-start(f32[4,2]{0,1:T(2,128)} %param.13) | copy-start | bytes 100
  0.7 10.8 %copy-start.2 = (f32[4,3]{1,0:T(4,128)S(1)}, f32[4,3]{1,0:T(4,128)}, u32[]{:S(2)}) copy-start(f32[4,3]{1,0:T(4,128)} %param.12) | copy-start | bytes 148
  0.7 10.9 %copy-start.4 = (f32[4]{0:T(128)S(1)}, f32[4]{0:T(128)}, u32[]{:S(2)}) copy-start(f32[4]{0:T(128)} %param.14) | copy-start | bytes 52
  3.8 33.0 %collective-permute-start.1 = (f32[5,16,32,128]{3,2,1,0:T(8,128)}, f32[5,16,32,128]{3,2,1,0:T(8,128)S(1)}, u32[]{:S(2)}, u32[]{:S(2)}) collective-permute-start(f32[5,16,32,128]{3,2,1,0:T(8,128)} %get-tuple-element.11), channel_id=1, source_target_pairs={{4,0},{5,4},{6,6},{7,2},{8,1},{9,5},{10,7},{11,3},{12,8},{13,12},{... | collective-permute-start | bytes 3932168 | tf_op jit(solution)/shard_map/ppermute | solution.py:203
  6.8 33.0 %copy-start.5 = (f32[2]{0:T(128)S(1)}, f32[2]{0:T(128)}, u32[]{:S(2)}) copy-start(f32[2]{0:T(128)} %param.15) | copy-start | bytes 28
  6.8 33.2 %copy-start.3 = (f32[16,2]{0,1:T(2,128)S(1)}, f32[16,2]{0,1:T(2,128)}, u32[]{:S(2)}) copy-start(f32[16,2]{0,1:T(2,128)} %param.16) | copy-start | bytes 388
  6.8 23.7 %collective-permute-start = (f32[5,8,32,128]{3,2,1,0:T(8,128)}, f32[5,8,32,128]{3,2,1,0:T(8,128)S(1)}, u32[]{:S(2)}, u32[]{:S(2)}) collective-permute-start(f32[5,8,32,128]{3,2,1,0:T(8,128)} %get-tuple-element.10), channel_id=1, source_target_pairs={{0,0},{1,4},{2,6},{3,2},{4,1},{5,5},{6,7},{7,3},{8,8},{9,12},{10,1... | collective-permute-start | bytes 1966088 | tf_op jit(solution)/shard_map/ppermute | solution.py:203
  10.7 29.8 %collective-permute-start.4 = (s32[3,8,32,128]{3,2,1,0:T(8,128)}, s32[3,8,32,128]{3,2,1,0:T(8,128)S(1)}, u32[]{:S(2)}, u32[]{:S(2)}) collective-permute-start(s32[3,8,32,128]{3,2,1,0:T(8,128)} %slice.67), channel_id=1, source_target_pairs={{28,25},{29,29},{30,31},{31,27}} | collective-permute-start | bytes 1179656 | tf_op jit(solution)/shard_map/ppermute | solution.py:226
  37.6 7.4 %collective-permute-start.3 = (f32[5,24,4,128]{3,2,1,0:T(4,128)}, f32[5,24,4,128]{3,2,1,0:T(4,128)S(1)}, u32[]{:S(2)}, u32[]{:S(2)}) collective-permute-start(f32[5,24,4,128]{3,2,1,0:T(4,128)} %pad_maximum_fusion.1), channel_id=1, source_target_pairs={{4,0},{6,4},{2,6},{0,2},{5,1},{7,5},{3,7},{1,3},{12,8},{14,12},{10... | collective-permute-start | bytes 737288 | tf_op jit(solution)/shard_map/ppermute | solution.py:209
  38.4 8.2 %collective-permute-start.2 = (f32[5,24,4,128]{3,2,1,0:T(4,128)}, f32[5,24,4,128]{3,2,1,0:T(4,128)S(1)}, u32[]{:S(2)}, u32[]{:S(2)}) collective-permute-start(f32[5,24,4,128]{3,2,1,0:T(4,128)} %pad_maximum_fusion), channel_id=1, source_target_pairs={{0,4},{4,6},{6,2},{2,0},{1,5},{5,7},{7,3},{3,1},{8,12},{12,14},{14... | collective-permute-start | bytes 737288 | tf_op jit(solution)/shard_map/ppermute | solution.py:208
  63.3 15.4 %collective-permute-start.5 = (f32[5,12,32,128]{3,2,1,0:T(8,128)S(1)}, f32[5,12,32,128]{3,2,1,0:T(8,128)S(1)}, u32[]{:S(2)}, u32[]{:S(2)}) collective-permute-start(f32[5,12,32,128]{3,2,1,0:T(8,128)S(1)} %get-tuple-element.13), channel_id=1, source_target_pairs={{1,0},{5,4},{7,6},{3,2},{8,1},{12,5},{14,7},{10,3},{9,8},{13,12},{... | collective-permute-start | bytes 2949128 | tf_op jit(solution)/shard_map/ppermute | solution.py:203
  78.8 6.9 %collective-permute-start.7 = (f32[5,24,4,128]{3,2,1,0:T(4,128)S(1)}, f32[5,24,4,128]{3,2,1,0:T(4,128)S(1)}, u32[]{:S(2)}, u32[]{:S(2)}) collective-permute-start(f32[5,24,4,128]{3,2,1,0:T(4,128)S(1)} %pad_maximum_fusion.3), channel_id=1, source_target_pairs={{4,0},{6,4},{2,6},{0,2},{5,1},{7,5},{3,7},{1,3},{12,8},{14,12},{10... | collective-permute-start | bytes 737288 | tf_op jit(solution)/shard_map/ppermute | solution.py:209
  78.9 6.9 %collective-permute-start.6 = (f32[5,24,4,128]{3,2,1,0:T(4,128)S(1)}, f32[5,24,4,128]{3,2,1,0:T(4,128)S(1)}, u32[]{:S(2)}, u32[]{:S(2)}) collective-permute-start(f32[5,24,4,128]{3,2,1,0:T(4,128)S(1)} %pad_maximum_fusion.2), channel_id=1, source_target_pairs={{0,4},{4,6},{6,2},{2,0},{1,5},{5,7},{7,3},{3,1},{8,12},{12,14},{14... | collective-permute-start | bytes 737288 | tf_op jit(solution)/shard_map/ppermute | solution.py:208
  102.6 11.9 %collective-permute-start.8 = (f32[5,8,32,128]{3,2,1,0:T(8,128)S(1)}, f32[5,8,32,128]{3,2,1,0:T(8,128)S(1)}, u32[]{:S(2)}, u32[]{:S(2)}) collective-permute-start(f32[5,8,32,128]{3,2,1,0:T(8,128)S(1)} %get-tuple-element.15), channel_id=1, source_target_pairs={{1,0},{5,4},{7,6},{3,2},{8,1},{12,5},{14,7},{10,3},{9,8},{13,12},{... | collective-permute-start | bytes 1966088 | tf_op jit(solution)/shard_map/ppermute | solution.py:203
  114.6 6.7 %collective-permute-start.10 = (f32[5,24,4,128]{3,2,1,0:T(4,128)S(1)}, f32[5,24,4,128]{3,2,1,0:T(4,128)S(1)}, u32[]{:S(2)}, u32[]{:S(2)}) collective-permute-start(f32[5,24,4,128]{3,2,1,0:T(4,128)S(1)} %pad_maximum_fusion.5), channel_id=1, source_target_pairs={{4,0},{6,4},{2,6},{0,2},{5,1},{7,5},{3,7},{1,3},{12,8},{14,12},{10... | collective-permute-start | bytes 737288 | tf_op jit(solution)/shard_map/ppermute | solution.py:209
  115.2 6.8 %collective-permute-start.9 = (f32[5,24,4,128]{3,2,1,0:T(4,128)S(1)}, f32[5,24,4,128]{3,2,1,0:T(4,128)S(1)}, u32[]{:S(2)}, u32[]{:S(2)}) collective-permute-start(f32[5,24,4,128]{3,2,1,0:T(4,128)S(1)} %pad_maximum_fusion.4), channel_id=1, source_target_pairs={{0,4},{4,6},{6,2},{2,0},{1,5},{5,7},{7,3},{3,1},{8,12},{12,14},{14... | collective-permute-start | bytes 737288 | tf_op jit(solution)/shard_map/ppermute | solution.py:208
  138.7 24.1 %collective-permute-start.11 = (f32[5,12,32,128]{3,2,1,0:T(8,128)S(1)}, f32[5,12,32,128]{3,2,1,0:T(8,128)S(1)}, u32[]{:S(2)}, u32[]{:S(2)}) collective-permute-start(f32[5,12,32,128]{3,2,1,0:T(8,128)S(1)} %get-tuple-element.16), channel_id=1, source_target_pairs={{0,0},{4,1},{6,2},{2,3},{1,4},{5,5},{7,6},{3,7},{8,8},{12,9},{14,1... | collective-permute-start | bytes 2949128 | tf_op jit(solution)/shard_map/ppermute | solution.py:203
  141.3 23.4 %collective-permute-start.12 = (f32[5,12,32,128]{3,2,1,0:T(8,128)S(1)}, f32[5,12,32,128]{3,2,1,0:T(8,128)S(1)}, u32[]{:S(2)}, u32[]{:S(2)}) collective-permute-start(f32[5,12,32,128]{3,2,1,0:T(8,128)S(1)} %get-tuple-element.17), channel_id=1, source_target_pairs={{1,0},{5,1},{7,2},{3,3},{8,4},{12,5},{14,6},{10,7},{9,8},{13,9},{1... | collective-permute-start | bytes 2949128 | tf_op jit(solution)/shard_map/ppermute | solution.py:203
  164.8 8.6 %collective-permute-start.14 = (f32[5,24,4,128]{3,2,1,0:T(4,128)S(1)}, f32[5,24,4,128]{3,2,1,0:T(4,128)S(1)}, u32[]{:S(2)}, u32[]{:S(2)}) collective-permute-start(f32[5,24,4,128]{3,2,1,0:T(4,128)S(1)} %pad_maximum_fusion.7), channel_id=1, source_target_pairs={{1,0},{2,1},{3,2},{0,3},{5,4},{6,5},{7,6},{4,7},{9,8},{10,9},{11,1... | collective-permute-start | bytes 737288 | tf_op jit(solution)/shard_map/ppermute | solution.py:209
  164.9 8.5 %collective-permute-start.13 = (f32[5,24,4,128]{3,2,1,0:T(4,128)S(1)}, f32[5,24,4,128]{3,2,1,0:T(4,128)S(1)}, u32[]{:S(2)}, u32[]{:S(2)}) collective-permute-start(f32[5,24,4,128]{3,2,1,0:T(4,128)S(1)} %pad_maximum_fusion.6), channel_id=1, source_target_pairs={{0,1},{1,2},{2,3},{3,0},{4,5},{5,6},{6,7},{7,4},{8,9},{9,10},{10,1... | collective-permute-start | bytes 737288 | tf_op jit(solution)/shard_map/ppermute | solution.py:208

commit v2 on v1

--- a/solution.py
+++ b/solution.py
@@ -14,6 +14,7 @@
 SENT = 5
 PAD = 8
 DT = 0.04
+PLANES = 2
 AXES = ("grow", "lat")
 GRAD, CENTER, COUPLE, LATENT, RELEASE, SPREAD, STAY, MELT = 0, 12, 16, 24, 28, 36, 38, 40
 
@@ -24,9 +25,9 @@
         [
             scaled.reshape(-1),
             1.0 + DT - 2.0 * jnp.sum(scaled, axis=1),
-            (DT * composition).reshape(-1),
-            DT * latent,
-            composition.reshape(-1),
+            (DT * (composition - jnp.mean(composition, axis=0))).reshape(-1),
+            DT * (latent - jnp.mean(latent)),
+            (composition - composition[3]).reshape(-1),
             DT * diffusivity,
             1.0 - 6.0 * DT * diffusivity,
             melt_table.reshape(-1),
@@ -74,87 +75,90 @@
         xsum = [src[f, e, pl.ds(at + 1, 8)] + src[f, e, pl.ds(at - 1, 8)] for f in range(6)]
         ysum = [pltpu.roll(v, 1, 1) + pltpu.roll(v, v.shape[1] - 1, 1) for v in mid]
         m0, m1 = mid[4], mid[5]
-        guess = []
-        for a in range(4):
-            guess.append(
-                table[GRAD + 3 * a] * gsum[a]
-                + table[GRAD + 3 * a + 1] * xsum[a]
-                + table[GRAD + 3 * a + 2] * ysum[a]
-                + table[CENTER + a] * mid[a]
-                - table[COUPLE + 2 * a] * m0
-                - table[COUPLE + 2 * a + 1] * m1
-                - table[LATENT + a] * theta
-            )
-        phase_sum = mid[0] + mid[1] + mid[2] + mid[3]
-        mean = 0.25 * (guess[0] + guess[1] + guess[2] + guess[3] - phase_sum)
-        clipped = [jnp.clip(g - mean, 0.0, 1.0) for g in guess]
+        spread = [
+            table[GRAD + 3 * a] * gsum[a]
+            + table[GRAD + 3 * a + 1] * xsum[a]
+            + table[GRAD + 3 * a + 2] * ysum[a]
+            + table[CENTER + a] * mid[a]
+            for a in range(4)
+        ]
+        mean = 0.25 * (spread[0] + spread[1] + spread[2] + spread[3]) - 0.25
+        trial = [
+            spread[a]
+            - mean
+            - table[COUPLE + 2 * a] * m0
+            - table[COUPLE + 2 * a + 1] * m1
+            - table[LATENT + a] * theta
+            for a in range(3)
+        ]
+        trial.append(1.0 - trial[0] - trial[1] - trial[2])
+        clipped = [jnp.clip(t, 0.0, 1.0) for t in trial]
         inverse = 1.0 / (clipped[0] + clipped[1] + clipped[2] + clipped[3])
         new = [c * inverse for c in clipped]
-        change = [n - v for n, v in zip(new, mid)]
+        change = [n - v for n, v in zip(new[:3], mid[:3])]
         for k in range(2):
             release = table[RELEASE + k] * change[0]
-            for a in range(1, 4):
+            for a in range(1, 3):
                 release = release + table[RELEASE + 2 * a + k] * change[a]
             sides = gsum[4 + k] + xsum[4 + k] + ysum[4 + k]
             new.append(table[SPREAD + k] * sides + table[STAY + k] * mid[4 + k] - release)
         return new
 
+    def sweep(src, first, stop, tiles, put):
+        @pl.loop(0, (stop - first) // PLANES)
+        def _(i):
+            for p in range(PLANES):
+                e = first + PLANES * i + p
+                for at in tiles:
+                    put(e, at, advance(src, e, at))
+
     buffers = (even, odd)
     for step in range(1, STEPS):
         src, dst = buffers[(step - 1) % 2], buffers[step % 2]
 
-        @pl.loop(step, height - step)
-        def _(e, src=src, dst=dst):
-            for t in range(rows // 8 + 1):
-                at = PAD - STEPS + 8 * t
-                for f, value in enumerate(advance(src, e, at)):
-                    dst[f, e, pl.ds(at, 8)] = value
+        def keep(e, at, new, dst=dst):
+            for f in range(6):
+                dst[f, e, pl.ds(at, 8)] = new[f]
+
+        sweep(src, step, height - step, [PAD - STEPS + 8 * t for t in range(rows // 8 + 1)], keep)
 
     src = buffers[(STEPS - 1) % 2]
-    if last:
-        phases, potentials = outs
-
-        def put(o, here, new):
-            for a in range(4):
-                phases[a, o, here] = new[a]
-            for k in range(2):
-                potentials[k, o, here] = new[4 + k]
-
-    else:
-        climbing, staying = outs
-
-        def put(o, here, new):
-            sent = [new[f] for f in (0, 1, 2, 4, 5)]
-
-            @pl.when(o < climbing.shape[1])
-            def _():
-                for f in range(SENT):
-                    climbing[f, o, here] = sent[f]
-
-            @pl.when(o >= keeps)
-            def _():
-                for f in range(SENT):
-                    staying[f, o - keeps, here] = sent[f]
-
-    @pl.loop(0, block)
-    def _(o):
-        for t in range(rows // 8):
-            put(o, pl.ds(8 * t, 8), advance(src, o + STEPS, PAD + 8 * t))
+
+    def put(climbs, stays):
+        def write(e, at, new):
+            o, here = e - STEPS, pl.ds(at - PAD, 8)
+            if last:
+                for a in range(4):
+                    outs[0][a, o, here] = new[a]
+                for k in range(2):
+                    outs[1][k, o, here] = new[4 + k]
+                return
+            for f, value in enumerate([new[f] for f in (0, 1, 2, 4, 5)]):
+                if climbs:
+                    outs[0][f, o, here] = value
+                if stays:
+                    outs[1][f, o - keeps, here] = value
+
+        return write
+
+    climbed = block if last else outs[0].shape[1]
+    for first, stop in ((0, keeps), (keeps, climbed), (climbed, block)):
+        write = put(stop <= climbed, first >= keeps)
+        sweep(src, first + STEPS, stop + STEPS, [PAD + 8 * t for t in range(rows // 8)], write)
 
     fresh = ng * block + SHIFT * turn - (ng - 1) * block - base
 
     @pl.when(place == ng - 1)
     def _():
-        @pl.loop(0, SHIFT)
-        def _(j):
+        for j in range(SHIFT):
+            write = put(fresh + j < climbed, fresh + j >= keeps)
             for t in range(rows // 8):
-                here = pl.ds(8 * t, 8)
-                row = index[j, here]
+                row = index[j, pl.ds(8 * t, 8)]
                 mu = [jnp.zeros(row.shape, jnp.float32)] * 2
                 for m in range((table.shape[0] - MELT) // 2):
                     mu = [jnp.where(row == m, table[MELT + 2 * m + k], mu[k]) for k in range(2)]
                 none = jnp.zeros(row.shape, jnp.float32)
-                put(fresh + j, here, [none, none, none, none + 1.0] + mu)
+                write(fresh + j + STEPS, PAD + 8 * t, [none, none, none, none + 1.0] + mu)
 
 
 def prepare_kernel(labels, roughness, potential, climbing, staying):

time: 187 us -> 163 us (0.87)
  Pallas kernels: 66.4 us -> 42.6 us
    pallas_call x4, Pallas kernels: 63.3 us -> 39.5 us  [on_device(): pl.pallas_call(functools.partial(round_kernel, turn, home_place if last e...]
  transfers between devices with their start and end apart: 15 -> 15, of which waited for: 13 -> 13; matrix products, arithmetic and copies ran while one was open for 2% -> 3% of each run, Pallas kernels for 0% -> 0%
where the time goes in v2:
time: 163 us
  waiting for transfers between devices  91.6 us (56%)
  Pallas kernels  42.6 us (26%)
  starting transfers between devices  22.3 us (14%)
  other arithmetic  2.74 us (2%)
  local copies, waits for them, and re-layouts  2.07 us (1%)
    ppermute x6, waiting for transfers between devices, moved(): return lax.ppermute(array, AXES, route)  68.1 us
    pallas_call x4, Pallas kernels, on_device(): pl.pallas_call(functools.partial(round_kernel, turn, home_place if last e...  39.5 us
    ppermute x4, waiting for transfers between devices, sides(): lax.ppermute(first, AXES, [(where(g, (l + 1) % nl), where(g, l)) for g, l...  21.1 us
    ppermute x6, starting transfers between devices, moved(): return lax.ppermute(array, AXES, route)  14.8 us
    ppermute x4, starting transfers between devices, sides(): lax.ppermute(final, AXES, [(where(g, l), where(g, (l + 1) % nl)) for g, l...  6.18 us
  transfers between devices with their start and end apart: 15, of which 13 were waited for; matrix products, arithmetic and copies ran while one was open for 3% of the time, Pallas kernels for 0%

profile of v2, /device:TPU:17, one launch (start us, length us, event | category | flops | bytes accessed | tf_op | source)
XLA Modules:
  0.0 162.9 jit_solution(260432708481197963)
XLA Ops:
  0.7 3.1 %prepare.1 = (f32[5,16,32,128]{3,2,1,0:T(8,128)}, f32[5,8,32,128]{3,2,1,0:T(8,128)}) custom-call(s32[16,32,128]{2,1,0:T(8,128)} %labels.1, f32[4,16,32,128]{3,2,1,0:T(8,128)} %roughness.1, f32[2,16,32,128]{3,2,1,0:T(8,128)} %potential.1), custom_call_target="tpu_custom_call" | custom-call | tf_op jit(solution)/shard_map/prepare/pallas_call | solution.py:222
  3.8 3.0 %collective-permute-start.1 = (f32[5,16,32,128]{3,2,1,0:T(8,128)}, f32[5,16,32,128]{3,2,1,0:T(8,128)S(1)}, u32[]{:S(2)}, u32[]{:S(2)}) collective-permute-start(f32[5,16,32,128]{3,2,1,0:T(8,128)} %get-tuple-element.11), channel_id=1, source_target_pairs={{4,0},{5,4},{6,6},{7,2},{8,1},{9,5},{10,7},{11,3},{12,8},{13,12},{... | collective-permute-start | bytes 3932168 | tf_op jit(solution)/shard_map/ppermute | solution.py:207
  6.8 3.1 %collective-permute-start = (f32[5,8,32,128]{3,2,1,0:T(8,128)}, f32[5,8,32,128]{3,2,1,0:T(8,128)S(1)}, u32[]{:S(2)}, u32[]{:S(2)}) collective-permute-start(f32[5,8,32,128]{3,2,1,0:T(8,128)} %get-tuple-element.10), channel_id=1, source_target_pairs={{0,0},{1,4},{2,6},{3,2},{4,1},{5,5},{6,7},{7,3},{8,8},{9,12},{10,1... | collective-permute-start | bytes 1966088 | tf_op jit(solution)/shard_map/ppermute | solution.py:207
  9.9 0.8 slice.71
  10.7 0.7 collective-permute-start.4
  11.4 0.6 reduce_sum.29
  13.0 17.4 %collective-permute-done.own = f32[5,8,32,128]{3,2,1,0:T(8,128)S(1)} collective-permute-done((f32[5,8,32,128]{3,2,1,0:T(8,128)}, f32[5,8,32,128]{3,2,1,0:T(8,128)S(1)}, u32[]{:S(2)}, u32[]{:S(2)}) %collective-permute-start) | collective-permute-done | bytes 655392 | tf_op jit(solution)/shard_map/ppermute | solution.py:207
  30.5 6.3 %collective-permute-done.1.above = f32[5,16,32,128]{3,2,1,0:T(8,128)S(1)} collective-permute-done((f32[5,16,32,128]{3,2,1,0:T(8,128)}, f32[5,16,32,128]{3,2,1,0:T(8,128)S(1)}, u32[]{:S(2)}, u32[]{:S(2)}) %collective-permute-start.1) | collective-permute-done | bytes 1310752 | tf_op jit(solution)/shard_map/ppermute | solution.py:207
  36.9 0.8 pad_maximum_fusion.1
  37.6 0.8 pad_maximum_fusion
  38.4 1.5 collective-permute-start.2
  40.6 4.4 %collective-permute-done.3.right = f32[5,24,4,128]{3,2,1,0:T(4,128)S(1)} collective-permute-done((f32[5,24,4,128]{3,2,1,0:T(4,128)}, f32[5,24,4,128]{3,2,1,0:T(4,128)S(1)}, u32[]{:S(2)}, u32[]{:S(2)}) %collective-permute-start.3) | collective-permute-done | bytes 245792 | tf_op jit(solution)/shard_map/ppermute | solution.py:213
  45.0 1.6 collective-permute-done.2.left
  46.6 9.6 %advance.4 = (f32[5,12,32,128]{3,2,1,0:T(8,128)S(1)}, f32[5,12,32,128]{3,2,1,0:T(8,128)S(1)}) custom-call(f32[72]{0:T(128)S(1)} %concatenate.27.table, f32[5,8,32,128]{3,2,1,0:T(8,128)S(1)} %collective-permute-done.own, f32[5,16,32,128]{3,2,1,0:T(8,128)S(1)} %collective-permute-done.1.above, f32[5,24,4,128]{3,2,1,0:T(4,128)S(1)} %collective-permute-done.2.left, ...), custom_call_target="tpu_custom_call" | custom-call | tf_op jit(solution)/shard_map/advance/pallas_call | solution.py:251
  56.2 2.3 %collective-permute-start.5 = (f32[5,12,32,128]{3,2,1,0:T(8,128)S(1)}, f32[5,12,32,128]{3,2,1,0:T(8,128)S(1)}, u32[]{:S(2)}, u32[]{:S(2)}) collective-permute-start(f32[5,12,32,128]{3,2,1,0:T(8,128)S(1)} %get-tuple-element.13), channel_id=1, source_target_pairs={{1,0},{5,4},{7,6},{3,2},{8,1},{12,5},{14,7},{10,3},{9,8},{13,12},{... | collective-permute-start | bytes 2949128 | tf_op jit(solution)/shard_map/ppermute | solution.py:207
  58.6 13.1 %collective-permute-done.5.above = f32[5,12,32,128]{3,2,1,0:T(8,128)S(1)} collective-permute-done((f32[5,12,32,128]{3,2,1,0:T(8,128)S(1)}, f32[5,12,32,128]{3,2,1,0:T(8,128)S(1)}, u32[]{:S(2)}, u32[]{:S(2)}) %collective-permute-start.5) | collective-permute-done | bytes 983072 | tf_op jit(solution)/shard_map/ppermute | solution.py:207
  71.9 1.5 collective-permute-start.6
  73.4 5.3 %collective-permute-done.7.right = f32[5,24,4,128]{3,2,1,0:T(4,128)S(1)} collective-permute-done((f32[5,24,4,128]{3,2,1,0:T(4,128)S(1)}, f32[5,24,4,128]{3,2,1,0:T(4,128)S(1)}, u32[]{:S(2)}, u32[]{:S(2)}) %collective-permute-start.7) | collective-permute-done | bytes 245792 | tf_op jit(solution)/shard_map/ppermute | solution.py:213
  78.8 9.6 %advance.5 = (f32[5,8,32,128]{3,2,1,0:T(8,128)S(1)}, f32[5,16,32,128]{3,2,1,0:T(8,128)S(1)}) custom-call(f32[72]{0:T(128)S(1)} %concatenate.27.table, f32[5,12,32,128]{3,2,1,0:T(8,128)S(1)} %get-tuple-element.12.own, f32[5,12,32,128]{3,2,1,0:T(8,128)S(1)} %collective-permute-done.5.above, f32[5,24,4,128]{3,2,1,0:T(4,128)S(1)} %collective-permute-done.6.left, ...), custom_call_target="tpu_custom_call" | custom-call | tf_op jit(solution)/shard_map/advance/pallas_call | solution.py:251
  88.4 1.9 %collective-permute-start.8 = (f32[5,8,32,128]{3,2,1,0:T(8,128)S(1)}, f32[5,8,32,128]{3,2,1,0:T(8,128)S(1)}, u32[]{:S(2)}, u32[]{:S(2)}) collective-permute-start(f32[5,8,32,128]{3,2,1,0:T(8,128)S(1)} %get-tuple-element.15), channel_id=1, source_target_pairs={{1,0},{5,4},{7,6},{3,2},{8,1},{12,5},{14,7},{10,3},{9,8},{13,12},{... | collective-permute-start | bytes 1966088 | tf_op jit(solution)/shard_map/ppermute | solution.py:207
  90.4 9.9 %collective-permute-done.8.above = f32[5,8,32,128]{3,2,1,0:T(8,128)S(1)} collective-permute-done((f32[5,8,32,128]{3,2,1,0:T(8,128)S(1)}, f32[5,8,32,128]{3,2,1,0:T(8,128)S(1)}, u32[]{:S(2)}, u32[]{:S(2)}) %collective-permute-start.8) | collective-permute-done | bytes 655392 | tf_op jit(solution)/shard_map/ppermute | solution.py:207
  101.1 1.3 collective-permute-start.9
  102.4 4.8 %collective-permute-done.10.right = f32[5,24,4,128]{3,2,1,0:T(4,128)S(1)} collective-permute-done((f32[5,24,4,128]{3,2,1,0:T(4,128)S(1)}, f32[5,24,4,128]{3,2,1,0:T(4,128)S(1)}, u32[]{:S(2)}, u32[]{:S(2)}) %collective-permute-start.10) | collective-permute-done | bytes 245792 | tf_op jit(solution)/shard_map/ppermute | solution.py:213
  107.1 0.7 collective-permute-done.9.left
  107.9 9.6 %advance.6 = (f32[5,12,32,128]{3,2,1,0:T(8,128)S(1)}, f32[5,12,32,128]{3,2,1,0:T(8,128)S(1)}) custom-call(f32[72]{0:T(128)S(1)} %concatenate.27.table, f32[5,16,32,128]{3,2,1,0:T(8,128)S(1)} %get-tuple-element.14.own, f32[5,8,32,128]{3,2,1,0:T(8,128)S(1)} %collective-permute-done.8.above, f32[5,24,4,128]{3,2,1,0:T(4,128)S(1)} %collective-permute-done.9.left, ...), custom_call_target="tpu_custom_call" | custom-call | tf_op jit(solution)/shard_map/advance/pallas_call | solution.py:251
  117.5 2.6 %collective-permute-start.11 = (f32[5,12,32,128]{3,2,1,0:T(8,128)S(1)}, f32[5,12,32,128]{3,2,1,0:T(8,128)S(1)}, u32[]{:S(2)}, u32[]{:S(2)}) collective-permute-start(f32[5,12,32,128]{3,2,1,0:T(8,128)S(1)} %get-tuple-element.16), channel_id=1, source_target_pairs={{0,0},{4,1},{6,2},{2,3},{1,4},{5,5},{7,6},{3,7},{8,8},{12,9},{14,1... | collective-permute-start | bytes 2949128 | tf_op jit(solution)/shard_map/ppermute | solution.py:207
  120.0 1.9 %collective-permute-start.12 = (f32[5,12,32,128]{3,2,1,0:T(8,128)S(1)}, f32[5,12,32,128]{3,2,1,0:T(8,128)S(1)}, u32[]{:S(2)}, u32[]{:S(2)}) collective-permute-start(f32[5,12,32,128]{3,2,1,0:T(8,128)S(1)} %get-tuple-element.17), channel_id=1, source_target_pairs={{1,0},{5,1},{7,2},{3,3},{8,4},{12,5},{14,6},{10,7},{9,8},{13,9},{1... | collective-permute-start | bytes 2949128 | tf_op jit(solution)/shard_map/ppermute | solution.py:207
  122.0 19.6 %collective-permute-done.11.own = f32[5,12,32,128]{3,2,1,0:T(8,128)S(1)} collective-permute-done((f32[5,12,32,128]{3,2,1,0:T(8,128)S(1)}, f32[5,12,32,128]{3,2,1,0:T(8,128)S(1)}, u32[]{:S(2)}, u32[]{:S(2)}) %collective-permute-start.11) | collective-permute-done | bytes 983072 | tf_op jit(solution)/shard_map/ppermute | solution.py:207
  141.6 1.8 %collective-permute-done.12.above = f32[5,12,32,128]{3,2,1,0:T(8,128)S(1)} collective-permute-done((f32[5,12,32,128]{3,2,1,0:T(8,128)S(1)}, f32[5,12,32,128]{3,2,1,0:T(8,128)S(1)}, u32[]{:S(2)}, u32[]{:S(2)}) %collective-permute-start.12) | collective-permute-done | bytes 983072 | tf_op jit(solution)/shard_map/ppermute | solution.py:207
  143.7 1.9 %collective-permute-start.13 = (f32[5,24,4,128]{3,2,1,0:T(4,128)S(1)}, f32[5,24,4,128]{3,2,1,0:T(4,128)S(1)}, u32[]{:S(2)}, u32[]{:S(2)}) collective-permute-start(f32[5,24,4,128]{3,2,1,0:T(4,128)S(1)} %pad_maximum_fusion.6), channel_id=1, source_target_pairs={{0,1},{1,2},{2,3},{3,0},{4,5},{5,6},{6,7},{7,4},{8,9},{9,10},{10,1... | collective-permute-start | bytes 737288 | tf_op jit(solution)/shard_map/ppermute | solution.py:212
  145.6 6.6 %collective-permute-done.14.right = f32[5,24,4,128]{3,2,1,0:T(4,128)S(1)} collective-permute-done((f32[5,24,4,128]{3,2,1,0:T(4,128)S(1)}, f32[5,24,4,128]{3,2,1,0:T(4,128)S(1)}, u32[]{:S(2)}, u32[]{:S(2)}) %collective-permute-start.14) | collective-permute-done | bytes 245792 | tf_op jit(solution)/shard_map/ppermute | solution.py:213
  152.2 10.7 %advance.7 = (f32[4,16,32,128]{3,2,1,0:T(8,128)}, f32[2,16,32,128]{3,2,1,0:T(8,128)}) custom-call(f32[72]{0:T(128)S(1)} %concatenate.27.table, f32[5,12,32,128]{3,2,1,0:T(8,128)S(1)} %collective-permute-done.11.own, f32[5,12,32,128]{3,2,1,0:T(8,128)S(1)} %collective-permute-done.12.above, f32[5,24,4,128]{3,2,1,0:T(4,128)S(1)} %collective-permute-done.13.left, ...), custom_call_target="tpu_custom_call" | custom-call | tf_op jit(solution)/shard_map/advance/pallas_call | solution.py:251
  (50 shorter events, 2.8 us)
Async XLA Ops:
  0.6 9.3 %copy-start = (s32[4,8,32,128]{3,2,1,0:T(8,128)S(1)}, s32[4,8,32,128]{3,2,1,0:T(8,128)}, u32[]{:S(2)}) copy-start(s32[4,8,32,128]{3,2,1,0:T(8,128)} %param.17) | copy-start | bytes 1572868
  0.6 10.8 %copy-start.4 = (f32[4]{0:T(128)S(1)}, f32[4]{0:T(128)}, u32[]{:S(2)}) copy-start(f32[4]{0:T(128)} %param.14) | copy-start | bytes 52
  0.7 11.3 %copy-start.1 = (f32[4,2]{0,1:T(2,128)S(1)}, f32[4,2]{0,1:T(2,128)}, u32[]{:S(2)}) copy-start(f32[4,2]{0,1:T(2,128)} %param.13) | copy-start | bytes 100
  0.7 12.2 %copy-start.2 = (f32[4,3]{1,0:T(4,128)S(1)}, f32[4,3]{1,0:T(4,128)}, u32[]{:S(2)}) copy-start(f32[4,3]{1,0:T(4,128)} %param.12) | copy-start | bytes 148
  3.8 33.0 %collective-permute-start.1 = (f32[5,16,32,128]{3,2,1,0:T(8,128)}, f32[5,16,32,128]{3,2,1,0:T(8,128)S(1)}, u32[]{:S(2)}, u32[]{:S(2)}) collective-permute-start(f32[5,16,32,128]{3,2,1,0:T(8,128)} %get-tuple-element.11), channel_id=1, source_target_pairs={{4,0},{5,4},{6,6},{7,2},{8,1},{9,5},{10,7},{11,3},{12,8},{13,12},{... | collective-permute-start | bytes 3932168 | tf_op jit(solution)/shard_map/ppermute | solution.py:207
  6.8 33.0 %copy-start.5 = (f32[2]{0:T(128)S(1)}, f32[2]{0:T(128)}, u32[]{:S(2)}) copy-start(f32[2]{0:T(128)} %param.15) | copy-start | bytes 28
  6.8 33.5 %copy-start.3 = (f32[16,2]{0,1:T(2,128)S(1)}, f32[16,2]{0,1:T(2,128)}, u32[]{:S(2)}) copy-start(f32[16,2]{0,1:T(2,128)} %param.16) | copy-start | bytes 388
  6.8 23.7 %collective-permute-start = (f32[5,8,32,128]{3,2,1,0:T(8,128)}, f32[5,8,32,128]{3,2,1,0:T(8,128)S(1)}, u32[]{:S(2)}, u32[]{:S(2)}) collective-permute-start(f32[5,8,32,128]{3,2,1,0:T(8,128)} %get-tuple-element.10), channel_id=1, source_target_pairs={{0,0},{1,4},{2,6},{3,2},{4,1},{5,5},{6,7},{7,3},{8,8},{9,12},{10,1... | collective-permute-start | bytes 1966088 | tf_op jit(solution)/shard_map/ppermute | solution.py:207
  10.7 29.8 %collective-permute-start.4 = (s32[3,8,32,128]{3,2,1,0:T(8,128)}, s32[3,8,32,128]{3,2,1,0:T(8,128)S(1)}, u32[]{:S(2)}, u32[]{:S(2)}) collective-permute-start(s32[3,8,32,128]{3,2,1,0:T(8,128)} %slice.71), channel_id=1, source_target_pairs={{28,25},{29,29},{30,31},{31,27}} | collective-permute-start | bytes 1179656 | tf_op jit(solution)/shard_map/ppermute | solution.py:230
  37.6 7.4 %collective-permute-start.3 = (f32[5,24,4,128]{3,2,1,0:T(4,128)}, f32[5,24,4,128]{3,2,1,0:T(4,128)S(1)}, u32[]{:S(2)}, u32[]{:S(2)}) collective-permute-start(f32[5,24,4,128]{3,2,1,0:T(4,128)} %pad_maximum_fusion.1), channel_id=1, source_target_pairs={{4,0},{6,4},{2,6},{0,2},{5,1},{7,5},{3,7},{1,3},{12,8},{14,12},{10... | collective-permute-start | bytes 737288 | tf_op jit(solution)/shard_map/ppermute | solution.py:213
  38.4 8.2 %collective-permute-start.2 = (f32[5,24,4,128]{3,2,1,0:T(4,128)}, f32[5,24,4,128]{3,2,1,0:T(4,128)S(1)}, u32[]{:S(2)}, u32[]{:S(2)}) collective-permute-start(f32[5,24,4,128]{3,2,1,0:T(4,128)} %pad_maximum_fusion), channel_id=1, source_target_pairs={{0,4},{4,6},{6,2},{2,0},{1,5},{5,7},{7,3},{3,1},{8,12},{12,14},{14... | collective-permute-start | bytes 737288 | tf_op jit(solution)/shard_map/ppermute | solution.py:212
  56.2 15.4 %collective-permute-start.5 = (f32[5,12,32,128]{3,2,1,0:T(8,128)S(1)}, f32[5,12,32,128]{3,2,1,0:T(8,128)S(1)}, u32[]{:S(2)}, u32[]{:S(2)}) collective-permute-start(f32[5,12,32,128]{3,2,1,0:T(8,128)S(1)} %get-tuple-element.13), channel_id=1, source_target_pairs={{1,0},{5,4},{7,6},{3,2},{8,1},{12,5},{14,7},{10,3},{9,8},{13,12},{... | collective-permute-start | bytes 2949128 | tf_op jit(solution)/shard_map/ppermute | solution.py:207
  71.7 6.9 %collective-permute-start.7 = (f32[5,24,4,128]{3,2,1,0:T(4,128)S(1)}, f32[5,24,4,128]{3,2,1,0:T(4,128)S(1)}, u32[]{:S(2)}, u32[]{:S(2)}) collective-permute-start(f32[5,24,4,128]{3,2,1,0:T(4,128)S(1)} %pad_maximum_fusion.3), channel_id=1, source_target_pairs={{4,0},{6,4},{2,6},{0,2},{5,1},{7,5},{3,7},{1,3},{12,8},{14,12},{10... | collective-permute-start | bytes 737288 | tf_op jit(solution)/shard_map/ppermute | solution.py:213
  71.9 6.9 %collective-permute-start.6 = (f32[5,24,4,128]{3,2,1,0:T(4,128)S(1)}, f32[5,24,4,128]{3,2,1,0:T(4,128)S(1)}, u32[]{:S(2)}, u32[]{:S(2)}) collective-permute-start(f32[5,24,4,128]{3,2,1,0:T(4,128)S(1)} %pad_maximum_fusion.2), channel_id=1, source_target_pairs={{0,4},{4,6},{6,2},{2,0},{1,5},{5,7},{7,3},{3,1},{8,12},{12,14},{14... | collective-permute-start | bytes 737288 | tf_op jit(solution)/shard_map/ppermute | solution.py:212
  88.4 11.9 %collective-permute-start.8 = (f32[5,8,32,128]{3,2,1,0:T(8,128)S(1)}, f32[5,8,32,128]{3,2,1,0:T(8,128)S(1)}, u32[]{:S(2)}, u32[]{:S(2)}) collective-permute-start(f32[5,8,32,128]{3,2,1,0:T(8,128)S(1)} %get-tuple-element.15), channel_id=1, source_target_pairs={{1,0},{5,4},{7,6},{3,2},{8,1},{12,5},{14,7},{10,3},{9,8},{13,12},{... | collective-permute-start | bytes 1966088 | tf_op jit(solution)/shard_map/ppermute | solution.py:207
  100.4 6.7 %collective-permute-start.10 = (f32[5,24,4,128]{3,2,1,0:T(4,128)S(1)}, f32[5,24,4,128]{3,2,1,0:T(4,128)S(1)}, u32[]{:S(2)}, u32[]{:S(2)}) collective-permute-start(f32[5,24,4,128]{3,2,1,0:T(4,128)S(1)} %pad_maximum_fusion.5), channel_id=1, source_target_pairs={{4,0},{6,4},{2,6},{0,2},{5,1},{7,5},{3,7},{1,3},{12,8},{14,12},{10... | collective-permute-start | bytes 737288 | tf_op jit(solution)/shard_map/ppermute | solution.py:213
  101.1 6.8 %collective-permute-start.9 = (f32[5,24,4,128]{3,2,1,0:T(4,128)S(1)}, f32[5,24,4,128]{3,2,1,0:T(4,128)S(1)}, u32[]{:S(2)}, u32[]{:S(2)}) collective-permute-start(f32[5,24,4,128]{3,2,1,0:T(4,128)S(1)} %pad_maximum_fusion.4), channel_id=1, source_target_pairs={{0,4},{4,6},{6,2},{2,0},{1,5},{5,7},{7,3},{3,1},{8,12},{12,14},{14... | collective-permute-start | bytes 737288 | tf_op jit(solution)/shard_map/ppermute | solution.py:212
  117.5 24.1 %collective-permute-start.11 = (f32[5,12,32,128]{3,2,1,0:T(8,128)S(1)}, f32[5,12,32,128]{3,2,1,0:T(8,128)S(1)}, u32[]{:S(2)}, u32[]{:S(2)}) collective-permute-start(f32[5,12,32,128]{3,2,1,0:T(8,128)S(1)} %get-tuple-element.16), channel_id=1, source_target_pairs={{0,0},{4,1},{6,2},{2,3},{1,4},{5,5},{7,6},{3,7},{8,8},{12,9},{14,1... | collective-permute-start | bytes 2949128 | tf_op jit(solution)/shard_map/ppermute | solution.py:207
  120.0 23.4 %collective-permute-start.12 = (f32[5,12,32,128]{3,2,1,0:T(8,128)S(1)}, f32[5,12,32,128]{3,2,1,0:T(8,128)S(1)}, u32[]{:S(2)}, u32[]{:S(2)}) collective-permute-start(f32[5,12,32,128]{3,2,1,0:T(8,128)S(1)} %get-tuple-element.17), channel_id=1, source_target_pairs={{1,0},{5,1},{7,2},{3,3},{8,4},{12,5},{14,6},{10,7},{9,8},{13,9},{1... | collective-permute-start | bytes 2949128 | tf_op jit(solution)/shard_map/ppermute | solution.py:207
  143.5 8.6 %collective-permute-start.14 = (f32[5,24,4,128]{3,2,1,0:T(4,128)S(1)}, f32[5,24,4,128]{3,2,1,0:T(4,128)S(1)}, u32[]{:S(2)}, u32[]{:S(2)}) collective-permute-start(f32[5,24,4,128]{3,2,1,0:T(4,128)S(1)} %pad_maximum_fusion.7), channel_id=1, source_target_pairs={{1,0},{2,1},{3,2},{0,3},{5,4},{6,5},{7,6},{4,7},{9,8},{10,9},{11,1... | collective-permute-start | bytes 737288 | tf_op jit(solution)/shard_map/ppermute | solution.py:213
  143.7 8.5 %collective-permute-start.13 = (f32[5,24,4,128]{3,2,1,0:T(4,128)S(1)}, f32[5,24,4,128]{3,2,1,0:T(4,128)S(1)}, u32[]{:S(2)}, u32[]{:S(2)}) collective-permute-start(f32[5,24,4,128]{3,2,1,0:T(4,128)S(1)} %pad_maximum_fusion.6), channel_id=1, source_target_pairs={{0,1},{1,2},{2,3},{3,0},{4,5},{5,6},{6,7},{7,4},{8,9},{9,10},{10,1... | collective-permute-start | bytes 737288 | tf_op jit(solution)/shard_map/ppermute | solution.py:212

commit v3 on v2

v3 whole, which is shorter than its diff:
```python
import functools

import jax
import jax.numpy as jnp
from jax import lax
from jax.experimental import pallas as pl
from jax.experimental.pallas import tpu as pltpu
from jax.sharding import PartitionSpec as P

STEPS = 4
ROUNDS = 4
SHIFT = 8
SENT = (0, 1, 2, 4, 5)
PAD = 8
DT = 0.04
PLANES = 2
AXES = ("grow", "lat")
GRAD, CENTER, COUPLE, LATENT, RELEASE, SPREAD, STAY, MELT = 0, 12, 16, 24, 28, 36, 38, 40


def scalar_table(grad_coef, composition, latent, diffusivity, melt_table):
    scaled = DT * grad_coef
    return jnp.concatenate(
        [
            scaled.reshape(-1),
            1.0 + DT - 2.0 * jnp.sum(scaled, axis=1),
            (DT * (composition - jnp.mean(composition, axis=0))).reshape(-1),
            DT * (latent - jnp.mean(latent)),
            (composition - composition[3]).reshape(-1),
            DT * diffusivity,
            1.0 - 6.0 * DT * diffusivity,
            melt_table.reshape(-1),
        ]
    )


class Round:
    def __init__(self, turn, place, sizes, table, levels):
        self.ng, self.block, self.rows = sizes
        self.table, self.levels = table, levels
        self.start = place * self.block + SHIFT * (turn + 1) - STEPS
        self.lowest = SHIFT * turn - self.start
        self.top = self.ng * self.block + SHIFT * turn - 1 - self.start

    def fill(self, source, sides, planes, to):
        def store(values, e, at, length):
            for f, value in zip(SENT, values):
                self.levels[0][f, e, at : at + length] = value
            self.levels[0][3, e, at : at + length] = 1.0 - values[0] - values[1] - values[2]

        @pl.loop(0, planes)
        def _(i):
            store([source[f, i] for f in range(len(SENT))], i + to, PAD, self.rows)

        for side, at, first in ((sides[0], PAD - STEPS, sides[2]), (sides[1], PAD + self.rows, sides[2])):

            @pl.loop(0, planes)
            def _(i, side=side, at=at, first=first):
                store([side[f, i + first] for f in range(len(SENT))], i + to, at, STEPS)

    def advance(self, src, e, at):
        table, window = self.table, pl.ds(at, 8)
        up, down = jnp.minimum(e + 1, self.top), jnp.maximum(e - 1, self.lowest)
        total = float(self.ng * self.block)
        theta = ((e + self.start).astype(jnp.float32) - 0.5 * total) / total
        mid = [src[f, e, window] for f in range(6)]
        gsum = [src[f, up, window] + src[f, down, window] for f in range(6)]
        xsum = [src[f, e, pl.ds(at + 1, 8)] + src[f, e, pl.ds(at - 1, 8)] for f in range(6)]
        ysum = [pltpu.roll(v, 1, 1) + pltpu.roll(v, v.shape[1] - 1, 1) for v in mid]
        spread = [
            table[GRAD + 3 * a] * gsum[a]
            + table[GRAD + 3 * a + 1] * xsum[a]
            + table[GRAD + 3 * a + 2] * ysum[a]
            + table[CENTER + a] * mid[a]
            for a in range(4)
        ]
        mean = 0.25 * (spread[0] + spread[1] + spread[2] + spread[3]) - 0.25
        trial = [
            spread[a]
            - mean
            - table[COUPLE + 2 * a] * mid[4]
            - table[COUPLE + 2 * a + 1] * mid[5]
            - table[LATENT + a] * theta
            for a in range(3)
        ]
        trial.append(1.0 - trial[0] - trial[1] - trial[2])
        clipped = [jnp.clip(t, 0.0, 1.0) for t in trial]
        inverse = 1.0 / (clipped[0] + clipped[1] + clipped[2] + clipped[3])
        new = [c * inverse for c in clipped]
        change = [n - v for n, v in zip(new[:3], mid[:3])]
        for k in range(2):
            release = table[RELEASE + k] * change[0]
            for a in range(1, 3):
                release = release + table[RELEASE + 2 * a + k] * change[a]
            sides = gsum[4 + k] + xsum[4 + k] + ysum[4 + k]
            new.append(table[SPREAD + k] * sides + table[STAY + k] * mid[4 + k] - release)
        return new

    def sweep(self, step, first, stop, write=None):
        src, dst = self.levels[step - 1], self.levels[step % STEPS]
        if write is None:
            tiles = [PAD - STEPS + 8 * t for t in range(self.rows // 8 + 1)]

            def write(e, at, new):
                for f in range(6):
                    dst[f, e, pl.ds(at, 8)] = new[f]

        else:
            tiles = [PAD + 8 * t for t in range(self.rows // 8)]

        @pl.loop(0, (stop - first) // PLANES)
        def _(i):
            for p in range(PLANES):
                e = first + PLANES * i + p
                for at in tiles:
                    write(e, at, self.advance(src, e, at))


def first_kernel(turn, place_of, sizes, table, own, left, right, early, seam, even, odd):
    run = Round(turn, place_of(), sizes, table, (even, odd, even, odd))
    kept = own.shape[1]
    run.fill(own, (left, right, 0), kept, 0)
    fields = range(6) if early.shape[0] == 6 else SENT

    def write(e, at, new):
        for i, f in enumerate(fields):
            early[i, e - STEPS, pl.ds(at - PAD, 8)] = new[f]

    for step in range(1, STEPS):
        run.sweep(step, step, kept - step)
        for plane in range(2):
            for f in range(6):
                seam[step - 1, f, plane] = run.levels[step][f, kept - step - 2 + plane]
    run.sweep(STEPS, STEPS, kept - STEPS, write)


def second_kernel(
    turn, place_of, sizes, last, table, own, left, right, seam, early, low, high, left2, right2, index, *rest
):
    outs, (even, odd) = rest[:-2], rest[-2:]
    place = place_of()
    run = Round(turn, place, sizes, table, (even, odd, even, odd))
    kept, lows, highs = own.shape[1], low.shape[1], high.shape[1]
    height = kept + lows + highs
    run.fill(own.at[:, pl.ds(kept - 2, 2)], (left, right, kept - 2), 2, kept - 2)
    run.fill(low, (left2, right2, 0), lows, kept)
    run.fill(high, (left2, right2, lows), highs, kept + lows)
    for step in range(1, STEPS):
        for plane in range(2):
            for f in range(6):
                run.levels[step][f, kept - step - 2 + plane] = seam[step - 1, f, plane]
    ready = early.shape[1]

    def write(climbs):
        def put(e, at, new):
            o, here = e - STEPS, pl.ds(at - PAD, 8)
            if last:
                for a in range(4):
                    outs[0][a, o, here] = new[a]
                for k in range(2):
                    outs[1][k, o, here] = new[4 + k]
                return
            for i, f in enumerate(SENT):
                outs[0][i, o - ready, here] = new[f]
                if climbs:
                    outs[1][i, o - ready, here] = new[f]

        return put

    if last:
        for a in range(4):
            outs[0][a, :ready] = early[a]
        for k in range(2):
            outs[1][k, :ready] = early[4 + k]
    for step in range(1, STEPS):
        run.sweep(step, kept - step, height - step)
    climbed = run.block if last else ready + outs[1].shape[1]
    run.sweep(STEPS, kept - STEPS, climbed + STEPS, write(True))
    if not last:
        run.sweep(STEPS, climbed + STEPS, height - STEPS, write(False))

    fresh = run.block - SHIFT

    @pl.when(place == run.ng - 1)
    def _():
        for j in range(SHIFT):
            put = write(fresh + j < climbed)
            for t in range(run.rows // 8):
                row = index[j, pl.ds(8 * t, 8)]
                mu = [jnp.zeros(row.shape, jnp.float32)] * 2
                for m in range((table.shape[0] - MELT) // 2):
                    mu = [jnp.where(row == m, table[MELT + 2 * m + k], mu[k]) for k in range(2)]
                none = jnp.zeros(row.shape, jnp.float32)
                put(fresh + j + STEPS, PAD + 8 * t, [none, none, none, none + 1.0] + mu)


def prepare_kernel(labels, roughness, potential, staying, low, high):
    lows, highs = low.shape[1], high.shape[1]

    def plane(o, kept):
        kind = labels[o]
        rough = [roughness[a, o] for a in range(4)]
        inverse = 1.0 / (3.0 + rough[0] + rough[1] + rough[2] + rough[3])
        new = [(jnp.where(kind == a, 3.0, 0.0) + rough[a]) * inverse for a in range(3)]
        new += [potential[0, o], potential[1, o]]
        for ref, at in kept:
            for f, value in enumerate(new):
                ref[f, at] = value

    @pl.loop(0, lows)
    def _(o):
        plane(o, [(low, o)])

    @pl.loop(lows, lows + highs)
    def _(o):
        plane(o, [(high, o - lows), (staying, o - lows)])

    @pl.loop(lows + highs, labels.shape[0])
    def _(o):
        plane(o, [(staying, o - lows)])


def on_device(ng, nl, labels, roughness, potential, grad_coef, composition, latent, diffusivity, melt_table, melt_index):
    block, rows, lanes = labels.shape
    vmem = pl.BlockSpec(memory_space=pltpu.VMEM)
    smem = pl.BlockSpec(memory_space=pltpu.SMEM)
    f32 = jnp.float32
    kept = block - SHIFT + STEPS
    lows = block - kept
    highs = SHIFT + STEPS - lows
    height = kept + lows + highs
    table = scalar_table(grad_coef, composition, latent, diffusivity, melt_table)

    def home(g, l):
        return g * nl + l

    def away(g, l):
        return (g // 2 * 2 + (l % 2 ^ (l // 2 % 2))) * nl + l // 2 * 2 + g % 2

    def home_place():
        return lax.axis_index("grow")

    def away_place():
        return lax.axis_index("grow") // 2 * 2 + lax.axis_index("lat") % 2

    blocks = [(g, l) for g in range(ng) for l in range(nl)]

    def moved(array, before, after, climb):
        route = [(before(g + climb, l), after(g, l)) for g, l in blocks if g + climb < ng]
        return lax.ppermute(array, AXES, route)

    def beside(parts, where):
        first = jnp.concatenate([p[:, :, :STEPS] for p in parts], axis=1)
        final = jnp.concatenate([p[:, :, rows - STEPS :] for p in parts], axis=1)
        left = lax.ppermute(final, AXES, [(where(g, l), where(g, (l + 1) % nl)) for g, l in blocks])
        right = lax.ppermute(first, AXES, [(where(g, (l + 1) % nl), where(g, l)) for g, l in blocks])
        return left, right

    def piece(planes, fields=len(SENT)):
        return jax.ShapeDtypeStruct((fields, planes, rows, lanes), f32)

    def cost(planes, moved_bytes):
        return pl.CostEstimate(flops=130 * 6 * planes * rows * lanes, bytes_accessed=moved_bytes, transcendentals=0)

    staying, low, high = pl.pallas_call(
        prepare_kernel,
        out_shape=[piece(n) for n in (kept, lows, highs)],
        in_specs=[vmem] * 3,
        out_specs=[vmem] * 3,
        name="prepare",
    )(labels, roughness, potential)

    away_index = lax.ppermute(
        melt_index[: ROUNDS - 1],
        AXES,
        [(home(ng - 1, l), away(ng - 1, l)) for l in range(nl)],
    )

    scratch = [pltpu.VMEM((6, height, rows + 2 * PAD, lanes), f32)] * 2
    params = pltpu.CompilerParams(vmem_limit_bytes=40 << 20)
    for turn in range(ROUNDS):
        last = turn == ROUNDS - 1
        before = home if turn == 0 else away
        after = home if last else away
        place_of = home_place if last else away_place
        own = staying if before is after else moved(staying, before, after, 0)
        low, high = moved(low, before, after, 1), moved(high, before, after, 1)
        left, right = beside([own], after)
        early, seam = pl.pallas_call(
            functools.partial(first_kernel, turn, place_of, (ng, block, rows)),
            out_shape=[piece(lows, 6 if last else len(SENT)), jax.ShapeDtypeStruct((STEPS - 1, 6, 2, rows + 2 * PAD, lanes), f32)],
            in_specs=[smem] + [vmem] * 3,
            out_specs=[vmem] * 2,
            scratch_shapes=scratch,
            compiler_params=params,
            cost_estimate=cost(28, 3000000),
            name="first",
        )(table, own, left, right)
        left2, right2 = beside([low, high], after)
        if last:
            shapes = [jax.ShapeDtypeStruct((n, block, rows, lanes), f32) for n in (4, 2)]
        else:
            shapes = [piece(kept), piece(highs)]
        outs = pl.pallas_call(
            functools.partial(second_kernel, turn, place_of, (ng, block, rows), last),
            out_shape=shapes,
            in_specs=[smem] + [vmem] * 10,
            out_specs=[vmem] * 2,
            scratch_shapes=scratch,
            compiler_params=params,
            cost_estimate=cost(48, 6000000),
            name="second",
        )(table, own, left, right, seam, early, low, high, left2, right2, melt_index[turn] if last else away_index[turn])
        staying, high = outs
        low = early
    return outs[0], outs[1]


def solution(mesh):
    ng, nl = mesh.shape["grow"], mesh.shape["lat"]
    placed = (
        P("grow", "lat", None),
        P(None, "grow", "lat", None),
        P(None, "grow", "lat", None),
        P(),
        P(),
        P(),
        P(),
        P(),
        P(None, None, "lat", None),
    )
    return jax.shard_map(
        functools.partial(on_device, ng, nl),
        mesh=mesh,
        in_specs=placed,
        out_specs=(P(None, "grow", "lat", None), P(None, "grow", "lat", None)),
        check_vma=False,
    )
```

time: 163 us -> 147 us (0.902)
  waiting for transfers between devices: 91.6 us -> 58 us
  starting transfers between devices: 22.3 us -> 36.8 us
  Pallas kernels: 42.6 us -> 44.6 us
    ppermute x6 -> x10, waiting for transfers between devices: 68.1 us -> 48.9 us  [moved(): return lax.ppermute(array, AXES, route)]
    ppermute x8 -> x16, waiting for transfers between devices: 23.5 us -> 9.1 us  [the longest x8 7.16 us: beside(): lax.ppermute(final, AXES, [(where(g, l), where(g, (l + 1) % nl)) for g, l...]
    ppermute x6 -> x10, starting transfers between devices: 14.8 us -> 23.5 us  [moved(): return lax.ppermute(array, AXES, route)]
    ppermute x8 -> x16, starting transfers between devices: 6.86 us -> 12.7 us  [the longest x8 7.8 us: beside(): lax.ppermute(first, AXES, [(where(g, (l + 1) % nl), where(g, l)) for g, l...]
    pallas_call x5 -> x9, Pallas kernels: 42.6 us -> 44.6 us  [the longest x4 25.7 us: on_device(): pl.pallas_call(functools.partial(second_kernel, turn, place_of, (ng, bloc...]
    unnamed x13, local copies, waits for them, and re-layouts: 0.11 us -> 1.93 us
  transfers between devices with their start and end apart: 15 -> 27, of which waited for: 13 -> 9; matrix products, arithmetic and copies ran while one was open for 3% -> 2% of each run, Pallas kernels for 0% -> 15%
where the time goes in v3:
time: 147 us; the launch traced here: 146 us
  waiting for transfers between devices  58 us (39%)
  Pallas kernels  44.6 us (30%)
  starting transfers between devices  36.8 us (25%)
  local copies, waits for them, and re-layouts  3.15 us (2%)
  between operations  1.8 us (1%)
    ppermute x10, waiting for transfers between devices, moved(): return lax.ppermute(array, AXES, route)  48.9 us
    pallas_call x4, Pallas kernels, on_device(): pl.pallas_call(functools.partial(second_kernel, turn, place_of, (ng, bloc...  25.7 us
    ppermute x10, starting transfers between devices, moved(): return lax.ppermute(array, AXES, route)  23.5 us
    pallas_call x4, Pallas kernels, on_device(): pl.pallas_call(functools.partial(first_kernel, turn, place_of, (ng, block...  15.9 us
    ppermute x8, starting transfers between devices, beside(): lax.ppermute(first, AXES, [(where(g, (l + 1) % nl), where(g, l)) for g, l...  7.8 us
    ppermute x8, waiting for transfers between devices, beside(): lax.ppermute(final, AXES, [(where(g, l), where(g, (l + 1) % nl)) for g, l...  7.16 us
    ppermute x8, starting transfers between devices, beside(): lax.ppermute(final, AXES, [(where(g, l), where(g, (l + 1) % nl)) for g, l...  4.88 us
    pallas_call x1, Pallas kernels, on_device(): pl.pallas_call(prepare_kernel, out_shape=[piece(n) for n in (kept, lows,...  3.02 us
  transfers between devices with their start and end apart: 27, of which 9 were waited for; matrix products, arithmetic and copies ran while one was open for 2% of the time, Pallas kernels for 15%

profile of v3, /device:TPU:17, one launch (start us, length us, event | category | flops | bytes accessed | tf_op | source)
XLA Modules:
  0.0 145.6 jit_solution(14510466009963619277)
XLA Ops:
  0.6 3.0 %prepare.1 = (f32[5,12,32,128]{3,2,1,0:T(8,128)}, f32[5,4,32,128]{3,2,1,0:T(8,128)}, f32[5,8,32,128]{3,2,1,0:T(8,128)}) custom-call(s32[16,32,128]{2,1,0:T(8,128)} %labels.1, f32[4,16,32,128]{3,2,1,0:T(8,128)} %roughness.1, f32[2,16,32,128]{3,2,1,0:T(8,128)} %potential.1), custom_call_target="tpu_custom_call" | custom-call | tf_op jit(solution)/shard_map/prepare/pallas_call | solution.py:265
  3.7 3.7 %collective-permute-start = (f32[5,12,32,128]{3,2,1,0:T(8,128)}, f32[5,12,32,128]{3,2,1,0:T(8,128)S(1)}, u32[]{:S(2)}, u32[]{:S(2)}) collective-permute-start(f32[5,12,32,128]{3,2,1,0:T(8,128)} %get-tuple-element.19), channel_id=1, source_target_pairs={{0,0},{1,4},{2,6},{3,2},{4,1},{5,5},{6,7},{7,3},{8,8},{9,12},{10,1... | collective-permute-start | bytes 2949128 | tf_op jit(solution)/shard_map/ppermute | solution.py:250
  7.4 1.9 %collective-permute-start.4 = (f32[5,8,32,128]{3,2,1,0:T(8,128)}, f32[5,8,32,128]{3,2,1,0:T(8,128)S(1)}, u32[]{:S(2)}, u32[]{:S(2)}) collective-permute-start(f32[5,8,32,128]{3,2,1,0:T(8,128)} %get-tuple-element.23), channel_id=1, source_target_pairs={{4,0},{5,4},{6,6},{7,2},{8,1},{9,5},{10,7},{11,3},{12,8},{13,12},{... | collective-permute-start | bytes 1966088 | tf_op jit(solution)/shard_map/ppermute | solution.py:250
  9.3 1.9 %collective-permute-start.3 = (f32[5,4,32,128]{3,2,1,0:T(8,128)}, f32[5,4,32,128]{3,2,1,0:T(8,128)S(1)}, u32[]{:S(2)}, u32[]{:S(2)}) collective-permute-start(f32[5,4,32,128]{3,2,1,0:T(8,128)} %get-tuple-element.22), channel_id=1, source_target_pairs={{4,0},{5,4},{6,6},{7,2},{8,1},{9,5},{10,7},{11,3},{12,8},{13,12},{... | collective-permute-start | bytes 983048 | tf_op jit(solution)/shard_map/ppermute | solution.py:250
  16.4 15.8 %collective-permute-done.3.low = f32[5,4,32,128]{3,2,1,0:T(8,128)S(1)} collective-permute-done((f32[5,4,32,128]{3,2,1,0:T(8,128)}, f32[5,4,32,128]{3,2,1,0:T(8,128)S(1)}, u32[]{:S(2)}, u32[]{:S(2)}) %collective-permute-start.3) | collective-permute-done | bytes 327712 | tf_op jit(solution)/shard_map/ppermute | solution.py:250
  32.4 1.5 %collective-permute-start.6 = (f32[5,12,4,128]{3,2,1,0:T(4,128)S(1)}, f32[5,12,4,128]{3,2,1,0:T(4,128)S(1)}, u32[]{:S(2)}, u32[]{:S(2)}) collective-permute-start(f32[5,12,4,128]{3,2,1,0:T(4,128)S(1)} %pad_maximum_fusion.1), channel_id=1, source_target_pairs={{4,0},{6,4},{2,6},{0,2},{5,1},{7,5},{3,7},{1,3},{12,8},{14,12},{10... | collective-permute-start | bytes 368648 | tf_op jit(solution)/shard_map/ppermute | solution.py:256
  35.5 4.4 %collective-permute-done.1.left = f32[5,12,4,128]{3,2,1,0:T(4,128)S(1)} collective-permute-done((f32[5,12,4,128]{3,2,1,0:T(4,128)S(1)}, f32[5,12,4,128]{3,2,1,0:T(4,128)S(1)}, u32[]{:S(2)}, u32[]{:S(2)}) %collective-permute-start.1) | collective-permute-done | bytes 122912 | tf_op jit(solution)/shard_map/ppermute | solution.py:255
  40.0 4.0 %first.4 = (f32[5,4,32,128]{3,2,1,0:T(8,128)S(1)}, f32[3,6,2,48,128]{4,3,2,1,0:T(8,128)S(1)}) custom-call(f32[72]{0:T(128)S(1)} %concatenate.27.table, f32[5,12,32,128]{3,2,1,0:T(8,128)S(1)} %collective-permute-done.own, f32[5,12,4,128]{3,2,1,0:T(4,128)S(1)} %collective-permute-done.1.left, f32[5,12,4,128]{3,2,1,0:T(4,128)S(1)} %collective-permute-done.2.right), custom_call_target="tpu_custom_call" | custom-call | flops 89456640 | bytes 3000000 | tf_op jit(solution)/shard_map/first/pallas_call | solution.py:289
  44.0 6.1 %second.4 = (f32[5,12,32,128]{3,2,1,0:T(8,128)S(1)}, f32[5,8,32,128]{3,2,1,0:T(8,128)S(1)}) custom-call(f32[72]{0:T(128)S(1)} %concatenate.27.table, f32[5,12,32,128]{3,2,1,0:T(8,128)S(1)} %collective-permute-done.own, f32[5,12,4,128]{3,2,1,0:T(4,128)S(1)} %collective-permute-done.1.left, f32[5,12,4,128]{3,2,1,0:T(4,128)S(1)} %collective-permute-done.2.right, ...), custom_call_target="tpu_custom_call" | custom-call | flops 153354240 | bytes 6000000 | tf_op jit(solution)/shard_map/second/pallas_call | solution.py:304
  50.1 2.3 %collective-permute-start.11 = (f32[5,8,32,128]{3,2,1,0:T(8,128)S(1)}, f32[5,8,32,128]{3,2,1,0:T(8,128)S(1)}, u32[]{:S(2)}, u32[]{:S(2)}) collective-permute-start(f32[5,8,32,128]{3,2,1,0:T(8,128)S(1)} %get-tuple-element.27), channel_id=1, source_target_pairs={{1,0},{5,4},{7,6},{3,2},{8,1},{12,5},{14,7},{10,3},{9,8},{13,12},{... | collective-permute-start | bytes 1966088 | tf_op jit(solution)/shard_map/ppermute | solution.py:250
  52.4 2.1 %collective-permute-start.10 = (f32[5,4,32,128]{3,2,1,0:T(8,128)S(1)}, f32[5,4,32,128]{3,2,1,0:T(8,128)S(1)}, u32[]{:S(2)}, u32[]{:S(2)}) collective-permute-start(f32[5,4,32,128]{3,2,1,0:T(8,128)S(1)} %get-tuple-element.21.early), channel_id=1, source_target_pairs={{1,0},{5,4},{7,6},{3,2},{8,1},{12,5},{14,7},{10,3},{9,8},{13,12},{... | collective-permute-start | bytes 983048 | tf_op jit(solution)/shard_map/ppermute | solution.py:250
  55.5 1.0 collective-permute-start.9
  56.5 9.1 %collective-permute-done.10.low = f32[5,4,32,128]{3,2,1,0:T(8,128)S(1)} collective-permute-done((f32[5,4,32,128]{3,2,1,0:T(8,128)S(1)}, f32[5,4,32,128]{3,2,1,0:T(8,128)S(1)}, u32[]{:S(2)}, u32[]{:S(2)}) %collective-permute-start.10) | collective-permute-done | bytes 327712 | tf_op jit(solution)/shard_map/ppermute | solution.py:250
  65.6 1.9 %collective-permute-start.13 = (f32[5,12,4,128]{3,2,1,0:T(4,128)S(1)}, f32[5,12,4,128]{3,2,1,0:T(4,128)S(1)}, u32[]{:S(2)}, u32[]{:S(2)}) collective-permute-start(f32[5,12,4,128]{3,2,1,0:T(4,128)S(1)} %pad_maximum_fusion.3), channel_id=1, source_target_pairs={{4,0},{6,4},{2,6},{0,2},{5,1},{7,5},{3,7},{1,3},{12,8},{14,12},{10... | collective-permute-start | bytes 368648 | tf_op jit(solution)/shard_map/ppermute | solution.py:256
  67.7 4.0 %first.5 = (f32[5,4,32,128]{3,2,1,0:T(8,128)S(1)}, f32[3,6,2,48,128]{4,3,2,1,0:T(8,128)S(1)}) custom-call(f32[72]{0:T(128)S(1)} %concatenate.27.table, f32[5,12,32,128]{3,2,1,0:T(8,128)S(1)} %get-tuple-element.24.own, f32[5,12,4,128]{3,2,1,0:T(4,128)S(1)} %collective-permute-done.8.left, f32[5,12,4,128]{3,2,1,0:T(4,128)S(1)} %collective-permute-done.9.right), custom_call_target="tpu_custom_call" | custom-call | flops 89456640 | bytes 3000000 | tf_op jit(solution)/shard_map/first/pallas_call | solution.py:289
  71.6 1.9 %collective-permute-start.16 = (f32[5,4,32,128]{3,2,1,0:T(8,128)S(1)}, f32[5,4,32,128]{3,2,1,0:T(8,128)S(1)}, u32[]{:S(2)}, u32[]{:S(2)}) collective-permute-start(f32[5,4,32,128]{3,2,1,0:T(8,128)S(1)} %get-tuple-element.26.early), channel_id=1, source_target_pairs={{1,0},{5,4},{7,6},{3,2},{8,1},{12,5},{14,7},{10,3},{9,8},{13,12},{... | collective-permute-start | bytes 983048 | tf_op jit(solution)/shard_map/ppermute | solution.py:250
  73.6 6.1 %second.5 = (f32[5,12,32,128]{3,2,1,0:T(8,128)S(1)}, f32[5,8,32,128]{3,2,1,0:T(8,128)S(1)}) custom-call(f32[72]{0:T(128)S(1)} %concatenate.27.table, f32[5,12,32,128]{3,2,1,0:T(8,128)S(1)} %get-tuple-element.24.own, f32[5,12,4,128]{3,2,1,0:T(4,128)S(1)} %collective-permute-done.8.left, f32[5,12,4,128]{3,2,1,0:T(4,128)S(1)} %collective-permute-done.9.right, ...), custom_call_target="tpu_custom_call" | custom-call | flops 153354240 | bytes 6000000 | tf_op jit(solution)/shard_map/second/pallas_call | solution.py:304
  79.7 2.4 %collective-permute-start.17 = (f32[5,8,32,128]{3,2,1,0:T(8,128)S(1)}, f32[5,8,32,128]{3,2,1,0:T(8,128)S(1)}, u32[]{:S(2)}, u32[]{:S(2)}) collective-permute-start(f32[5,8,32,128]{3,2,1,0:T(8,128)S(1)} %get-tuple-element.31), channel_id=1, source_target_pairs={{1,0},{5,4},{7,6},{3,2},{8,1},{12,5},{14,7},{10,3},{9,8},{13,12},{... | collective-permute-start | bytes 1966088 | tf_op jit(solution)/shard_map/ppermute | solution.py:250
  83.8 7.9 %collective-permute-done.17.high = f32[5,8,32,128]{3,2,1,0:T(8,128)S(1)} collective-permute-done((f32[5,8,32,128]{3,2,1,0:T(8,128)S(1)}, f32[5,8,32,128]{3,2,1,0:T(8,128)S(1)}, u32[]{:S(2)}, u32[]{:S(2)}) %collective-permute-start.17) | collective-permute-done | bytes 655392 | tf_op jit(solution)/shard_map/ppermute | solution.py:250
  91.7 1.5 %collective-permute-start.19 = (f32[5,12,4,128]{3,2,1,0:T(4,128)S(1)}, f32[5,12,4,128]{3,2,1,0:T(4,128)S(1)}, u32[]{:S(2)}, u32[]{:S(2)}) collective-permute-start(f32[5,12,4,128]{3,2,1,0:T(4,128)S(1)} %pad_maximum_fusion.5), channel_id=1, source_target_pairs={{4,0},{6,4},{2,6},{0,2},{5,1},{7,5},{3,7},{1,3},{12,8},{14,12},{10... | collective-permute-start | bytes 368648 | tf_op jit(solution)/shard_map/ppermute | solution.py:256
  93.3 4.0 %first.6 = (f32[5,4,32,128]{3,2,1,0:T(8,128)S(1)}, f32[3,6,2,48,128]{4,3,2,1,0:T(8,128)S(1)}) custom-call(f32[72]{0:T(128)S(1)} %concatenate.27.table, f32[5,12,32,128]{3,2,1,0:T(8,128)S(1)} %get-tuple-element.28.own, f32[5,12,4,128]{3,2,1,0:T(4,128)S(1)} %collective-permute-done.14.left, f32[5,12,4,128]{3,2,1,0:T(4,128)S(1)} %collective-permute-done.15.right), custom_call_target="tpu_custom_call" | custom-call | flops 89456640 | bytes 3000000 | tf_op jit(solution)/shard_map/first/pallas_call | solution.py:289
  97.7 6.1 %second.6 = (f32[5,12,32,128]{3,2,1,0:T(8,128)S(1)}, f32[5,8,32,128]{3,2,1,0:T(8,128)S(1)}) custom-call(f32[72]{0:T(128)S(1)} %concatenate.27.table, f32[5,12,32,128]{3,2,1,0:T(8,128)S(1)} %get-tuple-element.28.own, f32[5,12,4,128]{3,2,1,0:T(4,128)S(1)} %collective-permute-done.14.left, f32[5,12,4,128]{3,2,1,0:T(4,128)S(1)} %collective-permute-done.15.right, ...), custom_call_target="tpu_custom_call" | custom-call | flops 153354240 | bytes 6000000 | tf_op jit(solution)/shard_map/second/pallas_call | solution.py:304
  103.8 1.9 %collective-permute-start.24 = (f32[5,8,32,128]{3,2,1,0:T(8,128)S(1)}, f32[5,8,32,128]{3,2,1,0:T(8,128)S(1)}, u32[]{:S(2)}, u32[]{:S(2)}) collective-permute-start(f32[5,8,32,128]{3,2,1,0:T(8,128)S(1)} %get-tuple-element.35), channel_id=1, source_target_pairs={{1,0},{5,1},{7,2},{3,3},{8,4},{12,5},{14,6},{10,7},{9,8},{13,9},{1... | collective-permute-start | bytes 1966088 | tf_op jit(solution)/shard_map/ppermute | solution.py:250
  105.8 1.9 %collective-permute-start.23 = (f32[5,4,32,128]{3,2,1,0:T(8,128)S(1)}, f32[5,4,32,128]{3,2,1,0:T(8,128)S(1)}, u32[]{:S(2)}, u32[]{:S(2)}) collective-permute-start(f32[5,4,32,128]{3,2,1,0:T(8,128)S(1)} %get-tuple-element.30.early), channel_id=1, source_target_pairs={{1,0},{5,1},{7,2},{3,3},{8,4},{12,5},{14,6},{10,7},{9,8},{13,9},{1... | collective-permute-start | bytes 983048 | tf_op jit(solution)/shard_map/ppermute | solution.py:250
  107.7 3.4 %collective-permute-start.20 = (f32[5,12,32,128]{3,2,1,0:T(8,128)S(1)}, f32[5,12,32,128]{3,2,1,0:T(8,128)S(1)}, u32[]{:S(2)}, u32[]{:S(2)}) collective-permute-start(f32[5,12,32,128]{3,2,1,0:T(8,128)S(1)} %get-tuple-element.32), channel_id=1, source_target_pairs={{0,0},{4,1},{6,2},{2,3},{1,4},{5,5},{7,6},{3,7},{8,8},{12,9},{14,1... | collective-permute-start | bytes 2949128 | tf_op jit(solution)/shard_map/ppermute | solution.py:250
  111.1 13.7 %collective-permute-done.23.low = f32[5,4,32,128]{3,2,1,0:T(8,128)S(1)} collective-permute-done((f32[5,4,32,128]{3,2,1,0:T(8,128)S(1)}, f32[5,4,32,128]{3,2,1,0:T(8,128)S(1)}, u32[]{:S(2)}, u32[]{:S(2)}) %collective-permute-start.23) | collective-permute-done | bytes 327712 | tf_op jit(solution)/shard_map/ppermute | solution.py:250
  125.0 1.8 %collective-permute-start.25 = (f32[5,12,4,128]{3,2,1,0:T(4,128)S(1)}, f32[5,12,4,128]{3,2,1,0:T(4,128)S(1)}, u32[]{:S(2)}, u32[]{:S(2)}) collective-permute-start(f32[5,12,4,128]{3,2,1,0:T(4,128)S(1)} %pad_maximum_fusion.6), channel_id=1, source_target_pairs={{0,1},{1,2},{2,3},{3,0},{4,5},{5,6},{6,7},{7,4},{8,9},{9,10},{10,1... | collective-permute-start | bytes 368648 | tf_op jit(solution)/shard_map/ppermute | solution.py:255
  126.8 2.4 %collective-permute-done.20.own = f32[5,12,32,128]{3,2,1,0:T(8,128)S(1)} collective-permute-done((f32[5,12,32,128]{3,2,1,0:T(8,128)S(1)}, f32[5,12,32,128]{3,2,1,0:T(8,128)S(1)}, u32[]{:S(2)}, u32[]{:S(2)}) %collective-permute-start.20) | collective-permute-done | bytes 983072 | tf_op jit(solution)/shard_map/ppermute | solution.py:250
  130.1 2.4 %collective-permute-done.21.left = f32[5,12,4,128]{3,2,1,0:T(4,128)S(1)} collective-permute-done((f32[5,12,4,128]{3,2,1,0:T(4,128)S(1)}, f32[5,12,4,128]{3,2,1,0:T(4,128)S(1)}, u32[]{:S(2)}, u32[]{:S(2)}) %collective-permute-start.21) | collective-permute-done | bytes 122912 | tf_op jit(solution)/shard_map/ppermute | solution.py:255
  132.4 1.9 %collective-permute-done.22.right = f32[5,12,4,128]{3,2,1,0:T(4,128)S(1)} collective-permute-done((f32[5,12,4,128]{3,2,1,0:T(4,128)S(1)}, f32[5,12,4,128]{3,2,1,0:T(4,128)S(1)}, u32[]{:S(2)}, u32[]{:S(2)}) %collective-permute-start.22) | collective-permute-done | bytes 122912 | tf_op jit(solution)/shard_map/ppermute | solution.py:256
  134.3 4.0 %first.7 = (f32[6,4,32,128]{3,2,1,0:T(8,128)S(1)}, f32[3,6,2,48,128]{4,3,2,1,0:T(8,128)S(1)}) custom-call(f32[72]{0:T(128)S(1)} %concatenate.27.table, f32[5,12,32,128]{3,2,1,0:T(8,128)S(1)} %collective-permute-done.20.own, f32[5,12,4,128]{3,2,1,0:T(4,128)S(1)} %collective-permute-done.21.left, f32[5,12,4,128]{3,2,1,0:T(4,128)S(1)} %collective-permute-done.22.right), custom_call_target="tpu_custom_call" | custom-call | flops 89456640 | bytes 3000000 | tf_op jit(solution)/shard_map/first/pallas_call | solution.py:289
  138.3 7.3 %second.7 = (f32[4,16,32,128]{3,2,1,0:T(8,128)}, f32[2,16,32,128]{3,2,1,0:T(8,128)}) custom-call(f32[72]{0:T(128)S(1)} %concatenate.27.table, f32[5,12,32,128]{3,2,1,0:T(8,128)S(1)} %collective-permute-done.20.own, f32[5,12,4,128]{3,2,1,0:T(4,128)S(1)} %collective-permute-done.21.left, f32[5,12,4,128]{3,2,1,0:T(4,128)S(1)} %collective-permute-done.22.right, ...), custom_call_target="tpu_custom_call" | custom-call | flops 153354240 | bytes 6000000 | tf_op jit(solution)/shard_map/second/pallas_call | solution.py:304
  (82 shorter events, 10.5 us)
Async XLA Ops:
  0.6 10.6 %copy-start = (s32[4,8,32,128]{3,2,1,0:T(8,128)S(1)}, s32[4,8,32,128]{3,2,1,0:T(8,128)}, u32[]{:S(2)}) copy-start(s32[4,8,32,128]{3,2,1,0:T(8,128)} %param.17) | copy-start | bytes 1572868
  3.7 30.3 %collective-permute-start = (f32[5,12,32,128]{3,2,1,0:T(8,128)}, f32[5,12,32,128]{3,2,1,0:T(8,128)S(1)}, u32[]{:S(2)}, u32[]{:S(2)}) collective-permute-start(f32[5,12,32,128]{3,2,1,0:T(8,128)} %get-tuple-element.19), channel_id=1, source_target_pairs={{0,0},{1,4},{2,6},{3,2},{4,1},{5,5},{6,7},{7,3},{8,8},{9,12},{10,1... | collective-permute-start | bytes 2949128 | tf_op jit(solution)/shard_map/ppermute | solution.py:250
  7.4 24.9 %collective-permute-start.4 = (f32[5,8,32,128]{3,2,1,0:T(8,128)}, f32[5,8,32,128]{3,2,1,0:T(8,128)S(1)}, u32[]{:S(2)}, u32[]{:S(2)}) collective-permute-start(f32[5,8,32,128]{3,2,1,0:T(8,128)} %get-tuple-element.23), channel_id=1, source_target_pairs={{4,0},{5,4},{6,6},{7,2},{8,1},{9,5},{10,7},{11,3},{12,8},{13,12},{... | collective-permute-start | bytes 1966088 | tf_op jit(solution)/shard_map/ppermute | solution.py:250
  9.3 2.7 %copy-start.2 = (f32[4,3]{1,0:T(4,128)S(1)}, f32[4,3]{1,0:T(4,128)}, u32[]{:S(2)}) copy-start(f32[4,3]{1,0:T(4,128)} %param.12) | copy-start | bytes 148
  9.3 22.9 %collective-permute-start.3 = (f32[5,4,32,128]{3,2,1,0:T(8,128)}, f32[5,4,32,128]{3,2,1,0:T(8,128)S(1)}, u32[]{:S(2)}, u32[]{:S(2)}) collective-permute-start(f32[5,4,32,128]{3,2,1,0:T(8,128)} %get-tuple-element.22), channel_id=1, source_target_pairs={{4,0},{5,4},{6,6},{7,2},{8,1},{9,5},{10,7},{11,3},{12,8},{13,12},{... | collective-permute-start | bytes 983048 | tf_op jit(solution)/shard_map/ppermute | solution.py:250
  11.3 0.8 copy-start.1
  11.3 24.2 %collective-permute-start.7 = (s32[3,8,32,128]{3,2,1,0:T(8,128)S(1)}, s32[3,8,32,128]{3,2,1,0:T(8,128)S(1)}, u32[]{:S(2)}, u32[]{:S(2)}) collective-permute-start(s32[3,8,32,128]{3,2,1,0:T(8,128)S(1)} %slice.97), channel_id=1, source_target_pairs={{28,25},{29,29},{30,31},{31,27}} | collective-permute-start | bytes 1179656 | tf_op jit(solution)/shard_map/ppermute | solution.py:273
  12.4 0.7 copy-start.5
  14.8 0.7 copy-start.3
  32.3 11.6 %collective-permute-start.5 = (f32[5,12,4,128]{3,2,1,0:T(4,128)S(1)}, f32[5,12,4,128]{3,2,1,0:T(4,128)S(1)}, u32[]{:S(2)}, u32[]{:S(2)}) collective-permute-start(f32[5,12,4,128]{3,2,1,0:T(4,128)S(1)} %pad_maximum_fusion), channel_id=1, source_target_pairs={{0,4},{4,6},{6,2},{2,0},{1,5},{5,7},{7,3},{3,1},{8,12},{12,14},{14... | collective-permute-start | bytes 368648 | tf_op jit(solution)/shard_map/ppermute | solution.py:255
  32.4 11.5 %collective-permute-start.6 = (f32[5,12,4,128]{3,2,1,0:T(4,128)S(1)}, f32[5,12,4,128]{3,2,1,0:T(4,128)S(1)}, u32[]{:S(2)}, u32[]{:S(2)}) collective-permute-start(f32[5,12,4,128]{3,2,1,0:T(4,128)S(1)} %pad_maximum_fusion.1), channel_id=1, source_target_pairs={{4,0},{6,4},{2,6},{0,2},{5,1},{7,5},{3,7},{1,3},{12,8},{14,12},{10... | collective-permute-start | bytes 368648 | tf_op jit(solution)/shard_map/ppermute | solution.py:256
  34.0 6.0 %collective-permute-start.1 = (f32[5,12,4,128]{3,2,1,0:T(4,128)S(1)}, f32[5,12,4,128]{3,2,1,0:T(4,128)S(1)}, u32[]{:S(2)}, u32[]{:S(2)}) collective-permute-start(f32[5,12,4,128]{3,2,1,0:T(4,128)S(1)} %get-tuple-element.43), channel_id=1, source_target_pairs={{0,4},{4,6},{6,2},{2,0},{1,5},{5,7},{7,3},{3,1},{8,12},{12,14},{14... | collective-permute-start | bytes 368648 | tf_op jit(solution)/shard_map/ppermute | solution.py:255
  34.6 5.4 %collective-permute-start.2 = (f32[5,12,4,128]{3,2,1,0:T(4,128)S(1)}, f32[5,12,4,128]{3,2,1,0:T(4,128)S(1)}, u32[]{:S(2)}, u32[]{:S(2)}) collective-permute-start(f32[5,12,4,128]{3,2,1,0:T(4,128)S(1)} %get-tuple-element.42), channel_id=1, source_target_pairs={{4,0},{6,4},{2,6},{0,2},{5,1},{7,5},{3,7},{1,3},{12,8},{14,12},{10... | collective-permute-start | bytes 368648 | tf_op jit(solution)/shard_map/ppermute | solution.py:256
  50.1 15.4 %collective-permute-start.11 = (f32[5,8,32,128]{3,2,1,0:T(8,128)S(1)}, f32[5,8,32,128]{3,2,1,0:T(8,128)S(1)}, u32[]{:S(2)}, u32[]{:S(2)}) collective-permute-start(f32[5,8,32,128]{3,2,1,0:T(8,128)S(1)} %get-tuple-element.27), channel_id=1, source_target_pairs={{1,0},{5,4},{7,6},{3,2},{8,1},{12,5},{14,7},{10,3},{9,8},{13,12},{... | collective-permute-start | bytes 1966088 | tf_op jit(solution)/shard_map/ppermute | solution.py:250
  52.4 13.1 %collective-permute-start.10 = (f32[5,4,32,128]{3,2,1,0:T(8,128)S(1)}, f32[5,4,32,128]{3,2,1,0:T(8,128)S(1)}, u32[]{:S(2)}, u32[]{:S(2)}) collective-permute-start(f32[5,4,32,128]{3,2,1,0:T(8,128)S(1)} %get-tuple-element.21.early), channel_id=1, source_target_pairs={{1,0},{5,4},{7,6},{3,2},{8,1},{12,5},{14,7},{10,3},{9,8},{13,12},{... | collective-permute-start | bytes 983048 | tf_op jit(solution)/shard_map/ppermute | solution.py:250
  54.6 13.1 %collective-permute-start.8 = (f32[5,12,4,128]{3,2,1,0:T(4,128)S(1)}, f32[5,12,4,128]{3,2,1,0:T(4,128)S(1)}, u32[]{:S(2)}, u32[]{:S(2)}) collective-permute-start(f32[5,12,4,128]{3,2,1,0:T(4,128)S(1)} %get-tuple-element.41), channel_id=1, source_target_pairs={{0,4},{4,6},{6,2},{2,0},{1,5},{5,7},{7,3},{3,1},{8,12},{12,14},{14... | collective-permute-start | bytes 368648 | tf_op jit(solution)/shard_map/ppermute | solution.py:255
  55.5 12.2 %collective-permute-start.9 = (f32[5,12,4,128]{3,2,1,0:T(4,128)S(1)}, f32[5,12,4,128]{3,2,1,0:T(4,128)S(1)}, u32[]{:S(2)}, u32[]{:S(2)}) collective-permute-start(f32[5,12,4,128]{3,2,1,0:T(4,128)S(1)} %get-tuple-element.40), channel_id=1, source_target_pairs={{4,0},{6,4},{2,6},{0,2},{5,1},{7,5},{3,7},{1,3},{12,8},{14,12},{10... | collective-permute-start | bytes 368648 | tf_op jit(solution)/shard_map/ppermute | solution.py:256
  65.6 7.9 %collective-permute-start.13 = (f32[5,12,4,128]{3,2,1,0:T(4,128)S(1)}, f32[5,12,4,128]{3,2,1,0:T(4,128)S(1)}, u32[]{:S(2)}, u32[]{:S(2)}) collective-permute-start(f32[5,12,4,128]{3,2,1,0:T(4,128)S(1)} %pad_maximum_fusion.3), channel_id=1, source_target_pairs={{4,0},{6,4},{2,6},{0,2},{5,1},{7,5},{3,7},{1,3},{12,8},{14,12},{10... | collective-permute-start | bytes 368648 | tf_op jit(solution)/shard_map/ppermute | solution.py:256
  67.6 6.0 %collective-permute-start.12 = (f32[5,12,4,128]{3,2,1,0:T(4,128)S(1)}, f32[5,12,4,128]{3,2,1,0:T(4,128)S(1)}, u32[]{:S(2)}, u32[]{:S(2)}) collective-permute-start(f32[5,12,4,128]{3,2,1,0:T(4,128)S(1)} %pad_maximum_fusion.2), channel_id=1, source_target_pairs={{0,4},{4,6},{6,2},{2,0},{1,5},{5,7},{7,3},{3,1},{8,12},{12,14},{14... | collective-permute-start | bytes 368648 | tf_op jit(solution)/shard_map/ppermute | solution.py:255
  71.6 10.5 %collective-permute-start.16 = (f32[5,4,32,128]{3,2,1,0:T(8,128)S(1)}, f32[5,4,32,128]{3,2,1,0:T(8,128)S(1)}, u32[]{:S(2)}, u32[]{:S(2)}) collective-permute-start(f32[5,4,32,128]{3,2,1,0:T(8,128)S(1)} %get-tuple-element.26.early), channel_id=1, source_target_pairs={{1,0},{5,4},{7,6},{3,2},{8,1},{12,5},{14,7},{10,3},{9,8},{13,12},{... | collective-permute-start | bytes 983048 | tf_op jit(solution)/shard_map/ppermute | solution.py:250
  79.7 11.9 %collective-permute-start.17 = (f32[5,8,32,128]{3,2,1,0:T(8,128)S(1)}, f32[5,8,32,128]{3,2,1,0:T(8,128)S(1)}, u32[]{:S(2)}, u32[]{:S(2)}) collective-permute-start(f32[5,8,32,128]{3,2,1,0:T(8,128)S(1)} %get-tuple-element.31), channel_id=1, source_target_pairs={{1,0},{5,4},{7,6},{3,2},{8,1},{12,5},{14,7},{10,3},{9,8},{13,12},{... | collective-permute-start | bytes 1966088 | tf_op jit(solution)/shard_map/ppermute | solution.py:250
  82.2 11.1 %collective-permute-start.14 = (f32[5,12,4,128]{3,2,1,0:T(4,128)S(1)}, f32[5,12,4,128]{3,2,1,0:T(4,128)S(1)}, u32[]{:S(2)}, u32[]{:S(2)}) collective-permute-start(f32[5,12,4,128]{3,2,1,0:T(4,128)S(1)} %get-tuple-element.39), channel_id=1, source_target_pairs={{0,4},{4,6},{6,2},{2,0},{1,5},{5,7},{7,3},{3,1},{8,12},{12,14},{14... | collective-permute-start | bytes 368648 | tf_op jit(solution)/shard_map/ppermute | solution.py:255
  82.8 10.5 %collective-permute-start.15 = (f32[5,12,4,128]{3,2,1,0:T(4,128)S(1)}, f32[5,12,4,128]{3,2,1,0:T(4,128)S(1)}, u32[]{:S(2)}, u32[]{:S(2)}) collective-permute-start(f32[5,12,4,128]{3,2,1,0:T(4,128)S(1)} %get-tuple-element.38), channel_id=1, source_target_pairs={{4,0},{6,4},{2,6},{0,2},{5,1},{7,5},{3,7},{1,3},{12,8},{14,12},{10... | collective-permute-start | bytes 368648 | tf_op jit(solution)/shard_map/ppermute | solution.py:256
  91.7 5.6 %collective-permute-start.19 = (f32[5,12,4,128]{3,2,1,0:T(4,128)S(1)}, f32[5,12,4,128]{3,2,1,0:T(4,128)S(1)}, u32[]{:S(2)}, u32[]{:S(2)}) collective-permute-start(f32[5,12,4,128]{3,2,1,0:T(4,128)S(1)} %pad_maximum_fusion.5), channel_id=1, source_target_pairs={{4,0},{6,4},{2,6},{0,2},{5,1},{7,5},{3,7},{1,3},{12,8},{14,12},{10... | collective-permute-start | bytes 368648 | tf_op jit(solution)/shard_map/ppermute | solution.py:256
  93.2 4.4 %collective-permute-start.18 = (f32[5,12,4,128]{3,2,1,0:T(4,128)S(1)}, f32[5,12,4,128]{3,2,1,0:T(4,128)S(1)}, u32[]{:S(2)}, u32[]{:S(2)}) collective-permute-start(f32[5,12,4,128]{3,2,1,0:T(4,128)S(1)} %pad_maximum_fusion.4), channel_id=1, source_target_pairs={{0,4},{4,6},{6,2},{2,0},{1,5},{5,7},{7,3},{3,1},{8,12},{12,14},{14... | collective-permute-start | bytes 368648 | tf_op jit(solution)/shard_map/ppermute | solution.py:255
  103.8 21.0 %collective-permute-start.24 = (f32[5,8,32,128]{3,2,1,0:T(8,128)S(1)}, f32[5,8,32,128]{3,2,1,0:T(8,128)S(1)}, u32[]{:S(2)}, u32[]{:S(2)}) collective-permute-start(f32[5,8,32,128]{3,2,1,0:T(8,128)S(1)} %get-tuple-element.35), channel_id=1, source_target_pairs={{1,0},{5,1},{7,2},{3,3},{8,4},{12,5},{14,6},{10,7},{9,8},{13,9},{1... | collective-permute-start | bytes 1966088 | tf_op jit(solution)/shard_map/ppermute | solution.py:250
  105.8 19.0 %collective-permute-start.23 = (f32[5,4,32,128]{3,2,1,0:T(8,128)S(1)}, f32[5,4,32,128]{3,2,1,0:T(8,128)S(1)}, u32[]{:S(2)}, u32[]{:S(2)}) collective-permute-start(f32[5,4,32,128]{3,2,1,0:T(8,128)S(1)} %get-tuple-element.30.early), channel_id=1, source_target_pairs={{1,0},{5,1},{7,2},{3,3},{8,4},{12,5},{14,6},{10,7},{9,8},{13,9},{1... | collective-permute-start | bytes 983048 | tf_op jit(solution)/shard_map/ppermute | solution.py:250
  107.7 21.5 %collective-permute-start.20 = (f32[5,12,32,128]{3,2,1,0:T(8,128)S(1)}, f32[5,12,32,128]{3,2,1,0:T(8,128)S(1)}, u32[]{:S(2)}, u32[]{:S(2)}) collective-permute-start(f32[5,12,32,128]{3,2,1,0:T(8,128)S(1)} %get-tuple-element.32), channel_id=1, source_target_pairs={{0,0},{4,1},{6,2},{2,3},{1,4},{5,5},{7,6},{3,7},{8,8},{12,9},{14,1... | collective-permute-start | bytes 2949128 | tf_op jit(solution)/shard_map/ppermute | solution.py:250
  124.9 13.4 %collective-permute-start.26 = (f32[5,12,4,128]{3,2,1,0:T(4,128)S(1)}, f32[5,12,4,128]{3,2,1,0:T(4,128)S(1)}, u32[]{:S(2)}, u32[]{:S(2)}) collective-permute-start(f32[5,12,4,128]{3,2,1,0:T(4,128)S(1)} %pad_maximum_fusion.7), channel_id=1, source_target_pairs={{1,0},{2,1},{3,2},{0,3},{5,4},{6,5},{7,6},{4,7},{9,8},{10,9},{11,1... | collective-permute-start | bytes 368648 | tf_op jit(solution)/shard_map/ppermute | solution.py:256
  125.0 13.3 %collective-permute-start.25 = (f32[5,12,4,128]{3,2,1,0:T(4,128)S(1)}, f32[5,12,4,128]{3,2,1,0:T(4,128)S(1)}, u32[]{:S(2)}, u32[]{:S(2)}) collective-permute-start(f32[5,12,4,128]{3,2,1,0:T(4,128)S(1)} %pad_maximum_fusion.6), channel_id=1, source_target_pairs={{0,1},{1,2},{2,3},{3,0},{4,5},{5,6},{6,7},{7,4},{8,9},{9,10},{10,1... | collective-permute-start | bytes 368648 | tf_op jit(solution)/shard_map/ppermute | solution.py:255
  129.2 3.2 %collective-permute-start.21 = (f32[5,12,4,128]{3,2,1,0:T(4,128)S(1)}, f32[5,12,4,128]{3,2,1,0:T(4,128)S(1)}, u32[]{:S(2)}, u32[]{:S(2)}) collective-permute-start(f32[5,12,4,128]{3,2,1,0:T(4,128)S(1)} %get-tuple-element.37), channel_id=1, source_target_pairs={{0,1},{1,2},{2,3},{3,0},{4,5},{5,6},{6,7},{7,4},{8,9},{9,10},{10,1... | collective-permute-start | bytes 368648 | tf_op jit(solution)/shard_map/ppermute | solution.py:255
  130.0 4.3 %collective-permute-start.22 = (f32[5,12,4,128]{3,2,1,0:T(4,128)S(1)}, f32[5,12,4,128]{3,2,1,0:T(4,128)S(1)}, u32[]{:S(2)}, u32[]{:S(2)}) collective-permute-start(f32[5,12,4,128]{3,2,1,0:T(4,128)S(1)} %get-tuple-element.36), channel_id=1, source_target_pairs={{1,0},{2,1},{3,2},{0,3},{5,4},{6,5},{7,6},{4,7},{9,8},{10,9},{11,1... | collective-permute-start | bytes 368648 | tf_op jit(solution)/shard_map/ppermute | solution.py:256
  (1 other events, 0.7 us)

commit v4 on v3

--- a/solution.py
+++ b/solution.py
@@ -6,6 +6,7 @@
 from jax.experimental import pallas as pl
 from jax.experimental.pallas import tpu as pltpu
 from jax.sharding import PartitionSpec as P
+
 
 STEPS = 4
 ROUNDS = 4
@@ -278,15 +279,16 @@
 
     scratch = [pltpu.VMEM((6, height, rows + 2 * PAD, lanes), f32)] * 2
     params = pltpu.CompilerParams(vmem_limit_bytes=40 << 20)
+    low = moved(low, home, away, 1)
     for turn in range(ROUNDS):
         last = turn == ROUNDS - 1
         before = home if turn == 0 else away
         after = home if last else away
         place_of = home_place if last else away_place
         own = staying if before is after else moved(staying, before, after, 0)
-        low, high = moved(low, before, after, 1), moved(high, before, after, 1)
+        high = moved(high, before, after, 1)
         left, right = beside([own], after)
-        early, seam = pl.pallas_call(
+        first = pl.pallas_call(
             functools.partial(first_kernel, turn, place_of, (ng, block, rows)),
             out_shape=[piece(lows, 6 if last else len(SENT)), jax.ShapeDtypeStruct((STEPS - 1, 6, 2, rows + 2 * PAD, lanes), f32)],
             in_specs=[smem] + [vmem] * 3,
@@ -295,13 +297,17 @@
             compiler_params=params,
             cost_estimate=cost(28, 3000000),
             name="first",
-        )(table, own, left, right)
+        )
+        early, seam = first(table, own, left, right)
+        if not last:
+            to = home if turn == ROUNDS - 2 else away
+            next_low = moved(early, away, to, 1)
         left2, right2 = beside([low, high], after)
         if last:
             shapes = [jax.ShapeDtypeStruct((n, block, rows, lanes), f32) for n in (4, 2)]
         else:
             shapes = [piece(kept), piece(highs)]
-        outs = pl.pallas_call(
+        second = pl.pallas_call(
             functools.partial(second_kernel, turn, place_of, (ng, block, rows), last),
             out_shape=shapes,
             in_specs=[smem] + [vmem] * 10,
@@ -310,9 +316,11 @@
             compiler_params=params,
             cost_estimate=cost(48, 6000000),
             name="second",
-        )(table, own, left, right, seam, early, low, high, left2, right2, melt_index[turn] if last else away_index[turn])
+        )
+        index = melt_index[turn] if last else away_index[turn]
+        outs = second(table, own, left, right, seam, early, low, high, left2, right2, index)
         staying, high = outs
-        low = early
+        low = next_low
     return outs[0], outs[1]
 
 

time: 147 us -> 147 us (level)
  no operation moved by 1% of the time
where the time goes in v4:
time: 147 us; the launch traced here: 146 us
  waiting for transfers between devices  58 us (39%)
  Pallas kernels  44.6 us (30%)
  starting transfers between devices  36.8 us (25%)
  local copies, waits for them, and re-layouts  3.15 us (2%)
  between operations  1.8 us (1%)
    ppermute x10, waiting for transfers between devices, moved(): return lax.ppermute(array, AXES, route)  48.9 us
    pallas_call x4, Pallas kernels, on_device(): second(table, own, left, right, seam, early, low, high, left2, right2, in...  25.7 us
    ppermute x10, starting transfers between devices, moved(): return lax.ppermute(array, AXES, route)  23.5 us
    pallas_call x4, Pallas kernels, on_device(): early, seam = first(table, own, left, right)  15.9 us
    ppermute x8, starting transfers between devices, beside(): lax.ppermute(first, AXES, [(where(g, (l + 1) % nl), where(g, l)) for g, l...  7.8 us
    ppermute x8, waiting for transfers between devices, beside(): lax.ppermute(final, AXES, [(where(g, l), where(g, (l + 1) % nl)) for g, l...  7.16 us
    ppermute x8, starting transfers between devices, beside(): lax.ppermute(final, AXES, [(where(g, l), where(g, (l + 1) % nl)) for g, l...  4.88 us
    pallas_call x1, Pallas kernels, on_device(): pl.pallas_call(prepare_kernel, out_shape=[piece(n) for n in (kept, lows,...  3.02 us
  transfers between devices with their start and end apart: 27, of which 9 were waited for; matrix products, arithmetic and copies ran while one was open for 2% of the time, Pallas kernels for 15%

profile of v4, /device:TPU:17, one launch (start us, length us, event | category | flops | bytes accessed | tf_op | source)
XLA Modules:
  0.0 145.6 jit_solution(14510466009963619277)
XLA Ops:
  0.6 3.0 %prepare.1 = (f32[5,12,32,128]{3,2,1,0:T(8,128)}, f32[5,4,32,128]{3,2,1,0:T(8,128)}, f32[5,8,32,128]{3,2,1,0:T(8,128)}) custom-call(s32[16,32,128]{2,1,0:T(8,128)} %labels.1, f32[4,16,32,128]{3,2,1,0:T(8,128)} %roughness.1, f32[2,16,32,128]{3,2,1,0:T(8,128)} %potential.1), custom_call_target="tpu_custom_call" | custom-call | tf_op jit(solution)/shard_map/prepare/pallas_call | solution.py:266
  3.7 3.7 %collective-permute-start = (f32[5,12,32,128]{3,2,1,0:T(8,128)}, f32[5,12,32,128]{3,2,1,0:T(8,128)S(1)}, u32[]{:S(2)}, u32[]{:S(2)}) collective-permute-start(f32[5,12,32,128]{3,2,1,0:T(8,128)} %get-tuple-element.19), channel_id=1, source_target_pairs={{0,0},{1,4},{2,6},{3,2},{4,1},{5,5},{6,7},{7,3},{8,8},{9,12},{10,1... | collective-permute-start | bytes 2949128 | tf_op jit(solution)/shard_map/ppermute | solution.py:251
  7.4 1.9 %collective-permute-start.4 = (f32[5,8,32,128]{3,2,1,0:T(8,128)}, f32[5,8,32,128]{3,2,1,0:T(8,128)S(1)}, u32[]{:S(2)}, u32[]{:S(2)}) collective-permute-start(f32[5,8,32,128]{3,2,1,0:T(8,128)} %get-tuple-element.23), channel_id=1, source_target_pairs={{4,0},{5,4},{6,6},{7,2},{8,1},{9,5},{10,7},{11,3},{12,8},{13,12},{... | collective-permute-start | bytes 1966088 | tf_op jit(solution)/shard_map/ppermute | solution.py:251
  9.3 1.9 %collective-permute-start.3 = (f32[5,4,32,128]{3,2,1,0:T(8,128)}, f32[5,4,32,128]{3,2,1,0:T(8,128)S(1)}, u32[]{:S(2)}, u32[]{:S(2)}) collective-permute-start(f32[5,4,32,128]{3,2,1,0:T(8,128)} %get-tuple-element.22), channel_id=1, source_target_pairs={{4,0},{5,4},{6,6},{7,2},{8,1},{9,5},{10,7},{11,3},{12,8},{13,12},{... | collective-permute-start | bytes 983048 | tf_op jit(solution)/shard_map/ppermute | solution.py:251
  16.4 15.8 %collective-permute-done.3.low = f32[5,4,32,128]{3,2,1,0:T(8,128)S(1)} collective-permute-done((f32[5,4,32,128]{3,2,1,0:T(8,128)}, f32[5,4,32,128]{3,2,1,0:T(8,128)S(1)}, u32[]{:S(2)}, u32[]{:S(2)}) %collective-permute-start.3) | collective-permute-done | bytes 327712 | tf_op jit(solution)/shard_map/ppermute | solution.py:251
  32.4 1.5 %collective-permute-start.6 = (f32[5,12,4,128]{3,2,1,0:T(4,128)S(1)}, f32[5,12,4,128]{3,2,1,0:T(4,128)S(1)}, u32[]{:S(2)}, u32[]{:S(2)}) collective-permute-start(f32[5,12,4,128]{3,2,1,0:T(4,128)S(1)} %pad_maximum_fusion.1), channel_id=1, source_target_pairs={{4,0},{6,4},{2,6},{0,2},{5,1},{7,5},{3,7},{1,3},{12,8},{14,12},{10... | collective-permute-start | bytes 368648 | tf_op jit(solution)/shard_map/ppermute | solution.py:257
  35.5 4.4 %collective-permute-done.1.left = f32[5,12,4,128]{3,2,1,0:T(4,128)S(1)} collective-permute-done((f32[5,12,4,128]{3,2,1,0:T(4,128)S(1)}, f32[5,12,4,128]{3,2,1,0:T(4,128)S(1)}, u32[]{:S(2)}, u32[]{:S(2)}) %collective-permute-start.1) | collective-permute-done | bytes 122912 | tf_op jit(solution)/shard_map/ppermute | solution.py:256
  40.0 4.0 %first.4 = (f32[5,4,32,128]{3,2,1,0:T(8,128)S(1)}, f32[3,6,2,48,128]{4,3,2,1,0:T(8,128)S(1)}) custom-call(f32[72]{0:T(128)S(1)} %concatenate.27.table, f32[5,12,32,128]{3,2,1,0:T(8,128)S(1)} %collective-permute-done.own, f32[5,12,4,128]{3,2,1,0:T(4,128)S(1)} %collective-permute-done.1.left, f32[5,12,4,128]{3,2,1,0:T(4,128)S(1)} %collective-permute-done.2.right), custom_call_target="tpu_custom_call" | custom-call | flops 89456640 | bytes 3000000 | tf_op jit(solution)/shard_map/first/pallas_call | solution.py:301
  44.0 6.1 %second.4 = (f32[5,12,32,128]{3,2,1,0:T(8,128)S(1)}, f32[5,8,32,128]{3,2,1,0:T(8,128)S(1)}) custom-call(f32[72]{0:T(128)S(1)} %concatenate.27.table, f32[5,12,32,128]{3,2,1,0:T(8,128)S(1)} %collective-permute-done.own, f32[5,12,4,128]{3,2,1,0:T(4,128)S(1)} %collective-permute-done.1.left, f32[5,12,4,128]{3,2,1,0:T(4,128)S(1)} %collective-permute-done.2.right, ...), custom_call_target="tpu_custom_call" | custom-call | flops 153354240 | bytes 6000000 | tf_op jit(solution)/shard_map/second/pallas_call | solution.py:321
  50.1 2.3 %collective-permute-start.11 = (f32[5,8,32,128]{3,2,1,0:T(8,128)S(1)}, f32[5,8,32,128]{3,2,1,0:T(8,128)S(1)}, u32[]{:S(2)}, u32[]{:S(2)}) collective-permute-start(f32[5,8,32,128]{3,2,1,0:T(8,128)S(1)} %get-tuple-element.27), channel_id=1, source_target_pairs={{1,0},{5,4},{7,6},{3,2},{8,1},{12,5},{14,7},{10,3},{9,8},{13,12},{... | collective-permute-start | bytes 1966088 | tf_op jit(solution)/shard_map/ppermute | solution.py:251
  52.4 2.1 %collective-permute-start.10 = (f32[5,4,32,128]{3,2,1,0:T(8,128)S(1)}, f32[5,4,32,128]{3,2,1,0:T(8,128)S(1)}, u32[]{:S(2)}, u32[]{:S(2)}) collective-permute-start(f32[5,4,32,128]{3,2,1,0:T(8,128)S(1)} %get-tuple-element.21.early), channel_id=1, source_target_pairs={{1,0},{5,4},{7,6},{3,2},{8,1},{12,5},{14,7},{10,3},{9,8},{13,12},{... | collective-permute-start | bytes 983048 | tf_op jit(solution)/shard_map/ppermute | solution.py:251
  55.5 1.0 collective-permute-start.9
  56.5 9.1 %collective-permute-done.10.low = f32[5,4,32,128]{3,2,1,0:T(8,128)S(1)} collective-permute-done((f32[5,4,32,128]{3,2,1,0:T(8,128)S(1)}, f32[5,4,32,128]{3,2,1,0:T(8,128)S(1)}, u32[]{:S(2)}, u32[]{:S(2)}) %collective-permute-start.10) | collective-permute-done | bytes 327712 | tf_op jit(solution)/shard_map/ppermute | solution.py:251
  65.6 1.9 %collective-permute-start.13 = (f32[5,12,4,128]{3,2,1,0:T(4,128)S(1)}, f32[5,12,4,128]{3,2,1,0:T(4,128)S(1)}, u32[]{:S(2)}, u32[]{:S(2)}) collective-permute-start(f32[5,12,4,128]{3,2,1,0:T(4,128)S(1)} %pad_maximum_fusion.3), channel_id=1, source_target_pairs={{4,0},{6,4},{2,6},{0,2},{5,1},{7,5},{3,7},{1,3},{12,8},{14,12},{10... | collective-permute-start | bytes 368648 | tf_op jit(solution)/shard_map/ppermute | solution.py:257
  67.7 4.0 %first.5 = (f32[5,4,32,128]{3,2,1,0:T(8,128)S(1)}, f32[3,6,2,48,128]{4,3,2,1,0:T(8,128)S(1)}) custom-call(f32[72]{0:T(128)S(1)} %concatenate.27.table, f32[5,12,32,128]{3,2,1,0:T(8,128)S(1)} %get-tuple-element.24.own, f32[5,12,4,128]{3,2,1,0:T(4,128)S(1)} %collective-permute-done.8.left, f32[5,12,4,128]{3,2,1,0:T(4,128)S(1)} %collective-permute-done.9.right), custom_call_target="tpu_custom_call" | custom-call | flops 89456640 | bytes 3000000 | tf_op jit(solution)/shard_map/first/pallas_call | solution.py:301
  71.6 1.9 %collective-permute-start.16 = (f32[5,4,32,128]{3,2,1,0:T(8,128)S(1)}, f32[5,4,32,128]{3,2,1,0:T(8,128)S(1)}, u32[]{:S(2)}, u32[]{:S(2)}) collective-permute-start(f32[5,4,32,128]{3,2,1,0:T(8,128)S(1)} %get-tuple-element.26.early), channel_id=1, source_target_pairs={{1,0},{5,4},{7,6},{3,2},{8,1},{12,5},{14,7},{10,3},{9,8},{13,12},{... | collective-permute-start | bytes 983048 | tf_op jit(solution)/shard_map/ppermute | solution.py:251
  73.6 6.1 %second.5 = (f32[5,12,32,128]{3,2,1,0:T(8,128)S(1)}, f32[5,8,32,128]{3,2,1,0:T(8,128)S(1)}) custom-call(f32[72]{0:T(128)S(1)} %concatenate.27.table, f32[5,12,32,128]{3,2,1,0:T(8,128)S(1)} %get-tuple-element.24.own, f32[5,12,4,128]{3,2,1,0:T(4,128)S(1)} %collective-permute-done.8.left, f32[5,12,4,128]{3,2,1,0:T(4,128)S(1)} %collective-permute-done.9.right, ...), custom_call_target="tpu_custom_call" | custom-call | flops 153354240 | bytes 6000000 | tf_op jit(solution)/shard_map/second/pallas_call | solution.py:321
  79.7 2.4 %collective-permute-start.17 = (f32[5,8,32,128]{3,2,1,0:T(8,128)S(1)}, f32[5,8,32,128]{3,2,1,0:T(8,128)S(1)}, u32[]{:S(2)}, u32[]{:S(2)}) collective-permute-start(f32[5,8,32,128]{3,2,1,0:T(8,128)S(1)} %get-tuple-element.31), channel_id=1, source_target_pairs={{1,0},{5,4},{7,6},{3,2},{8,1},{12,5},{14,7},{10,3},{9,8},{13,12},{... | collective-permute-start | bytes 1966088 | tf_op jit(solution)/shard_map/ppermute | solution.py:251
  83.8 7.9 %collective-permute-done.17.high = f32[5,8,32,128]{3,2,1,0:T(8,128)S(1)} collective-permute-done((f32[5,8,32,128]{3,2,1,0:T(8,128)S(1)}, f32[5,8,32,128]{3,2,1,0:T(8,128)S(1)}, u32[]{:S(2)}, u32[]{:S(2)}) %collective-permute-start.17) | collective-permute-done | bytes 655392 | tf_op jit(solution)/shard_map/ppermute | solution.py:251
  91.7 1.5 %collective-permute-start.19 = (f32[5,12,4,128]{3,2,1,0:T(4,128)S(1)}, f32[5,12,4,128]{3,2,1,0:T(4,128)S(1)}, u32[]{:S(2)}, u32[]{:S(2)}) collective-permute-start(f32[5,12,4,128]{3,2,1,0:T(4,128)S(1)} %pad_maximum_fusion.5), channel_id=1, source_target_pairs={{4,0},{6,4},{2,6},{0,2},{5,1},{7,5},{3,7},{1,3},{12,8},{14,12},{10... | collective-permute-start | bytes 368648 | tf_op jit(solution)/shard_map/ppermute | solution.py:257
  93.3 4.0 %first.6 = (f32[5,4,32,128]{3,2,1,0:T(8,128)S(1)}, f32[3,6,2,48,128]{4,3,2,1,0:T(8,128)S(1)}) custom-call(f32[72]{0:T(128)S(1)} %concatenate.27.table, f32[5,12,32,128]{3,2,1,0:T(8,128)S(1)} %get-tuple-element.28.own, f32[5,12,4,128]{3,2,1,0:T(4,128)S(1)} %collective-permute-done.14.left, f32[5,12,4,128]{3,2,1,0:T(4,128)S(1)} %collective-permute-done.15.right), custom_call_target="tpu_custom_call" | custom-call | flops 89456640 | bytes 3000000 | tf_op jit(solution)/shard_map/first/pallas_call | solution.py:301
  97.7 6.1 %second.6 = (f32[5,12,32,128]{3,2,1,0:T(8,128)S(1)}, f32[5,8,32,128]{3,2,1,0:T(8,128)S(1)}) custom-call(f32[72]{0:T(128)S(1)} %concatenate.27.table, f32[5,12,32,128]{3,2,1,0:T(8,128)S(1)} %get-tuple-element.28.own, f32[5,12,4,128]{3,2,1,0:T(4,128)S(1)} %collective-permute-done.14.left, f32[5,12,4,128]{3,2,1,0:T(4,128)S(1)} %collective-permute-done.15.right, ...), custom_call_target="tpu_custom_call" | custom-call | flops 153354240 | bytes 6000000 | tf_op jit(solution)/shard_map/second/pallas_call | solution.py:321
  103.8 1.9 %collective-permute-start.24 = (f32[5,8,32,128]{3,2,1,0:T(8,128)S(1)}, f32[5,8,32,128]{3,2,1,0:T(8,128)S(1)}, u32[]{:S(2)}, u32[]{:S(2)}) collective-permute-start(f32[5,8,32,128]{3,2,1,0:T(8,128)S(1)} %get-tuple-element.35), channel_id=1, source_target_pairs={{1,0},{5,1},{7,2},{3,3},{8,4},{12,5},{14,6},{10,7},{9,8},{13,9},{1... | collective-permute-start | bytes 1966088 | tf_op jit(solution)/shard_map/ppermute | solution.py:251
  105.8 1.9 %collective-permute-start.23 = (f32[5,4,32,128]{3,2,1,0:T(8,128)S(1)}, f32[5,4,32,128]{3,2,1,0:T(8,128)S(1)}, u32[]{:S(2)}, u32[]{:S(2)}) collective-permute-start(f32[5,4,32,128]{3,2,1,0:T(8,128)S(1)} %get-tuple-element.30.early), channel_id=1, source_target_pairs={{1,0},{5,1},{7,2},{3,3},{8,4},{12,5},{14,6},{10,7},{9,8},{13,9},{1... | collective-permute-start | bytes 983048 | tf_op jit(solution)/shard_map/ppermute | solution.py:251
  107.7 3.4 %collective-permute-start.20 = (f32[5,12,32,128]{3,2,1,0:T(8,128)S(1)}, f32[5,12,32,128]{3,2,1,0:T(8,128)S(1)}, u32[]{:S(2)}, u32[]{:S(2)}) collective-permute-start(f32[5,12,32,128]{3,2,1,0:T(8,128)S(1)} %get-tuple-element.32), channel_id=1, source_target_pairs={{0,0},{4,1},{6,2},{2,3},{1,4},{5,5},{7,6},{3,7},{8,8},{12,9},{14,1... | collective-permute-start | bytes 2949128 | tf_op jit(solution)/shard_map/ppermute | solution.py:251
  111.1 13.7 %collective-permute-done.23.low = f32[5,4,32,128]{3,2,1,0:T(8,128)S(1)} collective-permute-done((f32[5,4,32,128]{3,2,1,0:T(8,128)S(1)}, f32[5,4,32,128]{3,2,1,0:T(8,128)S(1)}, u32[]{:S(2)}, u32[]{:S(2)}) %collective-permute-start.23) | collective-permute-done | bytes 327712 | tf_op jit(solution)/shard_map/ppermute | solution.py:251
  125.0 1.8 %collective-permute-start.25 = (f32[5,12,4,128]{3,2,1,0:T(4,128)S(1)}, f32[5,12,4,128]{3,2,1,0:T(4,128)S(1)}, u32[]{:S(2)}, u32[]{:S(2)}) collective-permute-start(f32[5,12,4,128]{3,2,1,0:T(4,128)S(1)} %pad_maximum_fusion.6), channel_id=1, source_target_pairs={{0,1},{1,2},{2,3},{3,0},{4,5},{5,6},{6,7},{7,4},{8,9},{9,10},{10,1... | collective-permute-start | bytes 368648 | tf_op jit(solution)/shard_map/ppermute | solution.py:256
  126.8 2.4 %collective-permute-done.20.own = f32[5,12,32,128]{3,2,1,0:T(8,128)S(1)} collective-permute-done((f32[5,12,32,128]{3,2,1,0:T(8,128)S(1)}, f32[5,12,32,128]{3,2,1,0:T(8,128)S(1)}, u32[]{:S(2)}, u32[]{:S(2)}) %collective-permute-start.20) | collective-permute-done | bytes 983072 | tf_op jit(solution)/shard_map/ppermute | solution.py:251
  130.1 2.4 %collective-permute-done.21.left = f32[5,12,4,128]{3,2,1,0:T(4,128)S(1)} collective-permute-done((f32[5,12,4,128]{3,2,1,0:T(4,128)S(1)}, f32[5,12,4,128]{3,2,1,0:T(4,128)S(1)}, u32[]{:S(2)}, u32[]{:S(2)}) %collective-permute-start.21) | collective-permute-done | bytes 122912 | tf_op jit(solution)/shard_map/ppermute | solution.py:256
  132.4 1.9 %collective-permute-done.22.right = f32[5,12,4,128]{3,2,1,0:T(4,128)S(1)} collective-permute-done((f32[5,12,4,128]{3,2,1,0:T(4,128)S(1)}, f32[5,12,4,128]{3,2,1,0:T(4,128)S(1)}, u32[]{:S(2)}, u32[]{:S(2)}) %collective-permute-start.22) | collective-permute-done | bytes 122912 | tf_op jit(solution)/shard_map/ppermute | solution.py:257
  134.3 4.0 %first.7 = (f32[6,4,32,128]{3,2,1,0:T(8,128)S(1)}, f32[3,6,2,48,128]{4,3,2,1,0:T(8,128)S(1)}) custom-call(f32[72]{0:T(128)S(1)} %concatenate.27.table, f32[5,12,32,128]{3,2,1,0:T(8,128)S(1)} %collective-permute-done.20.own, f32[5,12,4,128]{3,2,1,0:T(4,128)S(1)} %collective-permute-done.21.left, f32[5,12,4,128]{3,2,1,0:T(4,128)S(1)} %collective-permute-done.22.right), custom_call_target="tpu_custom_call" | custom-call | flops 89456640 | bytes 3000000 | tf_op jit(solution)/shard_map/first/pallas_call | solution.py:301
  138.3 7.3 %second.7 = (f32[4,16,32,128]{3,2,1,0:T(8,128)}, f32[2,16,32,128]{3,2,1,0:T(8,128)}) custom-call(f32[72]{0:T(128)S(1)} %concatenate.27.table, f32[5,12,32,128]{3,2,1,0:T(8,128)S(1)} %collective-permute-done.20.own, f32[5,12,4,128]{3,2,1,0:T(4,128)S(1)} %collective-permute-done.21.left, f32[5,12,4,128]{3,2,1,0:T(4,128)S(1)} %collective-permute-done.22.right, ...), custom_call_target="tpu_custom_call" | custom-call | flops 153354240 | bytes 6000000 | tf_op jit(solution)/shard_map/second/pallas_call | solution.py:321
  (82 shorter events, 10.5 us)
Async XLA Ops:
  0.6 10.6 %copy-start = (s32[4,8,32,128]{3,2,1,0:T(8,128)S(1)}, s32[4,8,32,128]{3,2,1,0:T(8,128)}, u32[]{:S(2)}) copy-start(s32[4,8,32,128]{3,2,1,0:T(8,128)} %param.17) | copy-start | bytes 1572868
  3.7 30.3 %collective-permute-start = (f32[5,12,32,128]{3,2,1,0:T(8,128)}, f32[5,12,32,128]{3,2,1,0:T(8,128)S(1)}, u32[]{:S(2)}, u32[]{:S(2)}) collective-permute-start(f32[5,12,32,128]{3,2,1,0:T(8,128)} %get-tuple-element.19), channel_id=1, source_target_pairs={{0,0},{1,4},{2,6},{3,2},{4,1},{5,5},{6,7},{7,3},{8,8},{9,12},{10,1... | collective-permute-start | bytes 2949128 | tf_op jit(solution)/shard_map/ppermute | solution.py:251
  7.4 24.9 %collective-permute-start.4 = (f32[5,8,32,128]{3,2,1,0:T(8,128)}, f32[5,8,32,128]{3,2,1,0:T(8,128)S(1)}, u32[]{:S(2)}, u32[]{:S(2)}) collective-permute-start(f32[5,8,32,128]{3,2,1,0:T(8,128)} %get-tuple-element.23), channel_id=1, source_target_pairs={{4,0},{5,4},{6,6},{7,2},{8,1},{9,5},{10,7},{11,3},{12,8},{13,12},{... | collective-permute-start | bytes 1966088 | tf_op jit(solution)/shard_map/ppermute | solution.py:251
  9.3 2.7 %copy-start.2 = (f32[4,3]{1,0:T(4,128)S(1)}, f32[4,3]{1,0:T(4,128)}, u32[]{:S(2)}) copy-start(f32[4,3]{1,0:T(4,128)} %param.12) | copy-start | bytes 148
  9.3 22.9 %collective-permute-start.3 = (f32[5,4,32,128]{3,2,1,0:T(8,128)}, f32[5,4,32,128]{3,2,1,0:T(8,128)S(1)}, u32[]{:S(2)}, u32[]{:S(2)}) collective-permute-start(f32[5,4,32,128]{3,2,1,0:T(8,128)} %get-tuple-element.22), channel_id=1, source_target_pairs={{4,0},{5,4},{6,6},{7,2},{8,1},{9,5},{10,7},{11,3},{12,8},{13,12},{... | collective-permute-start | bytes 983048 | tf_op jit(solution)/shard_map/ppermute | solution.py:251
  11.3 0.8 copy-start.1
  11.3 24.2 %collective-permute-start.7 = (s32[3,8,32,128]{3,2,1,0:T(8,128)S(1)}, s32[3,8,32,128]{3,2,1,0:T(8,128)S(1)}, u32[]{:S(2)}, u32[]{:S(2)}) collective-permute-start(s32[3,8,32,128]{3,2,1,0:T(8,128)S(1)} %slice.97), channel_id=1, source_target_pairs={{28,25},{29,29},{30,31},{31,27}} | collective-permute-start | bytes 1179656 | tf_op jit(solution)/shard_map/ppermute | solution.py:274
  12.4 0.7 copy-start.5
  14.8 0.7 copy-start.3
  32.3 11.6 %collective-permute-start.5 = (f32[5,12,4,128]{3,2,1,0:T(4,128)S(1)}, f32[5,12,4,128]{3,2,1,0:T(4,128)S(1)}, u32[]{:S(2)}, u32[]{:S(2)}) collective-permute-start(f32[5,12,4,128]{3,2,1,0:T(4,128)S(1)} %pad_maximum_fusion), channel_id=1, source_target_pairs={{0,4},{4,6},{6,2},{2,0},{1,5},{5,7},{7,3},{3,1},{8,12},{12,14},{14... | collective-permute-start | bytes 368648 | tf_op jit(solution)/shard_map/ppermute | solution.py:256
  32.4 11.5 %collective-permute-start.6 = (f32[5,12,4,128]{3,2,1,0:T(4,128)S(1)}, f32[5,12,4,128]{3,2,1,0:T(4,128)S(1)}, u32[]{:S(2)}, u32[]{:S(2)}) collective-permute-start(f32[5,12,4,128]{3,2,1,0:T(4,128)S(1)} %pad_maximum_fusion.1), channel_id=1, source_target_pairs={{4,0},{6,4},{2,6},{0,2},{5,1},{7,5},{3,7},{1,3},{12,8},{14,12},{10... | collective-permute-start | bytes 368648 | tf_op jit(solution)/shard_map/ppermute | solution.py:257
  34.0 6.0 %collective-permute-start.1 = (f32[5,12,4,128]{3,2,1,0:T(4,128)S(1)}, f32[5,12,4,128]{3,2,1,0:T(4,128)S(1)}, u32[]{:S(2)}, u32[]{:S(2)}) collective-permute-start(f32[5,12,4,128]{3,2,1,0:T(4,128)S(1)} %get-tuple-element.43), channel_id=1, source_target_pairs={{0,4},{4,6},{6,2},{2,0},{1,5},{5,7},{7,3},{3,1},{8,12},{12,14},{14... | collective-permute-start | bytes 368648 | tf_op jit(solution)/shard_map/ppermute | solution.py:256
  34.6 5.4 %collective-permute-start.2 = (f32[5,12,4,128]{3,2,1,0:T(4,128)S(1)}, f32[5,12,4,128]{3,2,1,0:T(4,128)S(1)}, u32[]{:S(2)}, u32[]{:S(2)}) collective-permute-start(f32[5,12,4,128]{3,2,1,0:T(4,128)S(1)} %get-tuple-element.42), channel_id=1, source_target_pairs={{4,0},{6,4},{2,6},{0,2},{5,1},{7,5},{3,7},{1,3},{12,8},{14,12},{10... | collective-permute-start | bytes 368648 | tf_op jit(solution)/shard_map/ppermute | solution.py:257
  50.1 15.4 %collective-permute-start.11 = (f32[5,8,32,128]{3,2,1,0:T(8,128)S(1)}, f32[5,8,32,128]{3,2,1,0:T(8,128)S(1)}, u32[]{:S(2)}, u32[]{:S(2)}) collective-permute-start(f32[5,8,32,128]{3,2,1,0:T(8,128)S(1)} %get-tuple-element.27), channel_id=1, source_target_pairs={{1,0},{5,4},{7,6},{3,2},{8,1},{12,5},{14,7},{10,3},{9,8},{13,12},{... | collective-permute-start | bytes 1966088 | tf_op jit(solution)/shard_map/ppermute | solution.py:251
  52.4 13.1 %collective-permute-start.10 = (f32[5,4,32,128]{3,2,1,0:T(8,128)S(1)}, f32[5,4,32,128]{3,2,1,0:T(8,128)S(1)}, u32[]{:S(2)}, u32[]{:S(2)}) collective-permute-start(f32[5,4,32,128]{3,2,1,0:T(8,128)S(1)} %get-tuple-element.21.early), channel_id=1, source_target_pairs={{1,0},{5,4},{7,6},{3,2},{8,1},{12,5},{14,7},{10,3},{9,8},{13,12},{... | collective-permute-start | bytes 983048 | tf_op jit(solution)/shard_map/ppermute | solution.py:251
  54.6 13.1 %collective-permute-start.8 = (f32[5,12,4,128]{3,2,1,0:T(4,128)S(1)}, f32[5,12,4,128]{3,2,1,0:T(4,128)S(1)}, u32[]{:S(2)}, u32[]{:S(2)}) collective-permute-start(f32[5,12,4,128]{3,2,1,0:T(4,128)S(1)} %get-tuple-element.41), channel_id=1, source_target_pairs={{0,4},{4,6},{6,2},{2,0},{1,5},{5,7},{7,3},{3,1},{8,12},{12,14},{14... | collective-permute-start | bytes 368648 | tf_op jit(solution)/shard_map/ppermute | solution.py:256
  55.5 12.2 %collective-permute-start.9 = (f32[5,12,4,128]{3,2,1,0:T(4,128)S(1)}, f32[5,12,4,128]{3,2,1,0:T(4,128)S(1)}, u32[]{:S(2)}, u32[]{:S(2)}) collective-permute-start(f32[5,12,4,128]{3,2,1,0:T(4,128)S(1)} %get-tuple-element.40), channel_id=1, source_target_pairs={{4,0},{6,4},{2,6},{0,2},{5,1},{7,5},{3,7},{1,3},{12,8},{14,12},{10... | collective-permute-start | bytes 368648 | tf_op jit(solution)/shard_map/ppermute | solution.py:257
  65.6 7.9 %collective-permute-start.13 = (f32[5,12,4,128]{3,2,1,0:T(4,128)S(1)}, f32[5,12,4,128]{3,2,1,0:T(4,128)S(1)}, u32[]{:S(2)}, u32[]{:S(2)}) collective-permute-start(f32[5,12,4,128]{3,2,1,0:T(4,128)S(1)} %pad_maximum_fusion.3), channel_id=1, source_target_pairs={{4,0},{6,4},{2,6},{0,2},{5,1},{7,5},{3,7},{1,3},{12,8},{14,12},{10... | collective-permute-start | bytes 368648 | tf_op jit(solution)/shard_map/ppermute | solution.py:257
  67.6 6.0 %collective-permute-start.12 = (f32[5,12,4,128]{3,2,1,0:T(4,128)S(1)}, f32[5,12,4,128]{3,2,1,0:T(4,128)S(1)}, u32[]{:S(2)}, u32[]{:S(2)}) collective-permute-start(f32[5,12,4,128]{3,2,1,0:T(4,128)S(1)} %pad_maximum_fusion.2), channel_id=1, source_target_pairs={{0,4},{4,6},{6,2},{2,0},{1,5},{5,7},{7,3},{3,1},{8,12},{12,14},{14... | collective-permute-start | bytes 368648 | tf_op jit(solution)/shard_map/ppermute | solution.py:256
  71.6 10.5 %collective-permute-start.16 = (f32[5,4,32,128]{3,2,1,0:T(8,128)S(1)}, f32[5,4,32,128]{3,2,1,0:T(8,128)S(1)}, u32[]{:S(2)}, u32[]{:S(2)}) collective-permute-start(f32[5,4,32,128]{3,2,1,0:T(8,128)S(1)} %get-tuple-element.26.early), channel_id=1, source_target_pairs={{1,0},{5,4},{7,6},{3,2},{8,1},{12,5},{14,7},{10,3},{9,8},{13,12},{... | collective-permute-start | bytes 983048 | tf_op jit(solution)/shard_map/ppermute | solution.py:251
  79.7 11.9 %collective-permute-start.17 = (f32[5,8,32,128]{3,2,1,0:T(8,128)S(1)}, f32[5,8,32,128]{3,2,1,0:T(8,128)S(1)}, u32[]{:S(2)}, u32[]{:S(2)}) collective-permute-start(f32[5,8,32,128]{3,2,1,0:T(8,128)S(1)} %get-tuple-element.31), channel_id=1, source_target_pairs={{1,0},{5,4},{7,6},{3,2},{8,1},{12,5},{14,7},{10,3},{9,8},{13,12},{... | collective-permute-start | bytes 1966088 | tf_op jit(solution)/shard_map/ppermute | solution.py:251
  82.2 11.1 %collective-permute-start.14 = (f32[5,12,4,128]{3,2,1,0:T(4,128)S(1)}, f32[5,12,4,128]{3,2,1,0:T(4,128)S(1)}, u32[]{:S(2)}, u32[]{:S(2)}) collective-permute-start(f32[5,12,4,128]{3,2,1,0:T(4,128)S(1)} %get-tuple-element.39), channel_id=1, source_target_pairs={{0,4},{4,6},{6,2},{2,0},{1,5},{5,7},{7,3},{3,1},{8,12},{12,14},{14... | collective-permute-start | bytes 368648 | tf_op jit(solution)/shard_map/ppermute | solution.py:256
  82.8 10.5 %collective-permute-start.15 = (f32[5,12,4,128]{3,2,1,0:T(4,128)S(1)}, f32[5,12,4,128]{3,2,1,0:T(4,128)S(1)}, u32[]{:S(2)}, u32[]{:S(2)}) collective-permute-start(f32[5,12,4,128]{3,2,1,0:T(4,128)S(1)} %get-tuple-element.38), channel_id=1, source_target_pairs={{4,0},{6,4},{2,6},{0,2},{5,1},{7,5},{3,7},{1,3},{12,8},{14,12},{10... | collective-permute-start | bytes 368648 | tf_op jit(solution)/shard_map/ppermute | solution.py:257
  91.7 5.6 %collective-permute-start.19 = (f32[5,12,4,128]{3,2,1,0:T(4,128)S(1)}, f32[5,12,4,128]{3,2,1,0:T(4,128)S(1)}, u32[]{:S(2)}, u32[]{:S(2)}) collective-permute-start(f32[5,12,4,128]{3,2,1,0:T(4,128)S(1)} %pad_maximum_fusion.5), channel_id=1, source_target_pairs={{4,0},{6,4},{2,6},{0,2},{5,1},{7,5},{3,7},{1,3},{12,8},{14,12},{10... | collective-permute-start | bytes 368648 | tf_op jit(solution)/shard_map/ppermute | solution.py:257
  93.2 4.4 %collective-permute-start.18 = (f32[5,12,4,128]{3,2,1,0:T(4,128)S(1)}, f32[5,12,4,128]{3,2,1,0:T(4,128)S(1)}, u32[]{:S(2)}, u32[]{:S(2)}) collective-permute-start(f32[5,12,4,128]{3,2,1,0:T(4,128)S(1)} %pad_maximum_fusion.4), channel_id=1, source_target_pairs={{0,4},{4,6},{6,2},{2,0},{1,5},{5,7},{7,3},{3,1},{8,12},{12,14},{14... | collective-permute-start | bytes 368648 | tf_op jit(solution)/shard_map/ppermute | solution.py:256
  103.8 21.0 %collective-permute-start.24 = (f32[5,8,32,128]{3,2,1,0:T(8,128)S(1)}, f32[5,8,32,128]{3,2,1,0:T(8,128)S(1)}, u32[]{:S(2)}, u32[]{:S(2)}) collective-permute-start(f32[5,8,32,128]{3,2,1,0:T(8,128)S(1)} %get-tuple-element.35), channel_id=1, source_target_pairs={{1,0},{5,1},{7,2},{3,3},{8,4},{12,5},{14,6},{10,7},{9,8},{13,9},{1... | collective-permute-start | bytes 1966088 | tf_op jit(solution)/shard_map/ppermute | solution.py:251
  105.8 19.0 %collective-permute-start.23 = (f32[5,4,32,128]{3,2,1,0:T(8,128)S(1)}, f32[5,4,32,128]{3,2,1,0:T(8,128)S(1)}, u32[]{:S(2)}, u32[]{:S(2)}) collective-permute-start(f32[5,4,32,128]{3,2,1,0:T(8,128)S(1)} %get-tuple-element.30.early), channel_id=1, source_target_pairs={{1,0},{5,1},{7,2},{3,3},{8,4},{12,5},{14,6},{10,7},{9,8},{13,9},{1... | collective-permute-start | bytes 983048 | tf_op jit(solution)/shard_map/ppermute | solution.py:251
  107.7 21.5 %collective-permute-start.20 = (f32[5,12,32,128]{3,2,1,0:T(8,128)S(1)}, f32[5,12,32,128]{3,2,1,0:T(8,128)S(1)}, u32[]{:S(2)}, u32[]{:S(2)}) collective-permute-start(f32[5,12,32,128]{3,2,1,0:T(8,128)S(1)} %get-tuple-element.32), channel_id=1, source_target_pairs={{0,0},{4,1},{6,2},{2,3},{1,4},{5,5},{7,6},{3,7},{8,8},{12,9},{14,1... | collective-permute-start | bytes 2949128 | tf_op jit(solution)/shard_map/ppermute | solution.py:251
  124.9 13.4 %collective-permute-start.26 = (f32[5,12,4,128]{3,2,1,0:T(4,128)S(1)}, f32[5,12,4,128]{3,2,1,0:T(4,128)S(1)}, u32[]{:S(2)}, u32[]{:S(2)}) collective-permute-start(f32[5,12,4,128]{3,2,1,0:T(4,128)S(1)} %pad_maximum_fusion.7), channel_id=1, source_target_pairs={{1,0},{2,1},{3,2},{0,3},{5,4},{6,5},{7,6},{4,7},{9,8},{10,9},{11,1... | collective-permute-start | bytes 368648 | tf_op jit(solution)/shard_map/ppermute | solution.py:257
  125.0 13.3 %collective-permute-start.25 = (f32[5,12,4,128]{3,2,1,0:T(4,128)S(1)}, f32[5,12,4,128]{3,2,1,0:T(4,128)S(1)}, u32[]{:S(2)}, u32[]{:S(2)}) collective-permute-start(f32[5,12,4,128]{3,2,1,0:T(4,128)S(1)} %pad_maximum_fusion.6), channel_id=1, source_target_pairs={{0,1},{1,2},{2,3},{3,0},{4,5},{5,6},{6,7},{7,4},{8,9},{9,10},{10,1... | collective-permute-start | bytes 368648 | tf_op jit(solution)/shard_map/ppermute | solution.py:256
  129.2 3.2 %collective-permute-start.21 = (f32[5,12,4,128]{3,2,1,0:T(4,128)S(1)}, f32[5,12,4,128]{3,2,1,0:T(4,128)S(1)}, u32[]{:S(2)}, u32[]{:S(2)}) collective-permute-start(f32[5,12,4,128]{3,2,1,0:T(4,128)S(1)} %get-tuple-element.37), channel_id=1, source_target_pairs={{0,1},{1,2},{2,3},{3,0},{4,5},{5,6},{6,7},{7,4},{8,9},{9,10},{10,1... | collective-permute-start | bytes 368648 | tf_op jit(solution)/shard_map/ppermute | solution.py:256
  130.0 4.3 %collective-permute-start.22 = (f32[5,12,4,128]{3,2,1,0:T(4,128)S(1)}, f32[5,12,4,128]{3,2,1,0:T(4,128)S(1)}, u32[]{:S(2)}, u32[]{:S(2)}) collective-permute-start(f32[5,12,4,128]{3,2,1,0:T(4,128)S(1)} %get-tuple-element.36), channel_id=1, source_target_pairs={{1,0},{2,1},{3,2},{0,3},{5,4},{6,5},{7,6},{4,7},{9,8},{10,9},{11,1... | collective-permute-start | bytes 368648 | tf_op jit(solution)/shard_map/ppermute | solution.py:257
  (1 other events, 0.7 us)

commit v5 on v3

v5 whole, which is shorter than its diff:
```python
import functools

import jax
import jax.numpy as jnp
from jax import lax
from jax.experimental import pallas as pl
from jax.experimental.pallas import tpu as pltpu
from jax.sharding import PartitionSpec as P


STEPS = 4
ROUNDS = 4
SHIFT = 8
SENT = (0, 1, 2, 4, 5)
PAD = 8
DT = 0.04
PLANES = 2
AXES = ("grow", "lat")
GRAD, CENTER, COUPLE, LATENT, RELEASE, SPREAD, STAY, MELT = 0, 12, 16, 24, 28, 36, 38, 40


def scalar_table(grad_coef, composition, latent, diffusivity, melt_table):
    scaled = DT * grad_coef
    return jnp.concatenate(
        [
            scaled.reshape(-1),
            1.0 + DT - 2.0 * jnp.sum(scaled, axis=1),
            (DT * (composition - jnp.mean(composition, axis=0))).reshape(-1),
            DT * (latent - jnp.mean(latent)),
            (composition - composition[3]).reshape(-1),
            DT * diffusivity,
            1.0 - 6.0 * DT * diffusivity,
            melt_table.reshape(-1),
        ]
    )


class Round:
    def __init__(self, turn, place, sizes, table, even, odd):
        self.ng, self.block, self.rows = sizes
        self.table, self.levels = table, (even, odd, even, odd)
        self.start = place * self.block + SHIFT * (turn + 1) - STEPS
        self.lowest = SHIFT * turn - self.start
        self.top = self.ng * self.block + SHIFT * turn - 1 - self.start

    def fill(self, source, halo, planes, to, halo_from=0):
        level = self.levels[0]

        @pl.loop(0, planes)
        def _(i):
            body = [source[f, i] for f in range(len(SENT))]
            side = [halo[f, i + halo_from] for f in range(len(SENT))]
            body.insert(3, 1.0 - body[0] - body[1] - body[2])
            side.insert(3, 1.0 - side[0] - side[1] - side[2])
            for f in range(6):
                level[f, i + to, PAD : PAD + self.rows] = body[f]
                level[f, i + to, PAD - STEPS : PAD] = side[f][:STEPS]
                level[f, i + to, PAD + self.rows : PAD + self.rows + STEPS] = side[f][STEPS:]

    def advance(self, src, e, at):
        table, window = self.table, pl.ds(at, 8)
        up, down = jnp.minimum(e + 1, self.top), jnp.maximum(e - 1, self.lowest)
        total = float(self.ng * self.block)
        theta = ((e + self.start).astype(jnp.float32) - 0.5 * total) / total
        mid = [src[f, e, window] for f in range(6)]
        gsum = [src[f, up, window] + src[f, down, window] for f in range(6)]
        xsum = [src[f, e, pl.ds(at + 1, 8)] + src[f, e, pl.ds(at - 1, 8)] for f in range(6)]
        ysum = [pltpu.roll(v, 1, 1) + pltpu.roll(v, v.shape[1] - 1, 1) for v in mid]
        spread = [
            table[GRAD + 3 * a] * gsum[a]
            + table[GRAD + 3 * a + 1] * xsum[a]
            + table[GRAD + 3 * a + 2] * ysum[a]
            + table[CENTER + a] * mid[a]
            for a in range(4)
        ]
        mean = 0.25 * (spread[0] + spread[1] + spread[2] + spread[3]) - 0.25
        trial = [
            spread[a]
            - mean
            - table[COUPLE + 2 * a] * mid[4]
            - table[COUPLE + 2 * a + 1] * mid[5]
            - table[LATENT + a] * theta
            for a in range(3)
        ]
        trial.append(1.0 - trial[0] - trial[1] - trial[2])
        clipped = [jnp.clip(t, 0.0, 1.0) for t in trial]
        inverse = 1.0 / (clipped[0] + clipped[1] + clipped[2] + clipped[3])
        new = [c * inverse for c in clipped]
        change = [n - v for n, v in zip(new[:3], mid[:3])]
        for k in range(2):
            release = table[RELEASE + k] * change[0]
            for a in range(1, 3):
                release = release + table[RELEASE + 2 * a + k] * change[a]
            sides = gsum[4 + k] + xsum[4 + k] + ysum[4 + k]
            new.append(table[SPREAD + k] * sides + table[STAY + k] * mid[4 + k] - release)
        return new

    def sweep(self, step, first, stop, write=None):
        src, dst = self.levels[step - 1], self.levels[step % STEPS]
        if write is None:
            tiles = [PAD - STEPS + 8 * t for t in range(self.rows // 8 + 1)]

            def write(e, at, new):
                for f in range(6):
                    dst[f, e, pl.ds(at, 8)] = new[f]

        else:
            tiles = [PAD + 8 * t for t in range(self.rows // 8)]

        @pl.loop(0, (stop - first) // PLANES)
        def _(i):
            for p in range(PLANES):
                e = first + PLANES * i + p
                for at in tiles:
                    write(e, at, self.advance(src, e, at))


def part_kernel(turn, place_of, sizes, begin, parts, has_seam, gives_seam, first_out, fresh, table, *refs):
    refs, (even, odd) = list(refs[:-2]), refs[-2:]
    place = place_of()
    run = Round(turn, place, sizes, table, even, odd)
    end = begin
    seam = refs.pop(0) if has_seam else None
    index = refs.pop(0) if fresh else None
    for planes, halo_from in parts:
        if halo_from == 0:
            source, halo = refs.pop(0), refs.pop(0)
        else:
            source = refs.pop(0)
        run.fill(source, halo, planes, end, halo_from)
        end += planes
    next_seam = refs.pop() if gives_seam else None
    outs = refs

    def bounds(step):
        return (begin if has_seam else 2 * step) - step, end - step

    for level in range(STEPS):
        if has_seam:
            for plane in range(2):
                for f in range(6):
                    run.levels[level][f, begin - level - 2 + plane] = seam[level, f, plane]

    def hold(level):
        if gives_seam:
            for plane in range(2):
                for f in range(6):
                    next_seam[level, f, plane] = run.levels[level][f, end - level - 2 + plane]

    def write(targets):
        def put(e, at, new):
            for ref in targets:
                for i, f in enumerate(SENT):
                    ref[i, e - STEPS - first_out, pl.ds(at - PAD, 8)] = new[f]

        return put

    hold(0)
    for step in range(1, STEPS):
        run.sweep(step, *bounds(step))
        hold(step)
    first, last = bounds(STEPS)
    ends = [first_out + STEPS + ref.shape[1] for ref in outs]
    marks = sorted(set([first, last] + [m for m in ends if first < m < last]))
    for low, high in zip(marks, marks[1:]):
        run.sweep(STEPS, low, high, write([ref for ref, m in zip(outs, ends) if m >= high]))

    if fresh:

        @pl.when(place == run.ng - 1)
        def _():
            for j in range(SHIFT):
                e = run.block - SHIFT + j + STEPS
                put = write([ref for ref, m in zip(outs, ends) if m > e])
                for t in range(run.rows // 8):
                    put(e, PAD + 8 * t, melt(table, index[j, pl.ds(8 * t, 8)]))


def melt(table, row):
    mu = [jnp.zeros(row.shape, jnp.float32)] * 2
    for m in range((table.shape[0] - MELT) // 2):
        mu = [jnp.where(row == m, table[MELT + 2 * m + k], mu[k]) for k in range(2)]
    none = jnp.zeros(row.shape, jnp.float32)
    return [none, none, none, none + 1.0] + mu


def finish_kernel(place_of, ng, table, index, *refs):
    pieces, (phases, potentials) = refs[:-2], refs[-2:]

    def put(o, here, new):
        for a in range(4):
            phases[a, o, here] = new[a]
        for k in range(2):
            potentials[k, o, here] = new[4 + k]

    at = 0
    for part in pieces:

        @pl.loop(0, part.shape[1])
        def _(i, part=part, at=at):
            new = [part[f, i] for f in range(len(SENT))]
            new.insert(3, 1.0 - new[0] - new[1] - new[2])
            put(i + at, slice(None), new)

        at += part.shape[1]

    @pl.when(place_of() == ng - 1)
    def _():
        for j in range(SHIFT):
            for t in range(index.shape[1] // 8):
                here = pl.ds(8 * t, 8)
                put(at - SHIFT + j, here, melt(table, index[j, here]))


def prepare_kernel(labels, roughness, potential, low, high, staying):
    lows, highs = low.shape[1], high.shape[1]

    def plane(o, kept):
        kind = labels[o]
        rough = [roughness[a, o] for a in range(4)]
        inverse = 1.0 / (3.0 + rough[0] + rough[1] + rough[2] + rough[3])
        new = [(jnp.where(kind == a, 3.0, 0.0) + rough[a]) * inverse for a in range(3)]
        new += [potential[0, o], potential[1, o]]
        for ref, at in kept:
            for f, value in enumerate(new):
                ref[f, at] = value

    @pl.loop(0, lows)
    def _(o):
        plane(o, [(low, o)])

    @pl.loop(lows, lows + highs)
    def _(o):
        plane(o, [(high, o - lows), (staying, o - lows)])

    @pl.loop(lows + highs, labels.shape[0])
    def _(o):
        plane(o, [(staying, o - lows)])


def on_device(ng, nl, labels, roughness, potential, grad_coef, composition, latent, diffusivity, melt_table, melt_index):
    block, rows, lanes = labels.shape
    vmem = pl.BlockSpec(memory_space=pltpu.VMEM)
    smem = pl.BlockSpec(memory_space=pltpu.SMEM)
    f32 = jnp.float32
    kept = block - SHIFT + STEPS
    lows = block - kept
    highs = SHIFT + STEPS - lows
    height = kept + lows + highs
    table = scalar_table(grad_coef, composition, latent, diffusivity, melt_table)

    def home(g, l):
        return g * nl + l

    def away(g, l):
        return (g // 2 * 2 + (l % 2 ^ (l // 2 % 2))) * nl + l // 2 * 2 + g % 2

    def home_place():
        return lax.axis_index("grow")

    def away_place():
        return lax.axis_index("grow") // 2 * 2 + lax.axis_index("lat") % 2

    blocks = [(g, l) for g in range(ng) for l in range(nl)]

    def moved(array, before, after, climb):
        route = [(before(g + climb, l), after(g, l)) for g, l in blocks if g + climb < ng]
        return lax.ppermute(array, AXES, route)

    def beside(parts, where):
        first = jnp.concatenate([p[:, :, :STEPS] for p in parts], axis=1)
        final = jnp.concatenate([p[:, :, rows - STEPS :] for p in parts], axis=1)
        left = lax.ppermute(final, AXES, [(where(g, l), where(g, (l + 1) % nl)) for g, l in blocks])
        right = lax.ppermute(first, AXES, [(where(g, (l + 1) % nl), where(g, l)) for g, l in blocks])
        return left, right

    def piece(planes, width=rows):
        return jax.ShapeDtypeStruct((len(SENT), planes, width, lanes), f32)

    def cost(planes, moved_bytes):
        return pl.CostEstimate(flops=130 * 6 * planes * rows * lanes, bytes_accessed=moved_bytes, transcendentals=0)

    seam_shape = jax.ShapeDtypeStruct((STEPS, 6, 2, rows + 2 * PAD, lanes), f32)
    scratch = [pltpu.VMEM((6, height, rows + 2 * PAD, lanes), f32)] * 2

    def part(turn, begin, planes, has_seam, gives_seam, first_out, sent, *args, fresh=False):
        size = sum(n for n, _ in planes)
        return pl.pallas_call(
            functools.partial(
                part_kernel, turn, away_place, (ng, block, rows), begin, planes, has_seam, gives_seam, first_out, fresh
            ),
            out_shape=[piece(n) for n in sent] + [seam_shape] * gives_seam,
            in_specs=[smem] + [vmem] * len(args),
            out_specs=[vmem] * (len(sent) + gives_seam),
            scratch_shapes=scratch,
            compiler_params=pltpu.CompilerParams(vmem_limit_bytes=40 << 20),
            cost_estimate=cost(4 * size, 4000000),
            name="part",
        )(table, *args)

    low, high, staying = pl.pallas_call(
        prepare_kernel,
        out_shape=[piece(n) for n in (lows, highs, kept)],
        in_specs=[vmem] * 3,
        out_specs=[vmem] * 3,
        name="prepare",
    )(labels, roughness, potential)

    away_index = lax.ppermute(
        melt_index[: ROUNDS - 1],
        AXES,
        [(home(ng - 1, l), away(ng - 1, l)) for l in range(nl)],
    )

    early = low
    for turn in range(ROUNDS):
        last = turn == ROUNDS - 1
        before = home if turn == 0 else away
        left, right = beside([early, staying], before)
        own_halo = jnp.concatenate([left[:, lows:], right[:, lows:]], axis=2)
        halo = jnp.concatenate([left[:, : lows + highs], right[:, : lows + highs]], axis=2)
        if turn == 0:
            staying = moved(staying, before, away, 0)
            own_halo = moved(own_halo, before, away, 0)
            low = moved(low, before, away, 1)
        high = moved(high, before, away, 1)
        halo = moved(halo, before, away, 1)
        early, seam = part(turn, 0, [(kept, 0)], False, True, 0, [lows], staying, own_halo)
        next_low = moved(early, away, home if last else away, 0 if last else 1)
        if last:
            break
        staying, high = functools.partial(part, fresh=True)(
            turn,
            kept,
            [(lows, 0), (highs, lows)],
            True,
            False,
            lows,
            [kept, highs],
            seam,
            away_index[turn],
            low,
            halo,
            high,
        )
        low = next_low

    cut = 2
    middle, seam = part(
        turn, kept, [(lows, 0), (cut, lows)], True, True, lows, [lows + cut], seam, low, halo, high[:, :cut]
    )
    middle = moved(middle, away, home, 0)
    (final,) = part(
        turn,
        kept + lows + cut,
        [(highs - cut, 0)],
        True,
        False,
        2 * lows + cut,
        [highs - cut],
        seam,
        high[:, cut:],
        halo[:, lows + cut :],
    )
    final = moved(final, away, home, 0)
    return pl.pallas_call(
        functools.partial(finish_kernel, home_place, ng),
        out_shape=[jax.ShapeDtypeStruct((n, block, rows, lanes), f32) for n in (4, 2)],
        in_specs=[smem] + [vmem] * 4,
        out_specs=[vmem] * 2,
        name="finish",
    )(table, melt_index[turn], next_low, middle, final)


def solution(mesh):
    ng, nl = mesh.shape["grow"], mesh.shape["lat"]
    placed = (
        P("grow", "lat", None),
        P(None, "grow", "lat", None),
        P(None, "grow", "lat", None),
        P(),
        P(),
        P(),
        P(),
        P(),
        P(None, None, "lat", None),
    )
    return jax.shard_map(
        functools.partial(on_device, ng, nl),
        mesh=mesh,
        in_specs=placed,
        out_specs=(P(None, "grow", "lat", None), P(None, "grow", "lat", None)),
        check_vma=False,
    )
```

time: 147 us -> 148 us (level)
  waiting for transfers between devices: 58 us -> 32.5 us
  starting transfers between devices: 36.8 us -> 54.7 us
  local copies, waits for them, and re-layouts: 3.15 us -> 8.15 us
  Pallas kernels: 44.6 us -> 47.4 us
    ppermute x10 -> x17, waiting for transfers between devices: 48.9 us -> 25.1 us  [moved(): return lax.ppermute(array, AXES, route)]
    ppermute x10 -> x17, starting transfers between devices: 23.5 us -> 44.3 us  [moved(): return lax.ppermute(array, AXES, route)]
    ppermute x8 -> x4, waiting for transfers between devices: 7.16 us -> 0.19 us  [beside(): lax.ppermute(final, AXES, [(where(g, l), where(g, (l + 1) % nl)) for g, l...]
    ppermute x8 -> x4, starting transfers between devices: 7.8 us -> 1.5 us  [beside(): lax.ppermute(first, AXES, [(where(g, (l + 1) % nl), where(g, l)) for g, l...]
    ppermute x8 -> x4, waiting for transfers between devices: 1.94 us -> 7.22 us  [beside(): lax.ppermute(first, AXES, [(where(g, (l + 1) % nl), where(g, l)) for g, l...]
    ppermute x8 -> x4, starting transfers between devices: 4.88 us -> 8.21 us  [beside(): lax.ppermute(final, AXES, [(where(g, l), where(g, (l + 1) % nl)) for g, l...]
    pallas_call x9 -> x11, Pallas kernels: 44.6 us -> 47.4 us  [the longest x9 41.8 us: part(): pl.pallas_call(functools.partial(part_kernel, turn, away_place, (ng, bloc...]
    slice x12 -> x19, local copies, waits for them, and re-layouts: 0.37 us -> 2.53 us  [the longest x8 2.25 us: beside(): final = jnp.concatenate([p[:, :, rows - STEPS:] for p in parts], axis=1)]
  transfers between devices with their start and end apart: 27 -> 26, of which waited for: 9 -> 9; matrix products, arithmetic and copies ran while one was open for 2% -> 6% of each run, Pallas kernels for 15% -> 11%
where the time goes in v5:
time: 148 us; the launch traced here: 147 us
  starting transfers between devices  54.7 us (37%)
  Pallas kernels  47.4 us (32%)
  waiting for transfers between devices  32.5 us (22%)
  local copies, waits for them, and re-layouts  8.15 us (6%)
  other arithmetic  2.27 us (2%)
  between operations  1.84 us (1%)
    ppermute x17, starting transfers between devices, moved(): return lax.ppermute(array, AXES, route)  44.3 us
    pallas_call x9, Pallas kernels, part(): pl.pallas_call(functools.partial(part_kernel, turn, away_place, (ng, bloc...  41.8 us
    ppermute x17, waiting for transfers between devices, moved(): return lax.ppermute(array, AXES, route)  25.1 us
    ppermute x4, starting transfers between devices, beside(): lax.ppermute(final, AXES, [(where(g, l), where(g, (l + 1) % nl)) for g, l...  8.21 us
    ppermute x4, waiting for transfers between devices, beside(): lax.ppermute(first, AXES, [(where(g, (l + 1) % nl), where(g, l)) for g, l...  7.22 us
    pallas_call x1, Pallas kernels, on_device(): pl.pallas_call(prepare_kernel, out_shape=[piece(n) for n in (lows, highs,...  3.03 us
  transfers between devices with their start and end apart: 26, of which 9 were waited for; matrix products, arithmetic and copies ran while one was open for 6% of the time, Pallas kernels for 11%

profile of v5, /device:TPU:17, one launch (start us, length us, event | category | flops | bytes accessed | tf_op | source)
XLA Modules:
  0.0 146.9 jit_solution(17547128045509372110)
XLA Ops:
  0.7 3.0 %prepare.1 = (f32[5,4,32,128]{3,2,1,0:T(8,128)}, f32[5,8,32,128]{3,2,1,0:T(8,128)}, f32[5,12,32,128]{3,2,1,0:T(8,128)}) custom-call(s32[16,32,128]{2,1,0:T(8,128)} %labels.1, f32[4,16,32,128]{3,2,1,0:T(8,128)} %roughness.1, f32[2,16,32,128]{3,2,1,0:T(8,128)} %potential.1), custom_call_target="tpu_custom_call" | custom-call | tf_op jit(solution)/shard_map/prepare/pallas_call | solution.py:301
  3.7 3.7 %collective-permute-start = (f32[5,12,32,128]{3,2,1,0:T(8,128)}, f32[5,12,32,128]{3,2,1,0:T(8,128)S(1)}, u32[]{:S(2)}, u32[]{:S(2)}) collective-permute-start(f32[5,12,32,128]{3,2,1,0:T(8,128)} %get-tuple-element.21), channel_id=1, source_target_pairs={{0,0},{1,4},{2,6},{3,2},{4,1},{5,5},{6,7},{7,3},{8,8},{9,12},{10,1... | collective-permute-start | bytes 2949128 | tf_op jit(solution)/shard_map/ppermute | solution.py:268
  7.4 1.9 %collective-permute-start.5 = (f32[5,4,32,128]{3,2,1,0:T(8,128)}, f32[5,4,32,128]{3,2,1,0:T(8,128)S(1)}, u32[]{:S(2)}, u32[]{:S(2)}) collective-permute-start(f32[5,4,32,128]{3,2,1,0:T(8,128)} %get-tuple-element.22), channel_id=1, source_target_pairs={{4,0},{5,4},{6,6},{7,2},{8,1},{9,5},{10,7},{11,3},{12,8},{13,12},{... | collective-permute-start | bytes 983048 | tf_op jit(solution)/shard_map/ppermute | solution.py:268
  13.1 1.9 %collective-permute-start.7 = (f32[5,8,32,128]{3,2,1,0:T(8,128)}, f32[5,8,32,128]{3,2,1,0:T(8,128)S(1)}, u32[]{:S(2)}, u32[]{:S(2)}) collective-permute-start(f32[5,8,32,128]{3,2,1,0:T(8,128)} %get-tuple-element.24), channel_id=1, source_target_pairs={{4,0},{5,4},{6,6},{7,2},{8,1},{9,5},{10,7},{11,3},{12,8},{13,12},{... | collective-permute-start | bytes 1966088 | tf_op jit(solution)/shard_map/ppermute | solution.py:268
  21.2 4.3 %collective-permute-start.3 = (f32[5,12,8,128]{3,2,1,0:T(8,128)S(1)}, f32[5,12,8,128]{3,2,1,0:T(8,128)S(1)}, u32[]{:S(2)}, u32[]{:S(2)}) collective-permute-start(f32[5,12,8,128]{3,2,1,0:T(8,128)S(1)} %pad_maximum_fusion), channel_id=1, source_target_pairs={{0,0},{1,4},{2,6},{3,2},{4,1},{5,5},{6,7},{7,3},{8,8},{9,12},{10,1... | collective-permute-start | bytes 737288 | tf_op jit(solution)/shard_map/ppermute | solution.py:268
  25.6 1.9 %collective-permute-start.6 = (f32[5,12,8,128]{3,2,1,0:T(8,128)S(1)}, f32[5,12,8,128]{3,2,1,0:T(8,128)S(1)}, u32[]{:S(2)}, u32[]{:S(2)}) collective-permute-start(f32[5,12,8,128]{3,2,1,0:T(8,128)S(1)} %pad_maximum_fusion.1), channel_id=1, source_target_pairs={{4,0},{5,4},{6,6},{7,2},{8,1},{9,5},{10,7},{11,3},{12,8},{13,12},{... | collective-permute-start | bytes 737288 | tf_op jit(solution)/shard_map/ppermute | solution.py:268
  27.6 5.0 %collective-permute-done.3.refs_1_ = f32[5,12,8,128]{3,2,1,0:T(8,128)S(1)} collective-permute-done((f32[5,12,8,128]{3,2,1,0:T(8,128)S(1)}, f32[5,12,8,128]{3,2,1,0:T(8,128)S(1)}, u32[]{:S(2)}, u32[]{:S(2)}) %collective-permute-start.3) | collective-permute-done | bytes 245792 | tf_op jit(solution)/shard_map/ppermute | solution.py:268
  32.6 4.0 %part.9 = (f32[5,4,32,128]{3,2,1,0:T(8,128)S(1)}, f32[4,6,2,48,128]{4,3,2,1,0:T(8,128)S(1)}) custom-call(f32[72]{0:T(128)S(1)} %concatenate.51.table, f32[5,12,32,128]{3,2,1,0:T(8,128)S(1)} %collective-permute-done.refs_0_, f32[5,12,8,128]{3,2,1,0:T(8,128)S(1)} %collective-permute-done.3.refs_1_), custom_call_target="tpu_custom_call" | custom-call | flops 153354240 | bytes 4000000 | tf_op jit(solution)/shard_map/part/pallas_call | solution.py:288
  36.6 6.2 %part.10 = (f32[5,12,32,128]{3,2,1,0:T(8,128)S(1)}, f32[5,8,32,128]{3,2,1,0:T(8,128)S(1)}) custom-call(f32[72]{0:T(128)S(1)} %concatenate.51.table, f32[4,6,2,48,128]{4,3,2,1,0:T(8,128)S(1)} %get-tuple-element.23.refs_0_, s32[8,32,128]{2,1,0:T(8,128)S(1)} %get-tuple-element.50.refs_1_, f32[5,4,32,128]{3,2,1,0:T(8,128)S(1)} %collective-permute-done.5.refs_2_, ...), custom_call_target="tpu_custom_call" | custom-call | flops 153354240 | bytes 4000000 | tf_op jit(solution)/shard_map/part/pallas_call | solution.py:288
  43.0 4.9 %collective-permute-start.8 = (f32[5,16,4,128]{3,2,1,0:T(4,128)S(1)}, f32[5,16,4,128]{3,2,1,0:T(4,128)S(1)}, u32[]{:S(2)}, u32[]{:S(2)}) collective-permute-start(f32[5,16,4,128]{3,2,1,0:T(4,128)S(1)} %pad_maximum_fusion.10), channel_id=1, source_target_pairs={{0,4},{4,6},{6,2},{2,0},{1,5},{5,7},{7,3},{3,1},{8,12},{12,14},{14... | collective-permute-start | bytes 491528 | tf_op jit(solution)/shard_map/ppermute | solution.py:273
  49.9 1.9 %collective-permute-start.12 = (f32[5,8,32,128]{3,2,1,0:T(8,128)S(1)}, f32[5,8,32,128]{3,2,1,0:T(8,128)S(1)}, u32[]{:S(2)}, u32[]{:S(2)}) collective-permute-start(f32[5,8,32,128]{3,2,1,0:T(8,128)S(1)} %get-tuple-element.28), channel_id=1, source_target_pairs={{1,0},{5,4},{7,6},{3,2},{8,1},{12,5},{14,7},{10,3},{9,8},{13,12},{... | collective-permute-start | bytes 1966088 | tf_op jit(solution)/shard_map/ppermute | solution.py:268
  52.1 4.1 %collective-permute-done.9 = f32[5,16,4,128]{3,2,1,0:T(4,128)S(1)} collective-permute-done((f32[5,16,4,128]{3,2,1,0:T(4,128)S(1)}, f32[5,16,4,128]{3,2,1,0:T(4,128)S(1)}, u32[]{:S(2)}, u32[]{:S(2)}) %collective-permute-start.9) | collective-permute-done | bytes 163872 | tf_op jit(solution)/shard_map/ppermute | solution.py:274
  56.3 2.5 %collective-permute-start.11 = (f32[5,12,8,128]{3,2,1,0:T(8,128)S(1)}, f32[5,12,8,128]{3,2,1,0:T(8,128)S(1)}, u32[]{:S(2)}, u32[]{:S(2)}) collective-permute-start(f32[5,12,8,128]{3,2,1,0:T(8,128)S(1)} %pad_maximum_fusion.3), channel_id=1, source_target_pairs={{1,0},{5,4},{7,6},{3,2},{8,1},{12,5},{14,7},{10,3},{9,8},{13,12},{... | collective-permute-start | bytes 737288 | tf_op jit(solution)/shard_map/ppermute | solution.py:268
  58.8 4.0 %part.11 = (f32[5,4,32,128]{3,2,1,0:T(8,128)S(1)}, f32[4,6,2,48,128]{4,3,2,1,0:T(8,128)S(1)}) custom-call(f32[72]{0:T(128)S(1)} %concatenate.51.table, f32[5,12,32,128]{3,2,1,0:T(8,128)S(1)} %get-tuple-element.25.refs_0_, f32[5,12,8,128]{3,2,1,0:T(8,128)S(1)} %pad_maximum_fusion.2.refs_1_), custom_call_target="tpu_custom_call" | custom-call | flops 153354240 | bytes 4000000 | tf_op jit(solution)/shard_map/part/pallas_call | solution.py:288
  62.9 3.0 %collective-permute-done.11.refs_3_ = f32[5,12,8,128]{3,2,1,0:T(8,128)S(1)} collective-permute-done((f32[5,12,8,128]{3,2,1,0:T(8,128)S(1)}, f32[5,12,8,128]{3,2,1,0:T(8,128)S(1)}, u32[]{:S(2)}, u32[]{:S(2)}) %collective-permute-start.11) | collective-permute-done | bytes 245792 | tf_op jit(solution)/shard_map/ppermute | solution.py:268
  66.0 6.2 %part.12 = (f32[5,12,32,128]{3,2,1,0:T(8,128)S(1)}, f32[5,8,32,128]{3,2,1,0:T(8,128)S(1)}) custom-call(f32[72]{0:T(128)S(1)} %concatenate.51.table, f32[4,6,2,48,128]{4,3,2,1,0:T(8,128)S(1)} %get-tuple-element.27.refs_0_, s32[8,32,128]{2,1,0:T(8,128)S(1)} %get-tuple-element.49.refs_1_, f32[5,4,32,128]{3,2,1,0:T(8,128)S(1)} %collective-permute-done.10.refs_2_, ...), custom_call_target="tpu_custom_call" | custom-call | flops 153354240 | bytes 4000000 | tf_op jit(solution)/shard_map/part/pallas_call | solution.py:288
  75.8 2.2 %collective-permute-start.17 = (f32[5,8,32,128]{3,2,1,0:T(8,128)S(1)}, f32[5,8,32,128]{3,2,1,0:T(8,128)S(1)}, u32[]{:S(2)}, u32[]{:S(2)}) collective-permute-start(f32[5,8,32,128]{3,2,1,0:T(8,128)S(1)} %get-tuple-element.32), channel_id=1, source_target_pairs={{1,0},{5,4},{7,6},{3,2},{8,1},{12,5},{14,7},{10,3},{9,8},{13,12},{... | collective-permute-start | bytes 1966088 | tf_op jit(solution)/shard_map/ppermute | solution.py:268
  79.5 3.9 %collective-permute-start.16 = (f32[5,12,8,128]{3,2,1,0:T(8,128)S(1)}, f32[5,12,8,128]{3,2,1,0:T(8,128)S(1)}, u32[]{:S(2)}, u32[]{:S(2)}) collective-permute-start(f32[5,12,8,128]{3,2,1,0:T(8,128)S(1)} %pad_maximum_fusion.5), channel_id=1, source_target_pairs={{1,0},{5,4},{7,6},{3,2},{8,1},{12,5},{14,7},{10,3},{9,8},{13,12},{... | collective-permute-start | bytes 737288 | tf_op jit(solution)/shard_map/ppermute | solution.py:268
  83.5 4.0 %part.13 = (f32[5,4,32,128]{3,2,1,0:T(8,128)S(1)}, f32[4,6,2,48,128]{4,3,2,1,0:T(8,128)S(1)}) custom-call(f32[72]{0:T(128)S(1)} %concatenate.51.table, f32[5,12,32,128]{3,2,1,0:T(8,128)S(1)} %get-tuple-element.29.refs_0_, f32[5,12,8,128]{3,2,1,0:T(8,128)S(1)} %pad_maximum_fusion.4.refs_1_), custom_call_target="tpu_custom_call" | custom-call | flops 153354240 | bytes 4000000 | tf_op jit(solution)/shard_map/part/pallas_call | solution.py:288
  87.5 3.1 %collective-permute-done.16.refs_3_ = f32[5,12,8,128]{3,2,1,0:T(8,128)S(1)} collective-permute-done((f32[5,12,8,128]{3,2,1,0:T(8,128)S(1)}, f32[5,12,8,128]{3,2,1,0:T(8,128)S(1)}, u32[]{:S(2)}, u32[]{:S(2)}) %collective-permute-start.16) | collective-permute-done | bytes 245792 | tf_op jit(solution)/shard_map/ppermute | solution.py:268
  90.7 6.2 %part.14 = (f32[5,12,32,128]{3,2,1,0:T(8,128)S(1)}, f32[5,8,32,128]{3,2,1,0:T(8,128)S(1)}) custom-call(f32[72]{0:T(128)S(1)} %concatenate.51.table, f32[4,6,2,48,128]{4,3,2,1,0:T(8,128)S(1)} %get-tuple-element.31.refs_0_, s32[8,32,128]{2,1,0:T(8,128)S(1)} %get-tuple-element.48.refs_1_, f32[5,4,32,128]{3,2,1,0:T(8,128)S(1)} %collective-permute-done.15.refs_2_, ...), custom_call_target="tpu_custom_call" | custom-call | flops 153354240 | bytes 4000000 | tf_op jit(solution)/shard_map/part/pallas_call | solution.py:288
  100.5 3.6 %collective-permute-start.23 = (f32[5,8,32,128]{3,2,1,0:T(8,128)S(1)}, f32[5,8,32,128]{3,2,1,0:T(8,128)S(1)}, u32[]{:S(2)}, u32[]{:S(2)}) collective-permute-start(f32[5,8,32,128]{3,2,1,0:T(8,128)S(1)} %get-tuple-element.37), channel_id=1, source_target_pairs={{1,0},{5,4},{7,6},{3,2},{8,1},{12,5},{14,7},{10,3},{9,8},{13,12},{... | collective-permute-start | bytes 1966088 | tf_op jit(solution)/shard_map/ppermute | solution.py:268
  106.0 3.2 %collective-permute-start.22 = (f32[5,12,8,128]{3,2,1,0:T(8,128)S(1)}, f32[5,12,8,128]{3,2,1,0:T(8,128)S(1)}, u32[]{:S(2)}, u32[]{:S(2)}) collective-permute-start(f32[5,12,8,128]{3,2,1,0:T(8,128)S(1)} %pad_maximum_fusion.7), channel_id=1, source_target_pairs={{1,0},{5,4},{7,6},{3,2},{8,1},{12,5},{14,7},{10,3},{9,8},{13,12},{... | collective-permute-start | bytes 737288 | tf_op jit(solution)/shard_map/ppermute | solution.py:268
  109.4 4.0 %part.15 = (f32[5,4,32,128]{3,2,1,0:T(8,128)S(1)}, f32[4,6,2,48,128]{4,3,2,1,0:T(8,128)S(1)}) custom-call(f32[72]{0:T(128)S(1)} %concatenate.51.table, f32[5,12,32,128]{3,2,1,0:T(8,128)S(1)} %get-tuple-element.33.refs_0_, f32[5,12,8,128]{3,2,1,0:T(8,128)S(1)} %pad_maximum_fusion.6.refs_1_), custom_call_target="tpu_custom_call" | custom-call | flops 153354240 | bytes 4000000 | tf_op jit(solution)/shard_map/part/pallas_call | solution.py:288
  113.4 3.1 %collective-permute-done.22.refs_2_ = f32[5,12,8,128]{3,2,1,0:T(8,128)S(1)} collective-permute-done((f32[5,12,8,128]{3,2,1,0:T(8,128)S(1)}, f32[5,12,8,128]{3,2,1,0:T(8,128)S(1)}, u32[]{:S(2)}, u32[]{:S(2)}) %collective-permute-start.22) | collective-permute-done | bytes 245792 | tf_op jit(solution)/shard_map/ppermute | solution.py:268
  116.6 3.5 %part.16 = (f32[5,6,32,128]{3,2,1,0:T(8,128)S(1)}, f32[4,6,2,48,128]{4,3,2,1,0:T(8,128)S(1)}) custom-call(f32[72]{0:T(128)S(1)} %concatenate.51.table, f32[4,6,2,48,128]{4,3,2,1,0:T(8,128)S(1)} %get-tuple-element.36.refs_0_, f32[5,4,32,128]{3,2,1,0:T(8,128)S(1)} %collective-permute-done.21.refs_1_, f32[5,12,8,128]{3,2,1,0:T(8,128)S(1)} %collective-permute-done.22.refs_2_, ...), custom_call_target="tpu_custom_call" | custom-call | flops 76677120 | bytes 4000000 | tf_op jit(solution)/shard_map/part/pallas_call | solution.py:288
  120.1 3.4 %part.17 = f32[5,6,32,128]{3,2,1,0:T(8,128)S(1)} custom-call(f32[72]{0:T(128)S(1)} %concatenate.51.table, f32[4,6,2,48,128]{4,3,2,1,0:T(8,128)S(1)} %get-tuple-element.39.refs_0_, f32[5,6,32,128]{3,2,1,0:T(8,128)S(1)} %slice.184.refs_1_, f32[5,6,8,128]{3,2,1,0:T(8,128)S(1)} %slice.185.refs_2_), custom_call_target="tpu_custom_call" | custom-call | flops 76677120 | bytes 4000000 | tf_op jit(solution)/shard_map/part/pallas_call | solution.py:288
  123.6 1.9 %collective-permute-start.25 = (f32[5,6,32,128]{3,2,1,0:T(8,128)S(1)}, f32[5,6,32,128]{3,2,1,0:T(8,128)S(1)}, u32[]{:S(2)}, u32[]{:S(2)}) collective-permute-start(f32[5,6,32,128]{3,2,1,0:T(8,128)S(1)} %part.17), channel_id=1, source_target_pairs={{0,0},{4,1},{6,2},{2,3},{1,4},{5,5},{7,6},{3,7},{8,8},{12,9},{14,1... | collective-permute-start | bytes 1474568 | tf_op jit(solution)/shard_map/ppermute | solution.py:268
  125.5 3.6 %collective-permute-start.24 = (f32[5,6,32,128]{3,2,1,0:T(8,128)S(1)}, f32[5,6,32,128]{3,2,1,0:T(8,128)S(1)}, u32[]{:S(2)}, u32[]{:S(2)}) collective-permute-start(f32[5,6,32,128]{3,2,1,0:T(8,128)S(1)} %get-tuple-element.38), channel_id=1, source_target_pairs={{0,0},{4,1},{6,2},{2,3},{1,4},{5,5},{7,6},{3,7},{8,8},{12,9},{14,1... | collective-permute-start | bytes 1474568 | tf_op jit(solution)/shard_map/ppermute | solution.py:268
  129.2 1.9 %collective-permute-start.20 = (f32[5,4,32,128]{3,2,1,0:T(8,128)S(1)}, f32[5,4,32,128]{3,2,1,0:T(8,128)S(1)}, u32[]{:S(2)}, u32[]{:S(2)}) collective-permute-start(f32[5,4,32,128]{3,2,1,0:T(8,128)S(1)} %get-tuple-element.35), channel_id=1, source_target_pairs={{0,0},{4,1},{6,2},{2,3},{1,4},{5,5},{7,6},{3,7},{8,8},{12,9},{14,1... | collective-permute-start | bytes 983048 | tf_op jit(solution)/shard_map/ppermute | solution.py:268
  131.8 10.8 %collective-permute-done.20.refs_0_ = f32[5,4,32,128]{3,2,1,0:T(8,128)S(1)} collective-permute-done((f32[5,4,32,128]{3,2,1,0:T(8,128)S(1)}, f32[5,4,32,128]{3,2,1,0:T(8,128)S(1)}, u32[]{:S(2)}, u32[]{:S(2)}) %collective-permute-start.20) | collective-permute-done | bytes 327712 | tf_op jit(solution)/shard_map/ppermute | solution.py:268
  144.2 2.6 %finish.1 = (f32[4,16,32,128]{3,2,1,0:T(8,128)}, f32[2,16,32,128]{3,2,1,0:T(8,128)}) custom-call(f32[72]{0:T(128)} %copy-done, s32[8,32,128]{2,1,0:T(8,128)} %slice_bitcast_fusion.3.index, f32[5,4,32,128]{3,2,1,0:T(8,128)} %copy-done.4, f32[5,6,32,128]{3,2,1,0:T(8,128)} %copy-done.3, f32[5,6,32,128]{3,2,1,0:T(8,128)} %copy-done.2), custom_call_target="tpu_custom_call" | custom-call | tf_op jit(solution)/shard_map/finish/pallas_call | solution.py:366
  (105 shorter events, 25.0 us)
Async XLA Ops:
  0.6 14.5 %copy-start.5 = (f32[4,2]{0,1:T(2,128)S(1)}, f32[4,2]{0,1:T(2,128)}, u32[]{:S(2)}) copy-start(f32[4,2]{0,1:T(2,128)} %param.13) | copy-start | bytes 100
  0.7 14.8 %copy-start.8 = (f32[4]{0:T(128)S(1)}, f32[4]{0:T(128)}, u32[]{:S(2)}) copy-start(f32[4]{0:T(128)} %param.14) | copy-start | bytes 52
  0.7 16.1 %copy-start.9 = (f32[2]{0:T(128)S(1)}, f32[2]{0:T(128)}, u32[]{:S(2)}) copy-start(f32[2]{0:T(128)} %param.15) | copy-start | bytes 28
  0.7 18.1 %copy-start.7 = (f32[16,2]{0,1:T(2,128)S(1)}, f32[16,2]{0,1:T(2,128)}, u32[]{:S(2)}) copy-start(f32[16,2]{0,1:T(2,128)} %param.16) | copy-start | bytes 388
  0.7 18.9 %copy-start.1 = (s32[4,8,32,128]{3,2,1,0:T(8,128)S(1)}, s32[4,8,32,128]{3,2,1,0:T(8,128)}, u32[]{:S(2)}) copy-start(s32[4,8,32,128]{3,2,1,0:T(8,128)} %param.17) | copy-start | bytes 1572868
  3.7 28.8 %collective-permute-start = (f32[5,12,32,128]{3,2,1,0:T(8,128)}, f32[5,12,32,128]{3,2,1,0:T(8,128)S(1)}, u32[]{:S(2)}, u32[]{:S(2)}) collective-permute-start(f32[5,12,32,128]{3,2,1,0:T(8,128)} %get-tuple-element.21), channel_id=1, source_target_pairs={{0,0},{1,4},{2,6},{3,2},{4,1},{5,5},{6,7},{7,3},{8,8},{9,12},{10,1... | collective-permute-start | bytes 2949128 | tf_op jit(solution)/shard_map/ppermute | solution.py:268
  7.4 29.2 %collective-permute-start.5 = (f32[5,4,32,128]{3,2,1,0:T(8,128)}, f32[5,4,32,128]{3,2,1,0:T(8,128)S(1)}, u32[]{:S(2)}, u32[]{:S(2)}) collective-permute-start(f32[5,4,32,128]{3,2,1,0:T(8,128)} %get-tuple-element.22), channel_id=1, source_target_pairs={{4,0},{5,4},{6,6},{7,2},{8,1},{9,5},{10,7},{11,3},{12,8},{13,12},{... | collective-permute-start | bytes 983048 | tf_op jit(solution)/shard_map/ppermute | solution.py:268
  11.5 8.9 %collective-permute-start.1 = (f32[5,16,4,128]{3,2,1,0:T(4,128)S(1)}, f32[5,16,4,128]{3,2,1,0:T(4,128)S(1)}, u32[]{:S(2)}, u32[]{:S(2)}) collective-permute-start(f32[5,16,4,128]{3,2,1,0:T(4,128)S(1)} %pad_maximum_fusion.8), channel_id=1, source_target_pairs={{0,1},{1,2},{2,3},{3,0},{4,5},{5,6},{6,7},{7,4},{8,9},{9,10},{10,1... | collective-permute-start | bytes 491528 | tf_op jit(solution)/shard_map/ppermute | solution.py:273
  13.1 8.0 %collective-permute-start.2 = (f32[5,16,4,128]{3,2,1,0:T(4,128)S(1)}, f32[5,16,4,128]{3,2,1,0:T(4,128)S(1)}, u32[]{:S(2)}, u32[]{:S(2)}) collective-permute-start(f32[5,16,4,128]{3,2,1,0:T(4,128)S(1)} %pad_maximum_fusion.9), channel_id=1, source_target_pairs={{1,0},{2,1},{3,2},{0,3},{5,4},{6,5},{7,6},{4,7},{9,8},{10,9},{11,1... | collective-permute-start | bytes 491528 | tf_op jit(solution)/shard_map/ppermute | solution.py:274
  13.1 23.5 %collective-permute-start.7 = (f32[5,8,32,128]{3,2,1,0:T(8,128)}, f32[5,8,32,128]{3,2,1,0:T(8,128)S(1)}, u32[]{:S(2)}, u32[]{:S(2)}) collective-permute-start(f32[5,8,32,128]{3,2,1,0:T(8,128)} %get-tuple-element.24), channel_id=1, source_target_pairs={{4,0},{5,4},{6,6},{7,2},{8,1},{9,5},{10,7},{11,3},{12,8},{13,12},{... | collective-permute-start | bytes 1966088 | tf_op jit(solution)/shard_map/ppermute | solution.py:268
  20.4 99.8 %copy-start = (f32[72]{0:T(128)}, f32[72]{0:T(128)S(1)}, u32[]{:S(2)}) copy-start(f32[72]{0:T(128)S(1)} %concatenate.51.table) | copy-start | bytes 868
  20.4 5.2 %collective-permute-start.4 = (s32[3,8,32,128]{3,2,1,0:T(8,128)S(1)}, s32[3,8,32,128]{3,2,1,0:T(8,128)S(1)}, u32[]{:S(2)}, u32[]{:S(2)}) collective-permute-start(s32[3,8,32,128]{3,2,1,0:T(8,128)S(1)} %slice.131), channel_id=1, source_target_pairs={{28,25},{29,29},{30,31},{31,27}} | collective-permute-start | bytes 1179656 | tf_op jit(solution)/shard_map/ppermute | solution.py:309
  21.2 11.4 %collective-permute-start.3 = (f32[5,12,8,128]{3,2,1,0:T(8,128)S(1)}, f32[5,12,8,128]{3,2,1,0:T(8,128)S(1)}, u32[]{:S(2)}, u32[]{:S(2)}) collective-permute-start(f32[5,12,8,128]{3,2,1,0:T(8,128)S(1)} %pad_maximum_fusion), channel_id=1, source_target_pairs={{0,0},{1,4},{2,6},{3,2},{4,1},{5,5},{6,7},{7,3},{8,8},{9,12},{10,1... | collective-permute-start | bytes 737288 | tf_op jit(solution)/shard_map/ppermute | solution.py:268
  25.6 11.0 %collective-permute-start.6 = (f32[5,12,8,128]{3,2,1,0:T(8,128)S(1)}, f32[5,12,8,128]{3,2,1,0:T(8,128)S(1)}, u32[]{:S(2)}, u32[]{:S(2)}) collective-permute-start(f32[5,12,8,128]{3,2,1,0:T(8,128)S(1)} %pad_maximum_fusion.1), channel_id=1, source_target_pairs={{4,0},{5,4},{6,6},{7,2},{8,1},{9,5},{10,7},{11,3},{12,8},{13,12},{... | collective-permute-start | bytes 737288 | tf_op jit(solution)/shard_map/ppermute | solution.py:268
  43.0 9.0 %collective-permute-start.8 = (f32[5,16,4,128]{3,2,1,0:T(4,128)S(1)}, f32[5,16,4,128]{3,2,1,0:T(4,128)S(1)}, u32[]{:S(2)}, u32[]{:S(2)}) collective-permute-start(f32[5,16,4,128]{3,2,1,0:T(4,128)S(1)} %pad_maximum_fusion.10), channel_id=1, source_target_pairs={{0,4},{4,6},{6,2},{2,0},{1,5},{5,7},{7,3},{3,1},{8,12},{12,14},{14... | collective-permute-start | bytes 491528 | tf_op jit(solution)/shard_map/ppermute | solution.py:273
  47.9 15.0 %collective-permute-start.10 = (f32[5,4,32,128]{3,2,1,0:T(8,128)S(1)}, f32[5,4,32,128]{3,2,1,0:T(8,128)S(1)}, u32[]{:S(2)}, u32[]{:S(2)}) collective-permute-start(f32[5,4,32,128]{3,2,1,0:T(8,128)S(1)} %get-tuple-element.26), channel_id=1, source_target_pairs={{1,0},{5,4},{7,6},{3,2},{8,1},{12,5},{14,7},{10,3},{9,8},{13,12},{... | collective-permute-start | bytes 983048 | tf_op jit(solution)/shard_map/ppermute | solution.py:268
  49.9 6.3 %collective-permute-start.9 = (f32[5,16,4,128]{3,2,1,0:T(4,128)S(1)}, f32[5,16,4,128]{3,2,1,0:T(4,128)S(1)}, u32[]{:S(2)}, u32[]{:S(2)}) collective-permute-start(f32[5,16,4,128]{3,2,1,0:T(4,128)S(1)} %pad_maximum_fusion.11), channel_id=1, source_target_pairs={{4,0},{6,4},{2,6},{0,2},{5,1},{7,5},{3,7},{1,3},{12,8},{14,12},{10... | collective-permute-start | bytes 491528 | tf_op jit(solution)/shard_map/ppermute | solution.py:274
  49.9 16.0 %collective-permute-start.12 = (f32[5,8,32,128]{3,2,1,0:T(8,128)S(1)}, f32[5,8,32,128]{3,2,1,0:T(8,128)S(1)}, u32[]{:S(2)}, u32[]{:S(2)}) collective-permute-start(f32[5,8,32,128]{3,2,1,0:T(8,128)S(1)} %get-tuple-element.28), channel_id=1, source_target_pairs={{1,0},{5,4},{7,6},{3,2},{8,1},{12,5},{14,7},{10,3},{9,8},{13,12},{... | collective-permute-start | bytes 1966088 | tf_op jit(solution)/shard_map/ppermute | solution.py:268
  56.3 9.7 %collective-permute-start.11 = (f32[5,12,8,128]{3,2,1,0:T(8,128)S(1)}, f32[5,12,8,128]{3,2,1,0:T(8,128)S(1)}, u32[]{:S(2)}, u32[]{:S(2)}) collective-permute-start(f32[5,12,8,128]{3,2,1,0:T(8,128)S(1)} %pad_maximum_fusion.3), channel_id=1, source_target_pairs={{1,0},{5,4},{7,6},{3,2},{8,1},{12,5},{14,7},{10,3},{9,8},{13,12},{... | collective-permute-start | bytes 737288 | tf_op jit(solution)/shard_map/ppermute | solution.py:268
  72.3 5.7 %collective-permute-start.13 = (f32[5,16,4,128]{3,2,1,0:T(4,128)S(1)}, f32[5,16,4,128]{3,2,1,0:T(4,128)S(1)}, u32[]{:S(2)}, u32[]{:S(2)}) collective-permute-start(f32[5,16,4,128]{3,2,1,0:T(4,128)S(1)} %pad_maximum_fusion.12), channel_id=1, source_target_pairs={{0,4},{4,6},{6,2},{2,0},{1,5},{5,7},{7,3},{3,1},{8,12},{12,14},{14... | collective-permute-start | bytes 491528 | tf_op jit(solution)/shard_map/ppermute | solution.py:273
  72.6 14.9 %collective-permute-start.15 = (f32[5,4,32,128]{3,2,1,0:T(8,128)S(1)}, f32[5,4,32,128]{3,2,1,0:T(8,128)S(1)}, u32[]{:S(2)}, u32[]{:S(2)}) collective-permute-start(f32[5,4,32,128]{3,2,1,0:T(8,128)S(1)} %get-tuple-element.30), channel_id=1, source_target_pairs={{1,0},{5,4},{7,6},{3,2},{8,1},{12,5},{14,7},{10,3},{9,8},{13,12},{... | collective-permute-start | bytes 983048 | tf_op jit(solution)/shard_map/ppermute | solution.py:268
  74.6 4.9 %collective-permute-start.14 = (f32[5,16,4,128]{3,2,1,0:T(4,128)S(1)}, f32[5,16,4,128]{3,2,1,0:T(4,128)S(1)}, u32[]{:S(2)}, u32[]{:S(2)}) collective-permute-start(f32[5,16,4,128]{3,2,1,0:T(4,128)S(1)} %pad_maximum_fusion.13), channel_id=1, source_target_pairs={{4,0},{6,4},{2,6},{0,2},{5,1},{7,5},{3,7},{1,3},{12,8},{14,12},{10... | collective-permute-start | bytes 491528 | tf_op jit(solution)/shard_map/ppermute | solution.py:274
  75.8 14.8 %collective-permute-start.17 = (f32[5,8,32,128]{3,2,1,0:T(8,128)S(1)}, f32[5,8,32,128]{3,2,1,0:T(8,128)S(1)}, u32[]{:S(2)}, u32[]{:S(2)}) collective-permute-start(f32[5,8,32,128]{3,2,1,0:T(8,128)S(1)} %get-tuple-element.32), channel_id=1, source_target_pairs={{1,0},{5,4},{7,6},{3,2},{8,1},{12,5},{14,7},{10,3},{9,8},{13,12},{... | collective-permute-start | bytes 1966088 | tf_op jit(solution)/shard_map/ppermute | solution.py:268
  79.5 11.1 %collective-permute-start.16 = (f32[5,12,8,128]{3,2,1,0:T(8,128)S(1)}, f32[5,12,8,128]{3,2,1,0:T(8,128)S(1)}, u32[]{:S(2)}, u32[]{:S(2)}) collective-permute-start(f32[5,12,8,128]{3,2,1,0:T(8,128)S(1)} %pad_maximum_fusion.5), channel_id=1, source_target_pairs={{1,0},{5,4},{7,6},{3,2},{8,1},{12,5},{14,7},{10,3},{9,8},{13,12},{... | collective-permute-start | bytes 737288 | tf_op jit(solution)/shard_map/ppermute | solution.py:268
  97.0 7.2 %collective-permute-start.18 = (f32[5,16,4,128]{3,2,1,0:T(4,128)S(1)}, f32[5,16,4,128]{3,2,1,0:T(4,128)S(1)}, u32[]{:S(2)}, u32[]{:S(2)}) collective-permute-start(f32[5,16,4,128]{3,2,1,0:T(4,128)S(1)} %pad_maximum_fusion.14), channel_id=1, source_target_pairs={{0,4},{4,6},{6,2},{2,0},{1,5},{5,7},{7,3},{3,1},{8,12},{12,14},{14... | collective-permute-start | bytes 491528 | tf_op jit(solution)/shard_map/ppermute | solution.py:273
  98.5 18.1 %collective-permute-start.21 = (f32[5,4,32,128]{3,2,1,0:T(8,128)S(1)}, f32[5,4,32,128]{3,2,1,0:T(8,128)S(1)}, u32[]{:S(2)}, u32[]{:S(2)}) collective-permute-start(f32[5,4,32,128]{3,2,1,0:T(8,128)S(1)} %get-tuple-element.34), channel_id=1, source_target_pairs={{1,0},{5,4},{7,6},{3,2},{8,1},{12,5},{14,7},{10,3},{9,8},{13,12},{... | collective-permute-start | bytes 983048 | tf_op jit(solution)/shard_map/ppermute | solution.py:268
  100.4 5.5 %collective-permute-start.19 = (f32[5,16,4,128]{3,2,1,0:T(4,128)S(1)}, f32[5,16,4,128]{3,2,1,0:T(4,128)S(1)}, u32[]{:S(2)}, u32[]{:S(2)}) collective-permute-start(f32[5,16,4,128]{3,2,1,0:T(4,128)S(1)} %pad_maximum_fusion.15), channel_id=1, source_target_pairs={{4,0},{6,4},{2,6},{0,2},{5,1},{7,5},{3,7},{1,3},{12,8},{14,12},{10... | collective-permute-start | bytes 491528 | tf_op jit(solution)/shard_map/ppermute | solution.py:274
  100.5 16.0 %collective-permute-start.23 = (f32[5,8,32,128]{3,2,1,0:T(8,128)S(1)}, f32[5,8,32,128]{3,2,1,0:T(8,128)S(1)}, u32[]{:S(2)}, u32[]{:S(2)}) collective-permute-start(f32[5,8,32,128]{3,2,1,0:T(8,128)S(1)} %get-tuple-element.37), channel_id=1, source_target_pairs={{1,0},{5,4},{7,6},{3,2},{8,1},{12,5},{14,7},{10,3},{9,8},{13,12},{... | collective-permute-start | bytes 1966088 | tf_op jit(solution)/shard_map/ppermute | solution.py:268
  106.0 10.5 %collective-permute-start.22 = (f32[5,12,8,128]{3,2,1,0:T(8,128)S(1)}, f32[5,12,8,128]{3,2,1,0:T(8,128)S(1)}, u32[]{:S(2)}, u32[]{:S(2)}) collective-permute-start(f32[5,12,8,128]{3,2,1,0:T(8,128)S(1)} %pad_maximum_fusion.7), channel_id=1, source_target_pairs={{1,0},{5,4},{7,6},{3,2},{8,1},{12,5},{14,7},{10,3},{9,8},{13,12},{... | collective-permute-start | bytes 737288 | tf_op jit(solution)/shard_map/ppermute | solution.py:268
  123.6 18.9 %collective-permute-start.25 = (f32[5,6,32,128]{3,2,1,0:T(8,128)S(1)}, f32[5,6,32,128]{3,2,1,0:T(8,128)S(1)}, u32[]{:S(2)}, u32[]{:S(2)}) collective-permute-start(f32[5,6,32,128]{3,2,1,0:T(8,128)S(1)} %part.17), channel_id=1, source_target_pairs={{0,0},{4,1},{6,2},{2,3},{1,4},{5,5},{7,6},{3,7},{8,8},{12,9},{14,1... | collective-permute-start | bytes 1474568 | tf_op jit(solution)/shard_map/ppermute | solution.py:268
  125.5 17.0 %collective-permute-start.24 = (f32[5,6,32,128]{3,2,1,0:T(8,128)S(1)}, f32[5,6,32,128]{3,2,1,0:T(8,128)S(1)}, u32[]{:S(2)}, u32[]{:S(2)}) collective-permute-start(f32[5,6,32,128]{3,2,1,0:T(8,128)S(1)} %get-tuple-element.38), channel_id=1, source_target_pairs={{0,0},{4,1},{6,2},{2,3},{1,4},{5,5},{7,6},{3,7},{8,8},{12,9},{14,1... | collective-permute-start | bytes 1474568 | tf_op jit(solution)/shard_map/ppermute | solution.py:268
  129.2 13.3 %collective-permute-start.20 = (f32[5,4,32,128]{3,2,1,0:T(8,128)S(1)}, f32[5,4,32,128]{3,2,1,0:T(8,128)S(1)}, u32[]{:S(2)}, u32[]{:S(2)}) collective-permute-start(f32[5,4,32,128]{3,2,1,0:T(8,128)S(1)} %get-tuple-element.35), channel_id=1, source_target_pairs={{0,0},{4,1},{6,2},{2,3},{1,4},{5,5},{7,6},{3,7},{8,8},{12,9},{14,1... | collective-permute-start | bytes 983048 | tf_op jit(solution)/shard_map/ppermute | solution.py:268
  (4 other events, 16.9 us)

commit v6 on v5

--- a/solution.py
+++ b/solution.py
@@ -14,7 +14,7 @@
 SENT = (0, 1, 2, 4, 5)
 PAD = 8
 DT = 0.04
-PLANES = 2
+PLANES = (2, 1)
 AXES = ("grow", "lat")
 GRAD, CENTER, COUPLE, LATENT, RELEASE, SPREAD, STAY, MELT = 0, 12, 16, 24, 28, 36, 38, 40
 
@@ -107,39 +107,32 @@
         else:
             tiles = [PAD + 8 * t for t in range(self.rows // 8)]
 
-        @pl.loop(0, (stop - first) // PLANES)
+        many = next(n for n in PLANES if (stop - first) % n == 0)
+
+        @pl.loop(0, (stop - first) // many)
         def _(i):
-            for p in range(PLANES):
-                e = first + PLANES * i + p
+            for p in range(many):
+                e = first + many * i + p
                 for at in tiles:
                     write(e, at, self.advance(src, e, at))
 
 
-def part_kernel(turn, place_of, sizes, begin, parts, has_seam, gives_seam, first_out, fresh, table, *refs):
+def part_kernel(turn, place_of, sizes, begin, parts, has_seam, gives_seam, out_from, fresh, table, *refs):
     refs, (even, odd) = list(refs[:-2]), refs[-2:]
     place = place_of()
     run = Round(turn, place, sizes, table, even, odd)
     end = begin
     seam = refs.pop(0) if has_seam else None
     index = refs.pop(0) if fresh else None
+    halo = refs.pop(0)
     for planes, halo_from in parts:
-        if halo_from == 0:
-            source, halo = refs.pop(0), refs.pop(0)
-        else:
-            source = refs.pop(0)
-        run.fill(source, halo, planes, end, halo_from)
+        run.fill(refs.pop(0), halo, planes, end, halo_from)
         end += planes
     next_seam = refs.pop() if gives_seam else None
-    outs = refs
+    outs = [(ref, o + STEPS, o + STEPS + ref.shape[1]) for ref, o in zip(refs, out_from)]
 
     def bounds(step):
         return (begin if has_seam else 2 * step) - step, end - step
-
-    for level in range(STEPS):
-        if has_seam:
-            for plane in range(2):
-                for f in range(6):
-                    run.levels[level][f, begin - level - 2 + plane] = seam[level, f, plane]
 
     def hold(level):
         if gives_seam:
@@ -147,23 +140,28 @@
                 for f in range(6):
                     next_seam[level, f, plane] = run.levels[level][f, end - level - 2 + plane]
 
-    def write(targets):
+    def write(first, stop):
+        targets = [(ref, at) for ref, at, until in outs if at <= first and stop <= until]
+
         def put(e, at, new):
-            for ref in targets:
+            for ref, origin in targets:
                 for i, f in enumerate(SENT):
-                    ref[i, e - STEPS - first_out, pl.ds(at - PAD, 8)] = new[f]
+                    ref[i, e - origin, pl.ds(at - PAD, 8)] = new[f]
 
         return put
 
+    if has_seam:
+        for level in range(STEPS):
+            for plane in range(2):
+                for f in range(6):
+                    run.levels[level][f, begin - level - 2 + plane] = seam[level, f, plane]
     hold(0)
     for step in range(1, STEPS):
         run.sweep(step, *bounds(step))
         hold(step)
-    first, last = bounds(STEPS)
-    ends = [first_out + STEPS + ref.shape[1] for ref in outs]
-    marks = sorted(set([first, last] + [m for m in ends if first < m < last]))
-    for low, high in zip(marks, marks[1:]):
-        run.sweep(STEPS, low, high, write([ref for ref, m in zip(outs, ends) if m >= high]))
+    marks = sorted(set(bounds(STEPS)) | set(m for _, *ends in outs for m in ends))
+    for first, stop in zip(marks, marks[1:]):
+        run.sweep(STEPS, first, stop, write(first, stop))
 
     if fresh:
 
@@ -171,9 +169,9 @@
         def _():
             for j in range(SHIFT):
                 e = run.block - SHIFT + j + STEPS
-                put = write([ref for ref, m in zip(outs, ends) if m > e])
-                for t in range(run.rows // 8):
-                    put(e, PAD + 8 * t, melt(table, index[j, pl.ds(8 * t, 8)]))
+                if any(at <= e < until for _, at, until in outs):
+                    for t in range(run.rows // 8):
+                        write(e, e + 1)(e, PAD + 8 * t, melt(table, index[j, pl.ds(8 * t, 8)]))
 
 
 def melt(table, row):
@@ -212,30 +210,23 @@
                 put(at - SHIFT + j, here, melt(table, index[j, here]))
 
 
-def prepare_kernel(labels, roughness, potential, low, high, staying):
-    lows, highs = low.shape[1], high.shape[1]
-
-    def plane(o, kept):
-        kind = labels[o]
-        rough = [roughness[a, o] for a in range(4)]
-        inverse = 1.0 / (3.0 + rough[0] + rough[1] + rough[2] + rough[3])
-        new = [(jnp.where(kind == a, 3.0, 0.0) + rough[a]) * inverse for a in range(3)]
-        new += [potential[0, o], potential[1, o]]
-        for ref, at in kept:
-            for f, value in enumerate(new):
-                ref[f, at] = value
-
-    @pl.loop(0, lows)
-    def _(o):
-        plane(o, [(low, o)])
-
-    @pl.loop(lows, lows + highs)
-    def _(o):
-        plane(o, [(high, o - lows), (staying, o - lows)])
-
-    @pl.loop(lows + highs, labels.shape[0])
-    def _(o):
-        plane(o, [(staying, o - lows)])
+def prepare_kernel(labels, roughness, potential, *outs):
+    starts = (0, outs[0].shape[1], labels.shape[0] - outs[2].shape[1])
+    ranges = [(ref, at, at + ref.shape[1]) for ref, at in zip(outs, starts)]
+    marks = sorted(set(m for _, *ends in ranges for m in ends))
+    for first, stop in zip(marks, marks[1:]):
+        targets = [(ref, at) for ref, at, until in ranges if at <= first and stop <= until]
+
+        @pl.loop(first, stop)
+        def _(o, targets=targets):
+            kind = labels[o]
+            rough = [roughness[a, o] for a in range(4)]
+            inverse = 1.0 / (3.0 + rough[0] + rough[1] + rough[2] + rough[3])
+            new = [(jnp.where(kind == a, 3.0, 0.0) + rough[a]) * inverse for a in range(3)]
+            new += [potential[0, o], potential[1, o]]
+            for ref, at in targets:
+                for f, value in enumerate(new):
+                    ref[f, o - at] = value
 
 
 def on_device(ng, nl, labels, roughness, potential, grad_coef, composition, latent, diffusivity, melt_table, melt_index):
@@ -283,84 +274,129 @@
     seam_shape = jax.ShapeDtypeStruct((STEPS, 6, 2, rows + 2 * PAD, lanes), f32)
     scratch = [pltpu.VMEM((6, height, rows + 2 * PAD, lanes), f32)] * 2
 
-    def part(turn, begin, planes, has_seam, gives_seam, first_out, sent, *args, fresh=False):
+    def limit(size):
+        return pltpu.CompilerParams(vmem_limit_bytes=size << 20)
+
+    def part(turn, begin, planes, has_seam, gives_seam, sent, fresh, *args):
         size = sum(n for n, _ in planes)
         return pl.pallas_call(
             functools.partial(
-                part_kernel, turn, away_place, (ng, block, rows), begin, planes, has_seam, gives_seam, first_out, fresh
+                part_kernel,
+                turn,
+                away_place,
+                (ng, block, rows),
+                begin,
+                planes,
+                has_seam,
+                gives_seam,
+                [o for o, _ in sent],
+                fresh,
             ),
-            out_shape=[piece(n) for n in sent] + [seam_shape] * gives_seam,
+            out_shape=[piece(n) for _, n in sent] + [seam_shape] * gives_seam,
             in_specs=[smem] + [vmem] * len(args),
             out_specs=[vmem] * (len(sent) + gives_seam),
             scratch_shapes=scratch,
-            compiler_params=pltpu.CompilerParams(vmem_limit_bytes=40 << 20),
+            compiler_params=limit(24),
             cost_estimate=cost(4 * size, 4000000),
             name="part",
         )(table, *args)
 
-    low, high, staying = pl.pallas_call(
+    front, back, own = pl.pallas_call(
         prepare_kernel,
-        out_shape=[piece(n) for n in (lows, highs, kept)],
+        out_shape=[piece(n) for n in (highs, lows, kept)],
         in_specs=[vmem] * 3,
         out_specs=[vmem] * 3,
+        compiler_params=limit(8),
         name="prepare",
     )(labels, roughness, potential)
 
+    def packed(left, right, first, stop):
+        return jnp.concatenate([left[:, first:stop], right[:, first:stop]], axis=2)
+
+    own_parts = [(kept, 0)]
+    left, right = beside([front[:, :lows], own], home)
+    own = [moved(own, home, away, 0)]
+    own_halo = moved(packed(left, right, lows, block), home, away, 0)
+    front = moved(front, home, away, 1)
+    halo = moved(packed(left, right, 0, lows + highs), home, away, 1)
+    back = moved(back, home, away, 1)
     away_index = lax.ppermute(
-        melt_index[: ROUNDS - 1],
-        AXES,
-        [(home(ng - 1, l), away(ng - 1, l)) for l in range(nl)],
-    )
-
-    early = low
-    for turn in range(ROUNDS):
+        melt_index[: ROUNDS - 1], AXES, [(home(ng - 1, l), away(ng - 1, l)) for l in range(nl)]
+    )
+    early, seam = part(0, 0, own_parts, False, True, [(0, lows)], False, own_halo, *own)
+    low = moved(early, away, away, 1)
+    high, seam = part(
+        0, kept, [(highs, 0)], True, True, [(lows, highs)], True, seam, away_index[0], halo, front
+    )
+    above = moved(high, away, away, 1)
+    (rest,) = part(
+        0,
+        kept + highs,
+        [(lows, highs)],
+        True,
+        False,
+        [(lows + highs, lows)],
+        True,
+        seam,
+        away_index[0],
+        halo,
+        back,
+    )
+
+    own_parts = [(highs, 0), (lows, highs)]
+    for turn in range(1, ROUNDS):
         last = turn == ROUNDS - 1
-        before = home if turn == 0 else away
-        left, right = beside([early, staying], before)
-        own_halo = jnp.concatenate([left[:, lows:], right[:, lows:]], axis=2)
-        halo = jnp.concatenate([left[:, : lows + highs], right[:, : lows + highs]], axis=2)
-        if turn == 0:
-            staying = moved(staying, before, away, 0)
-            own_halo = moved(own_halo, before, away, 0)
-            low = moved(low, before, away, 1)
-        high = moved(high, before, away, 1)
-        halo = moved(halo, before, away, 1)
-        early, seam = part(turn, 0, [(kept, 0)], False, True, 0, [lows], staying, own_halo)
-        next_low = moved(early, away, home if last else away, 0 if last else 1)
+        left, right = beside([early, high, rest], away)
+        own, own_halo = [high, rest], packed(left, right, lows, block)
+        if turn > 1:
+            above = moved(high, away, away, 1)
+        halo = moved(packed(left, right, 0, lows + highs), away, away, 1)
+        early, seam = part(turn, 0, own_parts, False, True, [(0, lows)], False, own_halo, *own)
+        sent = moved(early, away, home if last else away, 0 if last else 1)
         if last:
             break
-        staying, high = functools.partial(part, fresh=True)(
+        high, rest = part(
             turn,
             kept,
             [(lows, 0), (highs, lows)],
             True,
             False,
-            lows,
-            [kept, highs],
+            [(lows, highs), (lows + highs, lows)],
+            True,
             seam,
             away_index[turn],
+            halo,
             low,
-            halo,
-            high,
+            above,
         )
-        low = next_low
+        low = sent
 
     cut = 2
     middle, seam = part(
-        turn, kept, [(lows, 0), (cut, lows)], True, True, lows, [lows + cut], seam, low, halo, high[:, :cut]
+        turn,
+        kept,
+        [(lows, 0), (cut, lows)],
+        True,
+        True,
+        [(lows, lows + cut)],
+        False,
+        seam,
+        halo,
+        low,
+        above[:, :cut],
     )
     middle = moved(middle, away, home, 0)
     (final,) = part(
         turn,
         kept + lows + cut,
-        [(highs - cut, 0)],
+        [(highs - cut, lows + cut)],
         True,
         False,
-        2 * lows + cut,
-        [highs - cut],
+        [(2 * lows + cut, highs - cut)],
+        False,
         seam,
-        high[:, cut:],
-        halo[:, lows + cut :],
+        halo,
+        above[:, cut:],
     )
     final = moved(final, away, home, 0)
     return pl.pallas_call(
@@ -368,8 +404,9 @@
         out_shape=[jax.ShapeDtypeStruct((n, block, rows, lanes), f32) for n in (4, 2)],
         in_specs=[smem] + [vmem] * 4,
         out_specs=[vmem] * 2,
+        compiler_params=limit(8),
         name="finish",
-    )(table, melt_index[turn], next_low, middle, final)
+    )(table, melt_index[turn], sent, middle, final)
 
 
 def solution(mesh):

time: 148 us -> 147 us (level)
  Pallas kernels: 47.4 us -> 44.6 us
  waiting for transfers between devices: 32.5 us -> 34.6 us
  starting transfers between devices: 54.7 us -> 52.8 us
    ppermute x4, waiting for transfers between devices: 7.22 us -> 16.9 us  [beside(): lax.ppermute(first, AXES, [(where(g, (l + 1) % nl), where(g, l)) for g, l...]
    ppermute x17, waiting for transfers between devices: 25.1 us -> 17.6 us  [moved(): return lax.ppermute(array, AXES, route)]
    ppermute x4, starting transfers between devices: 8.21 us -> 5.14 us  [beside(): lax.ppermute(final, AXES, [(where(g, l), where(g, (l + 1) % nl)) for g, l...]
    pallas_call x1, Pallas kernels: 3.03 us -> 0.26 us  [on_device(): pl.pallas_call(prepare_kernel, out_shape=[piece(n) for n in (highs, lows,...]
    unnamed x21, local copies, waits for them, and re-layouts: 1.82 us -> 4.03 us
    slice x8 -> x11, local copies, waits for them, and re-layouts: 2.25 us -> 0.26 us  [beside(): final = jnp.concatenate([p[:, :, rows - STEPS:] for p in parts], axis=1)]
    ppermute x4, starting transfers between devices: 1.5 us -> 3.23 us  [beside(): lax.ppermute(first, AXES, [(where(g, (l + 1) % nl), where(g, l)) for g, l...]
    pallas_call x9 -> x10, Pallas kernels: 41.8 us -> 42.5 us  [part(): pl.pallas_call(functools.partial(part_kernel, turn, away_place, (ng, bloc...]
  transfers between devices with their start and end apart: 26 -> 26, of which waited for: 9 -> 8; matrix products, arithmetic and copies ran while one was open for 6% -> 5% of each run, Pallas kernels for 11% -> 14%
where the time goes in v6:
time: 147 us; the launch traced here: 146 us
  starting transfers between devices  52.8 us (36%)
  Pallas kernels  44.6 us (30%)
  waiting for transfers between devices  34.6 us (24%)
  local copies, waits for them, and re-layouts  9.08 us (6%)
  other arithmetic  3.01 us (2%)
  between operations  1.83 us (1%)
    ppermute x17, starting transfers between devices, moved(): return lax.ppermute(array, AXES, route)  43 us
    pallas_call x10, Pallas kernels, part(): pl.pallas_call(functools.partial(part_kernel, turn, away_place, (ng, bloc...  42.5 us
    ppermute x17, waiting for transfers between devices, moved(): return lax.ppermute(array, AXES, route)  17.6 us
    ppermute x4, waiting for transfers between devices, beside(): lax.ppermute(first, AXES, [(where(g, (l + 1) % nl), where(g, l)) for g, l...  16.9 us
    ppermute x4, starting transfers between devices, beside(): lax.ppermute(final, AXES, [(where(g, l), where(g, (l + 1) % nl)) for g, l...  5.14 us
    unnamed x21, local copies, waits for them, and re-layouts  4.03 us
    ppermute x4, starting transfers between devices, beside(): lax.ppermute(first, AXES, [(where(g, (l + 1) % nl), where(g, l)) for g, l...  3.23 us
  transfers between devices with their start and end apart: 26, of which 8 were waited for; matrix products, arithmetic and copies ran while one was open for 5% of the time, Pallas kernels for 14%

profile of v6, /device:TPU:17, one launch (start us, length us, event | category | flops | bytes accessed | tf_op | source)
XLA Modules:
  0.0 145.9 jit_solution(10519562970497292391)
XLA Ops:
  4.9 3.8 %collective-permute-start.3 = (f32[5,12,32,128]{3,2,1,0:T(8,128)S(1)}, f32[5,12,32,128]{3,2,1,0:T(8,128)S(1)}, u32[]{:S(2)}, u32[]{:S(2)}) collective-permute-start(f32[5,12,32,128]{3,2,1,0:T(8,128)S(1)} %get-tuple-element.22), channel_id=1, source_target_pairs={{0,0},{1,4},{2,6},{3,2},{4,1},{5,5},{6,7},{7,3},{8,8},{9,12},{10,1... | collective-permute-start | bytes 2949128 | tf_op jit(solution)/shard_map/ppermute | solution.py:259
  8.7 1.9 %collective-permute-start.6 = (f32[5,8,32,128]{3,2,1,0:T(8,128)S(1)}, f32[5,8,32,128]{3,2,1,0:T(8,128)S(1)}, u32[]{:S(2)}, u32[]{:S(2)}) collective-permute-start(f32[5,8,32,128]{3,2,1,0:T(8,128)S(1)} %get-tuple-element.21), channel_id=1, source_target_pairs={{4,0},{5,4},{6,6},{7,2},{8,1},{9,5},{10,7},{11,3},{12,8},{13,12},{... | collective-permute-start | bytes 1966088 | tf_op jit(solution)/shard_map/ppermute | solution.py:259
  18.3 1.9 %collective-permute-start.7 = (f32[5,4,32,128]{3,2,1,0:T(8,128)}, f32[5,4,32,128]{3,2,1,0:T(8,128)S(1)}, u32[]{:S(2)}, u32[]{:S(2)}) collective-permute-start(f32[5,4,32,128]{3,2,1,0:T(8,128)} %copy-done.3), channel_id=1, source_target_pairs={{4,0},{5,4},{6,6},{7,2},{8,1},{9,5},{10,7},{11,3},{12,8},{13,12},{... | collective-permute-start | bytes 983048 | tf_op jit(solution)/shard_map/ppermute | solution.py:259
  21.3 4.3 %collective-permute-start.2 = (f32[5,12,8,128]{3,2,1,0:T(8,128)S(1)}, f32[5,12,8,128]{3,2,1,0:T(8,128)S(1)}, u32[]{:S(2)}, u32[]{:S(2)}) collective-permute-start(f32[5,12,8,128]{3,2,1,0:T(8,128)S(1)} %pad_maximum_fusion), channel_id=1, source_target_pairs={{0,0},{1,4},{2,6},{3,2},{4,1},{5,5},{6,7},{7,3},{8,8},{9,12},{10,1... | collective-permute-start | bytes 737288 | tf_op jit(solution)/shard_map/ppermute | solution.py:259
  25.7 1.9 %collective-permute-start.5 = (f32[5,12,8,128]{3,2,1,0:T(8,128)S(1)}, f32[5,12,8,128]{3,2,1,0:T(8,128)S(1)}, u32[]{:S(2)}, u32[]{:S(2)}) collective-permute-start(f32[5,12,8,128]{3,2,1,0:T(8,128)S(1)} %pad_maximum_fusion.1), channel_id=1, source_target_pairs={{4,0},{5,4},{6,6},{7,2},{8,1},{9,5},{10,7},{11,3},{12,8},{13,12},{... | collective-permute-start | bytes 737288 | tf_op jit(solution)/shard_map/ppermute | solution.py:259
  28.7 5.0 %collective-permute-done.2.refs_0_ = f32[5,12,8,128]{3,2,1,0:T(8,128)S(1)} collective-permute-done((f32[5,12,8,128]{3,2,1,0:T(8,128)S(1)}, f32[5,12,8,128]{3,2,1,0:T(8,128)S(1)}, u32[]{:S(2)}, u32[]{:S(2)}) %collective-permute-start.2) | collective-permute-done | bytes 245792 | tf_op jit(solution)/shard_map/ppermute | solution.py:259
  33.7 4.0 %part.10 = (f32[5,4,32,128]{3,2,1,0:T(8,128)S(1)}, f32[4,6,2,48,128]{4,3,2,1,0:T(8,128)S(1)}) custom-call(f32[72]{0:T(128)S(1)} %concatenate.51.table, f32[5,12,8,128]{3,2,1,0:T(8,128)S(1)} %collective-permute-done.2.refs_0_, f32[5,12,32,128]{3,2,1,0:T(8,128)S(1)} %collective-permute-done.3.refs_1_), custom_call_target="tpu_custom_call" | custom-call | flops 153354240 | bytes 4000000 | tf_op jit(solution)/shard_map/part/pallas_call | solution.py:282
  37.7 4.5 %part.11 = (f32[5,8,32,128]{3,2,1,0:T(8,128)S(1)}, f32[4,6,2,48,128]{4,3,2,1,0:T(8,128)S(1)}) custom-call(f32[72]{0:T(128)S(1)} %concatenate.51.table, f32[4,6,2,48,128]{4,3,2,1,0:T(8,128)S(1)} %get-tuple-element.24.refs_0_, s32[8,32,128]{2,1,0:T(8,128)S(1)} %get-tuple-element.52.refs_1_, f32[5,12,8,128]{3,2,1,0:T(8,128)S(1)} %collective-permute-done.5.refs_2_, ...), custom_call_target="tpu_custom_call" | custom-call | flops 102236160 | bytes 4000000 | tf_op jit(solution)/shard_map/part/pallas_call | solution.py:282
  42.2 2.5 %part.12.refs_2_ = f32[5,4,32,128]{3,2,1,0:T(8,128)S(1)} custom-call(f32[72]{0:T(128)S(1)} %concatenate.51.table, f32[4,6,2,48,128]{4,3,2,1,0:T(8,128)S(1)} %get-tuple-element.26.refs_0_, s32[8,32,128]{2,1,0:T(8,128)S(1)} %get-tuple-element.52.refs_1_, f32[5,12,8,128]{3,2,1,0:T(8,128)S(1)} %collective-permute-done.5.refs_2_, ...), custom_call_target="tpu_custom_call" | custom-call | flops 51118080 | bytes 4000000 | tf_op jit(solution)/shard_map/part/pallas_call | solution.py:282
  44.8 2.2 %collective-permute-start.8 = (f32[5,16,4,128]{3,2,1,0:T(4,128)S(1)}, f32[5,16,4,128]{3,2,1,0:T(4,128)S(1)}, u32[]{:S(2)}, u32[]{:S(2)}) collective-permute-start(f32[5,16,4,128]{3,2,1,0:T(4,128)S(1)} %pad_maximum_fusion.10), channel_id=1, source_target_pairs={{0,4},{4,6},{6,2},{2,0},{1,5},{5,7},{7,3},{3,1},{8,12},{12,14},{14... | collective-permute-start | bytes 491528 | tf_op jit(solution)/shard_map/ppermute | solution.py:264
  47.0 1.9 %collective-permute-start.12 = (f32[5,8,32,128]{3,2,1,0:T(8,128)S(1)}, f32[5,8,32,128]{3,2,1,0:T(8,128)S(1)}, u32[]{:S(2)}, u32[]{:S(2)}) collective-permute-start(f32[5,8,32,128]{3,2,1,0:T(8,128)S(1)} %get-tuple-element.25.refs_1_), channel_id=1, source_target_pairs={{1,0},{5,4},{7,6},{3,2},{8,1},{12,5},{14,7},{10,3},{9,8},{13,12},{... | collective-permute-start | bytes 1966088 | tf_op jit(solution)/shard_map/ppermute | solution.py:259
  48.9 2.3 %collective-permute-start.11 = (f32[5,4,32,128]{3,2,1,0:T(8,128)S(1)}, f32[5,4,32,128]{3,2,1,0:T(8,128)S(1)}, u32[]{:S(2)}, u32[]{:S(2)}) collective-permute-start(f32[5,4,32,128]{3,2,1,0:T(8,128)S(1)} %get-tuple-element.23), channel_id=1, source_target_pairs={{1,0},{5,4},{7,6},{3,2},{8,1},{12,5},{14,7},{10,3},{9,8},{13,12},{... | collective-permute-start | bytes 983048 | tf_op jit(solution)/shard_map/ppermute | solution.py:259
  53.0 7.0 %collective-permute-done.9 = f32[5,16,4,128]{3,2,1,0:T(4,128)S(1)} collective-permute-done((f32[5,16,4,128]{3,2,1,0:T(4,128)S(1)}, f32[5,16,4,128]{3,2,1,0:T(4,128)S(1)}, u32[]{:S(2)}, u32[]{:S(2)}) %collective-permute-start.9) | collective-permute-done | bytes 163872 | tf_op jit(solution)/shard_map/ppermute | solution.py:265
  60.0 2.5 %collective-permute-start.10 = (f32[5,12,8,128]{3,2,1,0:T(8,128)S(1)}, f32[5,12,8,128]{3,2,1,0:T(8,128)S(1)}, u32[]{:S(2)}, u32[]{:S(2)}) collective-permute-start(f32[5,12,8,128]{3,2,1,0:T(8,128)S(1)} %pad_maximum_fusion.3), channel_id=1, source_target_pairs={{1,0},{5,4},{7,6},{3,2},{8,1},{12,5},{14,7},{10,3},{9,8},{13,12},{... | collective-permute-start | bytes 737288 | tf_op jit(solution)/shard_map/ppermute | solution.py:259
  62.6 4.0 %part.13 = (f32[5,4,32,128]{3,2,1,0:T(8,128)S(1)}, f32[4,6,2,48,128]{4,3,2,1,0:T(8,128)S(1)}) custom-call(f32[72]{0:T(128)S(1)} %concatenate.51.table, f32[5,12,8,128]{3,2,1,0:T(8,128)S(1)} %pad_maximum_fusion.2.refs_0_, f32[5,8,32,128]{3,2,1,0:T(8,128)S(1)} %get-tuple-element.25.refs_1_, f32[5,4,32,128]{3,2,1,0:T(8,128)S(1)} %part.12.refs_2_), custom_call_target="tpu_custom_call" | custom-call | flops 153354240 | bytes 4000000 | tf_op jit(solution)/shard_map/part/pallas_call | solution.py:282
  67.5 6.2 %part.14 = (f32[5,8,32,128]{3,2,1,0:T(8,128)S(1)}, f32[5,4,32,128]{3,2,1,0:T(8,128)S(1)}) custom-call(f32[72]{0:T(128)S(1)} %concatenate.51.table, f32[4,6,2,48,128]{4,3,2,1,0:T(8,128)S(1)} %get-tuple-element.29.refs_0_, s32[8,32,128]{2,1,0:T(8,128)S(1)} %get-tuple-element.51.refs_1_, f32[5,12,8,128]{3,2,1,0:T(8,128)S(1)} %collective-permute-done.10.refs_2_, ...), custom_call_target="tpu_custom_call" | custom-call | flops 153354240 | bytes 4000000 | tf_op jit(solution)/shard_map/part/pallas_call | solution.py:282
  75.1 1.9 %collective-permute-start.16 = (f32[5,4,32,128]{3,2,1,0:T(8,128)S(1)}, f32[5,4,32,128]{3,2,1,0:T(8,128)S(1)}, u32[]{:S(2)}, u32[]{:S(2)}) collective-permute-start(f32[5,4,32,128]{3,2,1,0:T(8,128)S(1)} %get-tuple-element.28), channel_id=1, source_target_pairs={{1,0},{5,4},{7,6},{3,2},{8,1},{12,5},{14,7},{10,3},{9,8},{13,12},{... | collective-permute-start | bytes 983048 | tf_op jit(solution)/shard_map/ppermute | solution.py:259
  77.0 2.8 %collective-permute-start.17 = (f32[5,8,32,128]{3,2,1,0:T(8,128)S(1)}, f32[5,8,32,128]{3,2,1,0:T(8,128)S(1)}, u32[]{:S(2)}, u32[]{:S(2)}) collective-permute-start(f32[5,8,32,128]{3,2,1,0:T(8,128)S(1)} %get-tuple-element.30.refs_1_), channel_id=1, source_target_pairs={{1,0},{5,4},{7,6},{3,2},{8,1},{12,5},{14,7},{10,3},{9,8},{13,12},{... | collective-permute-start | bytes 1966088 | tf_op jit(solution)/shard_map/ppermute | solution.py:259
  80.0 5.7 %collective-permute-done.14 = f32[5,16,4,128]{3,2,1,0:T(4,128)S(1)} collective-permute-done((f32[5,16,4,128]{3,2,1,0:T(4,128)S(1)}, f32[5,16,4,128]{3,2,1,0:T(4,128)S(1)}, u32[]{:S(2)}, u32[]{:S(2)}) %collective-permute-start.14) | collective-permute-done | bytes 163872 | tf_op jit(solution)/shard_map/ppermute | solution.py:265
  85.8 2.8 %collective-permute-start.15 = (f32[5,12,8,128]{3,2,1,0:T(8,128)S(1)}, f32[5,12,8,128]{3,2,1,0:T(8,128)S(1)}, u32[]{:S(2)}, u32[]{:S(2)}) collective-permute-start(f32[5,12,8,128]{3,2,1,0:T(8,128)S(1)} %pad_maximum_fusion.5), channel_id=1, source_target_pairs={{1,0},{5,4},{7,6},{3,2},{8,1},{12,5},{14,7},{10,3},{9,8},{13,12},{... | collective-permute-start | bytes 737288 | tf_op jit(solution)/shard_map/ppermute | solution.py:259
  88.6 4.0 %part.15 = (f32[5,4,32,128]{3,2,1,0:T(8,128)S(1)}, f32[4,6,2,48,128]{4,3,2,1,0:T(8,128)S(1)}) custom-call(f32[72]{0:T(128)S(1)} %concatenate.51.table, f32[5,12,8,128]{3,2,1,0:T(8,128)S(1)} %pad_maximum_fusion.4.refs_0_, f32[5,8,32,128]{3,2,1,0:T(8,128)S(1)} %get-tuple-element.30.refs_1_, f32[5,4,32,128]{3,2,1,0:T(8,128)S(1)} %get-tuple-element.31.refs_2_), custom_call_target="tpu_custom_call" | custom-call | flops 153354240 | bytes 4000000 | tf_op jit(solution)/shard_map/part/pallas_call | solution.py:282
  93.3 6.2 %part.16 = (f32[5,8,32,128]{3,2,1,0:T(8,128)S(1)}, f32[5,4,32,128]{3,2,1,0:T(8,128)S(1)}) custom-call(f32[72]{0:T(128)S(1)} %concatenate.51.table, f32[4,6,2,48,128]{4,3,2,1,0:T(8,128)S(1)} %get-tuple-element.33.refs_0_, s32[8,32,128]{2,1,0:T(8,128)S(1)} %get-tuple-element.50.refs_1_, f32[5,12,8,128]{3,2,1,0:T(8,128)S(1)} %collective-permute-done.15.refs_2_, ...), custom_call_target="tpu_custom_call" | custom-call | flops 153354240 | bytes 4000000 | tf_op jit(solution)/shard_map/part/pallas_call | solution.py:282
  101.9 2.7 %collective-permute-start.23 = (f32[5,8,32,128]{3,2,1,0:T(8,128)S(1)}, f32[5,8,32,128]{3,2,1,0:T(8,128)S(1)}, u32[]{:S(2)}, u32[]{:S(2)}) collective-permute-start(f32[5,8,32,128]{3,2,1,0:T(8,128)S(1)} %get-tuple-element.34.refs_1_), channel_id=1, source_target_pairs={{1,0},{5,4},{7,6},{3,2},{8,1},{12,5},{14,7},{10,3},{9,8},{13,12},{... | collective-permute-start | bytes 1966088 | tf_op jit(solution)/shard_map/ppermute | solution.py:259
  106.2 4.3 %collective-permute-done.19 = f32[5,16,4,128]{3,2,1,0:T(4,128)S(1)} collective-permute-done((f32[5,16,4,128]{3,2,1,0:T(4,128)S(1)}, f32[5,16,4,128]{3,2,1,0:T(4,128)S(1)}, u32[]{:S(2)}, u32[]{:S(2)}) %collective-permute-start.19) | collective-permute-done | bytes 163872 | tf_op jit(solution)/shard_map/ppermute | solution.py:265
  110.6 2.8 %collective-permute-start.21 = (f32[5,12,8,128]{3,2,1,0:T(8,128)S(1)}, f32[5,12,8,128]{3,2,1,0:T(8,128)S(1)}, u32[]{:S(2)}, u32[]{:S(2)}) collective-permute-start(f32[5,12,8,128]{3,2,1,0:T(8,128)S(1)} %pad_maximum_fusion.7), channel_id=1, source_target_pairs={{1,0},{5,4},{7,6},{3,2},{8,1},{12,5},{14,7},{10,3},{9,8},{13,12},{... | collective-permute-start | bytes 737288 | tf_op jit(solution)/shard_map/ppermute | solution.py:259
  113.4 4.0 %part.17 = (f32[5,4,32,128]{3,2,1,0:T(8,128)S(1)}, f32[4,6,2,48,128]{4,3,2,1,0:T(8,128)S(1)}) custom-call(f32[72]{0:T(128)S(1)} %concatenate.51.table, f32[5,12,8,128]{3,2,1,0:T(8,128)S(1)} %pad_maximum_fusion.6.refs_0_, f32[5,8,32,128]{3,2,1,0:T(8,128)S(1)} %get-tuple-element.34.refs_1_, f32[5,4,32,128]{3,2,1,0:T(8,128)S(1)} %get-tuple-element.35.refs_2_), custom_call_target="tpu_custom_call" | custom-call | flops 153354240 | bytes 4000000 | tf_op jit(solution)/shard_map/part/pallas_call | solution.py:282
  118.1 3.5 %part.18 = (f32[5,6,32,128]{3,2,1,0:T(8,128)S(1)}, f32[4,6,2,48,128]{4,3,2,1,0:T(8,128)S(1)}) custom-call(f32[72]{0:T(128)S(1)} %concatenate.51.table, f32[4,6,2,48,128]{4,3,2,1,0:T(8,128)S(1)} %get-tuple-element.37.refs_0_, f32[5,12,8,128]{3,2,1,0:T(8,128)S(1)} %collective-permute-done.21.refs_1_, f32[5,4,32,128]{3,2,1,0:T(8,128)S(1)} %collective-permute-done.22.refs_2_, ...), custom_call_target="tpu_custom_call" | custom-call | flops 76677120 | bytes 4000000 | tf_op jit(solution)/shard_map/part/pallas_call | solution.py:282
  121.7 3.4 %part.19 = f32[5,6,32,128]{3,2,1,0:T(8,128)S(1)} custom-call(f32[72]{0:T(128)S(1)} %concatenate.51.table, f32[4,6,2,48,128]{4,3,2,1,0:T(8,128)S(1)} %get-tuple-element.39.refs_0_, f32[5,12,8,128]{3,2,1,0:T(8,128)S(1)} %collective-permute-done.21.refs_1_, f32[5,6,32,128]{3,2,1,0:T(8,128)S(1)} %slice.210.refs_2_), custom_call_target="tpu_custom_call" | custom-call | flops 76677120 | bytes 4000000 | tf_op jit(solution)/shard_map/part/pallas_call | solution.py:282
  125.1 1.9 %collective-permute-start.25 = (f32[5,6,32,128]{3,2,1,0:T(8,128)S(1)}, f32[5,6,32,128]{3,2,1,0:T(8,128)S(1)}, u32[]{:S(2)}, u32[]{:S(2)}) collective-permute-start(f32[5,6,32,128]{3,2,1,0:T(8,128)S(1)} %part.19), channel_id=1, source_target_pairs={{0,0},{4,1},{6,2},{2,3},{1,4},{5,5},{7,6},{3,7},{8,8},{12,9},{14,1... | collective-permute-start | bytes 1474568 | tf_op jit(solution)/shard_map/ppermute | solution.py:259
  127.1 3.6 %collective-permute-start.24 = (f32[5,6,32,128]{3,2,1,0:T(8,128)S(1)}, f32[5,6,32,128]{3,2,1,0:T(8,128)S(1)}, u32[]{:S(2)}, u32[]{:S(2)}) collective-permute-start(f32[5,6,32,128]{3,2,1,0:T(8,128)S(1)} %get-tuple-element.38), channel_id=1, source_target_pairs={{0,0},{4,1},{6,2},{2,3},{1,4},{5,5},{7,6},{3,7},{8,8},{12,9},{14,1... | collective-permute-start | bytes 1474568 | tf_op jit(solution)/shard_map/ppermute | solution.py:259
  130.7 1.9 %collective-permute-start.20 = (f32[5,4,32,128]{3,2,1,0:T(8,128)S(1)}, f32[5,4,32,128]{3,2,1,0:T(8,128)S(1)}, u32[]{:S(2)}, u32[]{:S(2)}) collective-permute-start(f32[5,4,32,128]{3,2,1,0:T(8,128)S(1)} %get-tuple-element.36), channel_id=1, source_target_pairs={{0,0},{4,1},{6,2},{2,3},{1,4},{5,5},{7,6},{3,7},{8,8},{12,9},{14,1... | collective-permute-start | bytes 983048 | tf_op jit(solution)/shard_map/ppermute | solution.py:259
  133.6 10.5 %collective-permute-done.20.refs_0_ = f32[5,4,32,128]{3,2,1,0:T(8,128)S(1)} collective-permute-done((f32[5,4,32,128]{3,2,1,0:T(8,128)S(1)}, f32[5,4,32,128]{3,2,1,0:T(8,128)S(1)}, u32[]{:S(2)}, u32[]{:S(2)}) %collective-permute-start.20) | collective-permute-done | bytes 327712 | tf_op jit(solution)/shard_map/ppermute | solution.py:259
  (108 shorter events, 25.9 us)
Async XLA Ops:
  3.8 9.8 %copy-start.4 = (s32[4,8,32,128]{3,2,1,0:T(8,128)S(1)}, s32[4,8,32,128]{3,2,1,0:T(8,128)}, u32[]{:S(2)}) copy-start(s32[4,8,32,128]{3,2,1,0:T(8,128)} %param.17) | copy-start | bytes 1572868
  4.9 11.0 %copy-start.6 = (f32[4,3]{1,0:T(4,128)S(1)}, f32[4,3]{1,0:T(4,128)}, u32[]{:S(2)}) copy-start(f32[4,3]{1,0:T(4,128)} %param.12) | copy-start | bytes 148
  4.9 11.1 %copy-start.5 = (f32[4,2]{0,1:T(2,128)S(1)}, f32[4,2]{0,1:T(2,128)}, u32[]{:S(2)}) copy-start(f32[4,2]{0,1:T(2,128)} %param.13) | copy-start | bytes 100
  4.9 11.4 %copy-start.8 = (f32[4]{0:T(128)S(1)}, f32[4]{0:T(128)}, u32[]{:S(2)}) copy-start(f32[4]{0:T(128)} %param.14) | copy-start | bytes 52
  4.9 12.7 %copy-start.9 = (f32[2]{0:T(128)S(1)}, f32[2]{0:T(128)}, u32[]{:S(2)}) copy-start(f32[2]{0:T(128)} %param.15) | copy-start | bytes 28
  4.9 13.1 %copy-start.7 = (f32[16,2]{0,1:T(2,128)S(1)}, f32[16,2]{0,1:T(2,128)}, u32[]{:S(2)}) copy-start(f32[16,2]{0,1:T(2,128)} %param.16) | copy-start | bytes 388
  4.9 28.8 %collective-permute-start.3 = (f32[5,12,32,128]{3,2,1,0:T(8,128)S(1)}, f32[5,12,32,128]{3,2,1,0:T(8,128)S(1)}, u32[]{:S(2)}, u32[]{:S(2)}) collective-permute-start(f32[5,12,32,128]{3,2,1,0:T(8,128)S(1)} %get-tuple-element.22), channel_id=1, source_target_pairs={{0,0},{1,4},{2,6},{3,2},{4,1},{5,5},{6,7},{7,3},{8,8},{9,12},{10,1... | collective-permute-start | bytes 2949128 | tf_op jit(solution)/shard_map/ppermute | solution.py:259
  8.7 29.0 %collective-permute-start.6 = (f32[5,8,32,128]{3,2,1,0:T(8,128)S(1)}, f32[5,8,32,128]{3,2,1,0:T(8,128)S(1)}, u32[]{:S(2)}, u32[]{:S(2)}) collective-permute-start(f32[5,8,32,128]{3,2,1,0:T(8,128)S(1)} %get-tuple-element.21), channel_id=1, source_target_pairs={{4,0},{5,4},{6,6},{7,2},{8,1},{9,5},{10,7},{11,3},{12,8},{13,12},{... | collective-permute-start | bytes 1966088 | tf_op jit(solution)/shard_map/ppermute | solution.py:259
  11.4 6.8 %collective-permute-start = (f32[5,16,4,128]{3,2,1,0:T(4,128)}, f32[5,16,4,128]{3,2,1,0:T(4,128)S(1)}, u32[]{:S(2)}, u32[]{:S(2)}) collective-permute-start(f32[5,16,4,128]{3,2,1,0:T(4,128)} %pad_maximum_fusion.8), channel_id=1, source_target_pairs={{0,1},{1,2},{2,3},{3,0},{4,5},{5,6},{6,7},{7,4},{8,9},{9,10},{10,1... | collective-permute-start | bytes 491528 | tf_op jit(solution)/shard_map/ppermute | solution.py:264
  13.6 6.6 %collective-permute-start.1 = (f32[5,16,4,128]{3,2,1,0:T(4,128)}, f32[5,16,4,128]{3,2,1,0:T(4,128)}, u32[]{:S(2)}, u32[]{:S(2)}) collective-permute-start(f32[5,16,4,128]{3,2,1,0:T(4,128)} %pad_maximum_fusion.9), channel_id=1, source_target_pairs={{1,0},{2,1},{3,2},{0,3},{5,4},{6,5},{7,6},{4,7},{9,8},{10,9},{11,1... | collective-permute-start | bytes 491528 | tf_op jit(solution)/shard_map/ppermute | solution.py:265
  14.4 11.3 %collective-permute-start.4 = (s32[3,8,32,128]{3,2,1,0:T(8,128)}, s32[3,8,32,128]{3,2,1,0:T(8,128)}, u32[]{:S(2)}, u32[]{:S(2)}) collective-permute-start(s32[3,8,32,128]{3,2,1,0:T(8,128)} %slice.151), channel_id=1, source_target_pairs={{28,25},{29,29},{30,31},{31,27}} | collective-permute-start | bytes 1179656 | tf_op jit(solution)/shard_map/ppermute | solution.py:323
  18.3 23.9 %collective-permute-start.7 = (f32[5,4,32,128]{3,2,1,0:T(8,128)}, f32[5,4,32,128]{3,2,1,0:T(8,128)S(1)}, u32[]{:S(2)}, u32[]{:S(2)}) collective-permute-start(f32[5,4,32,128]{3,2,1,0:T(8,128)} %copy-done.3), channel_id=1, source_target_pairs={{4,0},{5,4},{6,6},{7,2},{8,1},{9,5},{10,7},{11,3},{12,8},{13,12},{... | collective-permute-start | bytes 983048 | tf_op jit(solution)/shard_map/ppermute | solution.py:259
  21.3 12.4 %collective-permute-start.2 = (f32[5,12,8,128]{3,2,1,0:T(8,128)S(1)}, f32[5,12,8,128]{3,2,1,0:T(8,128)S(1)}, u32[]{:S(2)}, u32[]{:S(2)}) collective-permute-start(f32[5,12,8,128]{3,2,1,0:T(8,128)S(1)} %pad_maximum_fusion), channel_id=1, source_target_pairs={{0,0},{1,4},{2,6},{3,2},{4,1},{5,5},{6,7},{7,3},{8,8},{9,12},{10,1... | collective-permute-start | bytes 737288 | tf_op jit(solution)/shard_map/ppermute | solution.py:259
  25.7 12.0 %collective-permute-start.5 = (f32[5,12,8,128]{3,2,1,0:T(8,128)S(1)}, f32[5,12,8,128]{3,2,1,0:T(8,128)S(1)}, u32[]{:S(2)}, u32[]{:S(2)}) collective-permute-start(f32[5,12,8,128]{3,2,1,0:T(8,128)S(1)} %pad_maximum_fusion.1), channel_id=1, source_target_pairs={{4,0},{5,4},{6,6},{7,2},{8,1},{9,5},{10,7},{11,3},{12,8},{13,12},{... | collective-permute-start | bytes 737288 | tf_op jit(solution)/shard_map/ppermute | solution.py:259
  44.8 8.1 %collective-permute-start.8 = (f32[5,16,4,128]{3,2,1,0:T(4,128)S(1)}, f32[5,16,4,128]{3,2,1,0:T(4,128)S(1)}, u32[]{:S(2)}, u32[]{:S(2)}) collective-permute-start(f32[5,16,4,128]{3,2,1,0:T(4,128)S(1)} %pad_maximum_fusion.10), channel_id=1, source_target_pairs={{0,4},{4,6},{6,2},{2,0},{1,5},{5,7},{7,3},{3,1},{8,12},{12,14},{14... | collective-permute-start | bytes 491528 | tf_op jit(solution)/shard_map/ppermute | solution.py:264
  47.0 20.6 %collective-permute-start.12 = (f32[5,8,32,128]{3,2,1,0:T(8,128)S(1)}, f32[5,8,32,128]{3,2,1,0:T(8,128)S(1)}, u32[]{:S(2)}, u32[]{:S(2)}) collective-permute-start(f32[5,8,32,128]{3,2,1,0:T(8,128)S(1)} %get-tuple-element.25.refs_1_), channel_id=1, source_target_pairs={{1,0},{5,4},{7,6},{3,2},{8,1},{12,5},{14,7},{10,3},{9,8},{13,12},{... | collective-permute-start | bytes 1966088 | tf_op jit(solution)/shard_map/ppermute | solution.py:259
  48.9 17.7 %collective-permute-start.11 = (f32[5,4,32,128]{3,2,1,0:T(8,128)S(1)}, f32[5,4,32,128]{3,2,1,0:T(8,128)S(1)}, u32[]{:S(2)}, u32[]{:S(2)}) collective-permute-start(f32[5,4,32,128]{3,2,1,0:T(8,128)S(1)} %get-tuple-element.23), channel_id=1, source_target_pairs={{1,0},{5,4},{7,6},{3,2},{8,1},{12,5},{14,7},{10,3},{9,8},{13,12},{... | collective-permute-start | bytes 983048 | tf_op jit(solution)/shard_map/ppermute | solution.py:259
  51.3 8.7 %collective-permute-start.9 = (f32[5,16,4,128]{3,2,1,0:T(4,128)S(1)}, f32[5,16,4,128]{3,2,1,0:T(4,128)S(1)}, u32[]{:S(2)}, u32[]{:S(2)}) collective-permute-start(f32[5,16,4,128]{3,2,1,0:T(4,128)S(1)} %pad_maximum_fusion.11), channel_id=1, source_target_pairs={{4,0},{6,4},{2,6},{0,2},{5,1},{7,5},{3,7},{1,3},{12,8},{14,12},{10... | collective-permute-start | bytes 491528 | tf_op jit(solution)/shard_map/ppermute | solution.py:265
  60.0 7.5 %collective-permute-start.10 = (f32[5,12,8,128]{3,2,1,0:T(8,128)S(1)}, f32[5,12,8,128]{3,2,1,0:T(8,128)S(1)}, u32[]{:S(2)}, u32[]{:S(2)}) collective-permute-start(f32[5,12,8,128]{3,2,1,0:T(8,128)S(1)} %pad_maximum_fusion.3), channel_id=1, source_target_pairs={{1,0},{5,4},{7,6},{3,2},{8,1},{12,5},{14,7},{10,3},{9,8},{13,12},{... | collective-permute-start | bytes 737288 | tf_op jit(solution)/shard_map/ppermute | solution.py:259
  73.9 6.1 %collective-permute-start.13 = (f32[5,16,4,128]{3,2,1,0:T(4,128)S(1)}, f32[5,16,4,128]{3,2,1,0:T(4,128)S(1)}, u32[]{:S(2)}, u32[]{:S(2)}) collective-permute-start(f32[5,16,4,128]{3,2,1,0:T(4,128)S(1)} %pad_maximum_fusion.12), channel_id=1, source_target_pairs={{0,4},{4,6},{6,2},{2,0},{1,5},{5,7},{7,3},{3,1},{8,12},{12,14},{14... | collective-permute-start | bytes 491528 | tf_op jit(solution)/shard_map/ppermute | solution.py:264
  75.1 17.5 %collective-permute-start.16 = (f32[5,4,32,128]{3,2,1,0:T(8,128)S(1)}, f32[5,4,32,128]{3,2,1,0:T(8,128)S(1)}, u32[]{:S(2)}, u32[]{:S(2)}) collective-permute-start(f32[5,4,32,128]{3,2,1,0:T(8,128)S(1)} %get-tuple-element.28), channel_id=1, source_target_pairs={{1,0},{5,4},{7,6},{3,2},{8,1},{12,5},{14,7},{10,3},{9,8},{13,12},{... | collective-permute-start | bytes 983048 | tf_op jit(solution)/shard_map/ppermute | solution.py:259
  77.0 16.3 %collective-permute-start.17 = (f32[5,8,32,128]{3,2,1,0:T(8,128)S(1)}, f32[5,8,32,128]{3,2,1,0:T(8,128)S(1)}, u32[]{:S(2)}, u32[]{:S(2)}) collective-permute-start(f32[5,8,32,128]{3,2,1,0:T(8,128)S(1)} %get-tuple-element.30.refs_1_), channel_id=1, source_target_pairs={{1,0},{5,4},{7,6},{3,2},{8,1},{12,5},{14,7},{10,3},{9,8},{13,12},{... | collective-permute-start | bytes 1966088 | tf_op jit(solution)/shard_map/ppermute | solution.py:259
  79.9 5.8 %collective-permute-start.14 = (f32[5,16,4,128]{3,2,1,0:T(4,128)S(1)}, f32[5,16,4,128]{3,2,1,0:T(4,128)S(1)}, u32[]{:S(2)}, u32[]{:S(2)}) collective-permute-start(f32[5,16,4,128]{3,2,1,0:T(4,128)S(1)} %pad_maximum_fusion.13), channel_id=1, source_target_pairs={{4,0},{6,4},{2,6},{0,2},{5,1},{7,5},{3,7},{1,3},{12,8},{14,12},{10... | collective-permute-start | bytes 491528 | tf_op jit(solution)/shard_map/ppermute | solution.py:265
  85.8 7.6 %collective-permute-start.15 = (f32[5,12,8,128]{3,2,1,0:T(8,128)S(1)}, f32[5,12,8,128]{3,2,1,0:T(8,128)S(1)}, u32[]{:S(2)}, u32[]{:S(2)}) collective-permute-start(f32[5,12,8,128]{3,2,1,0:T(8,128)S(1)} %pad_maximum_fusion.5), channel_id=1, source_target_pairs={{1,0},{5,4},{7,6},{3,2},{8,1},{12,5},{14,7},{10,3},{9,8},{13,12},{... | collective-permute-start | bytes 737288 | tf_op jit(solution)/shard_map/ppermute | solution.py:259
  99.7 6.5 %collective-permute-start.18 = (f32[5,16,4,128]{3,2,1,0:T(4,128)S(1)}, f32[5,16,4,128]{3,2,1,0:T(4,128)S(1)}, u32[]{:S(2)}, u32[]{:S(2)}) collective-permute-start(f32[5,16,4,128]{3,2,1,0:T(4,128)S(1)} %pad_maximum_fusion.14), channel_id=1, source_target_pairs={{0,4},{4,6},{6,2},{2,0},{1,5},{5,7},{7,3},{3,1},{8,12},{12,14},{14... | collective-permute-start | bytes 491528 | tf_op jit(solution)/shard_map/ppermute | solution.py:264
  100.0 17.6 %collective-permute-start.22 = (f32[5,4,32,128]{3,2,1,0:T(8,128)S(1)}, f32[5,4,32,128]{3,2,1,0:T(8,128)S(1)}, u32[]{:S(2)}, u32[]{:S(2)}) collective-permute-start(f32[5,4,32,128]{3,2,1,0:T(8,128)S(1)} %get-tuple-element.32), channel_id=1, source_target_pairs={{1,0},{5,4},{7,6},{3,2},{8,1},{12,5},{14,7},{10,3},{9,8},{13,12},{... | collective-permute-start | bytes 983048 | tf_op jit(solution)/shard_map/ppermute | solution.py:259
  101.9 15.6 %collective-permute-start.23 = (f32[5,8,32,128]{3,2,1,0:T(8,128)S(1)}, f32[5,8,32,128]{3,2,1,0:T(8,128)S(1)}, u32[]{:S(2)}, u32[]{:S(2)}) collective-permute-start(f32[5,8,32,128]{3,2,1,0:T(8,128)S(1)} %get-tuple-element.34.refs_1_), channel_id=1, source_target_pairs={{1,0},{5,4},{7,6},{3,2},{8,1},{12,5},{14,7},{10,3},{9,8},{13,12},{... | collective-permute-start | bytes 1966088 | tf_op jit(solution)/shard_map/ppermute | solution.py:259
  104.7 5.8 %collective-permute-start.19 = (f32[5,16,4,128]{3,2,1,0:T(4,128)S(1)}, f32[5,16,4,128]{3,2,1,0:T(4,128)S(1)}, u32[]{:S(2)}, u32[]{:S(2)}) collective-permute-start(f32[5,16,4,128]{3,2,1,0:T(4,128)S(1)} %pad_maximum_fusion.15), channel_id=1, source_target_pairs={{4,0},{6,4},{2,6},{0,2},{5,1},{7,5},{3,7},{1,3},{12,8},{14,12},{10... | collective-permute-start | bytes 491528 | tf_op jit(solution)/shard_map/ppermute | solution.py:265
  110.6 7.6 %collective-permute-start.21 = (f32[5,12,8,128]{3,2,1,0:T(8,128)S(1)}, f32[5,12,8,128]{3,2,1,0:T(8,128)S(1)}, u32[]{:S(2)}, u32[]{:S(2)}) collective-permute-start(f32[5,12,8,128]{3,2,1,0:T(8,128)S(1)} %pad_maximum_fusion.7), channel_id=1, source_target_pairs={{1,0},{5,4},{7,6},{3,2},{8,1},{12,5},{14,7},{10,3},{9,8},{13,12},{... | collective-permute-start | bytes 737288 | tf_op jit(solution)/shard_map/ppermute | solution.py:259
  125.1 18.9 %collective-permute-start.25 = (f32[5,6,32,128]{3,2,1,0:T(8,128)S(1)}, f32[5,6,32,128]{3,2,1,0:T(8,128)S(1)}, u32[]{:S(2)}, u32[]{:S(2)}) collective-permute-start(f32[5,6,32,128]{3,2,1,0:T(8,128)S(1)} %part.19), channel_id=1, source_target_pairs={{0,0},{4,1},{6,2},{2,3},{1,4},{5,5},{7,6},{3,7},{8,8},{12,9},{14,1... | collective-permute-start | bytes 1474568 | tf_op jit(solution)/shard_map/ppermute | solution.py:259
  127.1 17.0 %collective-permute-start.24 = (f32[5,6,32,128]{3,2,1,0:T(8,128)S(1)}, f32[5,6,32,128]{3,2,1,0:T(8,128)S(1)}, u32[]{:S(2)}, u32[]{:S(2)}) collective-permute-start(f32[5,6,32,128]{3,2,1,0:T(8,128)S(1)} %get-tuple-element.38), channel_id=1, source_target_pairs={{0,0},{4,1},{6,2},{2,3},{1,4},{5,5},{7,6},{3,7},{8,8},{12,9},{14,1... | collective-permute-start | bytes 1474568 | tf_op jit(solution)/shard_map/ppermute | solution.py:259
  130.7 13.3 %collective-permute-start.20 = (f32[5,4,32,128]{3,2,1,0:T(8,128)S(1)}, f32[5,4,32,128]{3,2,1,0:T(8,128)S(1)}, u32[]{:S(2)}, u32[]{:S(2)}) collective-permute-start(f32[5,4,32,128]{3,2,1,0:T(8,128)S(1)} %get-tuple-element.36), channel_id=1, source_target_pairs={{0,0},{4,1},{6,2},{2,3},{1,4},{5,5},{7,6},{3,7},{8,8},{12,9},{14,1... | collective-permute-start | bytes 983048 | tf_op jit(solution)/shard_map/ppermute | solution.py:259
  (4 other events, 3.9 us)

commit v7 on v6

--- a/solution.py
+++ b/solution.py
@@ -171,7 +171,7 @@
                 e = run.block - SHIFT + j + STEPS
                 if any(at <= e < until for _, at, until in outs):
                     for t in range(run.rows // 8):
-                        write(e, e + 1)(e, PAD + 8 * t, melt(table, index[j, pl.ds(8 * t, 8)]))
+                        write(e, e + 1)(e, PAD + 8 * t, melt(table, index[turn, j, pl.ds(8 * t, 8)]))
 
 
 def melt(table, row):
@@ -182,7 +182,7 @@
     return [none, none, none, none + 1.0] + mu
 
 
-def finish_kernel(place_of, ng, table, index, *refs):
+def finish_kernel(place_of, ng, turn, table, index, *refs):
     pieces, (phases, potentials) = refs[:-2], refs[-2:]
 
     def put(o, here, new):
@@ -205,17 +205,31 @@
     @pl.when(place_of() == ng - 1)
     def _():
         for j in range(SHIFT):
-            for t in range(index.shape[1] // 8):
+            for t in range(index.shape[2] // 8):
                 here = pl.ds(8 * t, 8)
-                put(at - SHIFT + j, here, melt(table, index[j, here]))
-
-
-def prepare_kernel(labels, roughness, potential, *outs):
-    starts = (0, outs[0].shape[1], labels.shape[0] - outs[2].shape[1])
+                put(at - SHIFT + j, here, melt(table, index[turn, j, here]))
+
+
+def prepare_kernel(labels_in, roughness_in, potential_in, *refs):
+    outs, (first_rows, final_rows), (labels, roughness, potential, sems) = refs[:-6], refs[-6:-4], refs[-4:]
+    rows = labels.shape[1]
+    block = labels.shape[0]
+    starts = (0, outs[0].shape[1], block - outs[2].shape[1])
     ranges = [(ref, at, at + ref.shape[1]) for ref, at in zip(outs, starts)]
     marks = sorted(set(m for _, *ends in ranges for m in ends))
-    for first, stop in zip(marks, marks[1:]):
+    copies = []
+    for n, (first, stop) in enumerate(zip(marks, marks[1:])):
+        span = pl.ds(first, stop - first)
+        pairs = [(labels_in.at[span], labels.at[span])]
+        pairs += [(roughness_in.at[a, span], roughness.at[a, span]) for a in range(4)]
+        pairs += [(potential_in.at[k, span], potential.at[k, span]) for k in range(2)]
+        copies.append([pltpu.make_async_copy(*pair, sems.at[n, i]) for i, pair in enumerate(pairs)])
+        for copy in copies[-1]:
+            copy.start()
+    for n, (first, stop) in enumerate(zip(marks, marks[1:])):
         targets = [(ref, at) for ref, at, until in ranges if at <= first and stop <= until]
+        for copy in copies[n]:
+            copy.wait()
 
         @pl.loop(first, stop)
         def _(o, targets=targets):
@@ -224,9 +238,11 @@
             inverse = 1.0 / (3.0 + rough[0] + rough[1] + rough[2] + rough[3])
             new = [(jnp.where(kind == a, 3.0, 0.0) + rough[a]) * inverse for a in range(3)]
             new += [potential[0, o], potential[1, o]]
-            for ref, at in targets:
-                for f, value in enumerate(new):
+            for f, value in enumerate(new):
+                for ref, at in targets:
                     ref[f, o - at] = value
+                first_rows[f, o] = value[:STEPS]
+                final_rows[f, o] = value[rows - STEPS :]
 
 
 def on_device(ng, nl, labels, roughness, potential, grad_coef, composition, latent, diffusivity, melt_table, melt_index):
@@ -258,9 +274,12 @@
         route = [(before(g + climb, l), after(g, l)) for g, l in blocks if g + climb < ng]
         return lax.ppermute(array, AXES, route)
 
-    def beside(parts, where):
+    def edges(parts):
         first = jnp.concatenate([p[:, :, :STEPS] for p in parts], axis=1)
         final = jnp.concatenate([p[:, :, rows - STEPS :] for p in parts], axis=1)
+        return first, final
+
+    def beside(first, final, where):
         left = lax.ppermute(final, AXES, [(where(g, l), where(g, (l + 1) % nl)) for g, l in blocks])
         right = lax.ppermute(first, AXES, [(where(g, (l + 1) % nl), where(g, l)) for g, l in blocks])
         return left, right
@@ -301,12 +320,20 @@
             name="part",
         )(table, *args)
 
-    front, back, own = pl.pallas_call(
+    away_index = lax.ppermute(melt_index, AXES, [(away(ng - 1, l) // nl * nl + l, away(ng - 1, l)) for l in range(nl)])
+
+    front, back, own, first_rows, final_rows = pl.pallas_call(
         prepare_kernel,
-        out_shape=[piece(n) for n in (highs, lows, kept)],
-        in_specs=[vmem] * 3,
-        out_specs=[vmem] * 3,
-        compiler_params=limit(8),
+        out_shape=[piece(n) for n in (highs, lows, kept)] + [piece(block, STEPS)] * 2,
+        in_specs=[pl.BlockSpec(memory_space=pltpu.HBM)] * 3,
+        out_specs=[vmem] * 5,
+        scratch_shapes=[
+            pltpu.VMEM(labels.shape, jnp.int32),
+            pltpu.VMEM(roughness.shape, f32),
+            pltpu.VMEM(potential.shape, f32),
+            pltpu.SemaphoreType.DMA((4, 7)),
+        ],
+        compiler_params=limit(58),
         name="prepare",
     )(labels, roughness, potential)
 
@@ -314,39 +341,24 @@
         return jnp.concatenate([left[:, first:stop], right[:, first:stop]], axis=2)
 
     own_parts = [(kept, 0)]
-    left, right = beside([front[:, :lows], own], home)
+    left, right = beside(first_rows, final_rows, home)
     own = [moved(own, home, away, 0)]
     own_halo = moved(packed(left, right, lows, block), home, away, 0)
     front = moved(front, home, away, 1)
     halo = moved(packed(left, right, 0, lows + highs), home, away, 1)
     back = moved(back, home, away, 1)
-    away_index = lax.ppermute(
-        melt_index[: ROUNDS - 1], AXES, [(home(ng - 1, l), away(ng - 1, l)) for l in range(nl)]
-    )
     early, seam = part(0, 0, own_parts, False, True, [(0, lows)], False, own_halo, *own)
     low = moved(early, away, away, 1)
-    high, seam = part(
-        0, kept, [(highs, 0)], True, True, [(lows, highs)], True, seam, away_index[0], halo, front
-    )
+    high, seam = part(0, kept, [(highs, 0)], True, True, [(lows, highs)], True, seam, away_index, halo, front)
     above = moved(high, away, away, 1)
     (rest,) = part(
-        0,
-        kept + highs,
-        [(lows, highs)],
-        True,
-        False,
-        [(lows + highs, lows)],
-        True,
-        seam,
-        away_index[0],
-        halo,
-        back,
+        0, kept + highs, [(lows, highs)], True, False, [(lows + highs, lows)], True, seam, away_index, halo, back
     )
 
     own_parts = [(highs, 0), (lows, highs)]
     for turn in range(1, ROUNDS):
         last = turn == ROUNDS - 1
-        left, right = beside([early, high, rest], away)
+        left, right = beside(*edges([early, high, rest]), away)
         own, own_halo = [high, rest], packed(left, right, lows, block)
         if turn > 1:
             above = moved(high, away, away, 1)
@@ -364,7 +376,7 @@
             [(lows, highs), (lows + highs, lows)],
             True,
             seam,
-            away_index[turn],
+            away_index,
             halo,
             low,
             above,
@@ -373,17 +385,7 @@
 
     cut = 2
     middle, seam = part(
-        turn,
-        kept,
-        [(lows, 0), (cut, lows)],
-        True,
-        True,
-        [(lows, lows + cut)],
-        False,
-        seam,
-        halo,
-        low,
-        above[:, :cut],
+        turn, kept, [(lows, 0), (cut, lows)], True, True, [(lows, lows + cut)], False, seam, halo, low, above[:, :cut]
     )
     middle = moved(middle, away, home, 0)
     (final,) = part(
@@ -400,13 +402,13 @@
     )
     final = moved(final, away, home, 0)
     return pl.pallas_call(
-        functools.partial(finish_kernel, home_place, ng),
+        functools.partial(finish_kernel, home_place, ng, turn),
         out_shape=[jax.ShapeDtypeStruct((n, block, rows, lanes), f32) for n in (4, 2)],
         in_specs=[smem] + [vmem] * 4,
         out_specs=[vmem] * 2,
         compiler_params=limit(8),
         name="finish",
-    )(table, melt_index[turn], sent, middle, final)
+    )(table, melt_index, sent, middle, final)
 
 
 def solution(mesh):

time: 147 us -> 150 us (1.020)
  waiting for transfers between devices: 34.6 us -> 45.2 us
  local copies, waits for them, and re-layouts: 9.08 us -> 1.38 us
  Pallas kernels: 44.6 us -> 47.5 us
  starting transfers between devices: 52.8 us -> 50.4 us
    ppermute x4, waiting for transfers between devices: 16.9 us -> 0.01 us  [beside(): lax.ppermute(first, AXES, [(where(g, (l + 1) % nl), where(g, l)) for g, l...]
    ppermute x4, waiting for transfers between devices: 0.01 us -> 15.2 us  [beside(): lax.ppermute(final, AXES, [(where(g, l), where(g, (l + 1) % nl)) for g, l...]
    ppermute x17, waiting for transfers between devices: 17.6 us -> 30 us  [moved(): return lax.ppermute(array, AXES, route)]
    unnamed x21 -> x13, local copies, waits for them, and re-layouts: 4.03 us -> 0.12 us
    pallas_call x1, Pallas kernels: 0.26 us -> 3.15 us  [on_device(): pl.pallas_call(prepare_kernel, out_shape=[piece(n) for n in (highs, lows,...]
    squeeze x2 -> x0, local copies, waits for them, and re-layouts: 1.98 us -> none  [the longest x1 1.06 us: on_device(): away_index[turn]]
    ppermute x4, starting transfers between devices: 5.14 us -> 3.62 us  [beside(): lax.ppermute(final, AXES, [(where(g, l), where(g, (l + 1) % nl)) for g, l...]
  transfers between devices with their start and end apart: 26 -> 26, of which waited for: 8 -> 9; matrix products, arithmetic and copies ran while one was open for 5% -> 2% of each run, Pallas kernels for 14% -> 18%
where the time goes in v7:
time: 150 us; the launch traced here: 148 us
  starting transfers between devices  50.4 us (34%)
  Pallas kernels  47.5 us (32%)
  waiting for transfers between devices  45.2 us (30%)
  between operations  1.87 us (1%)
  other arithmetic  1.71 us (1%)
    ppermute x17, starting transfers between devices, moved(): return lax.ppermute(array, AXES, route)  43.4 us
    pallas_call x10, Pallas kernels, part(): pl.pallas_call(functools.partial(part_kernel, turn, away_place, (ng, bloc...  42.5 us
    ppermute x17, waiting for transfers between devices, moved(): return lax.ppermute(array, AXES, route)  30 us
    ppermute x4, waiting for transfers between devices, beside(): lax.ppermute(final, AXES, [(where(g, l), where(g, (l + 1) % nl)) for g, l...  15.2 us
    ppermute x4, starting transfers between devices, beside(): lax.ppermute(final, AXES, [(where(g, l), where(g, (l + 1) % nl)) for g, l...  3.62 us
    pallas_call x1, Pallas kernels, on_device(): pl.pallas_call(prepare_kernel, out_shape=[piece(n) for n in (highs, lows,...  3.15 us
  transfers between devices with their start and end apart: 26, of which 9 were waited for; matrix products, arithmetic and copies ran while one was open for 2% of the time, Pallas kernels for 18%

profile of v7, /device:TPU:17, one launch (start us, length us, event | category | flops | bytes accessed | tf_op | source)
XLA Modules:
  0.0 148.1 jit_solution(18116392304699939123)
XLA Ops:
  1.5 3.1 %prepare.1 = (f32[5,8,32,128]{3,2,1,0:T(8,128)}, f32[5,4,32,128]{3,2,1,0:T(8,128)}, f32[5,12,32,128]{3,2,1,0:T(8,128)}, f32[5,16,4,128]{3,2,1,0:T(4,128)}, f32[5,16,4,128]{3,2,1,0:T(4,128)}) custom-call(s32[16,32,128]{2,1,0:T(8,128)} %labels_in.1, f32[4,16,32,128]{3,2,1,0:T(8,128)} %roughness_in.1, f32[2,16,32,128]{3,2,1,0:T(8,128)} %potential_in.1), custom_call_target="tpu_custom_call" | custom-call | tf_op jit(solution)/shard_map/prepare/pallas_call | solution.py:325
  6.5 3.0 %collective-permute-start.7 = (f32[5,4,32,128]{3,2,1,0:T(8,128)}, f32[5,4,32,128]{3,2,1,0:T(8,128)S(1)}, u32[]{:S(2)}, u32[]{:S(2)}) collective-permute-start(f32[5,4,32,128]{3,2,1,0:T(8,128)} %get-tuple-element.31), channel_id=1, source_target_pairs={{4,0},{5,4},{6,6},{7,2},{8,1},{9,5},{10,7},{11,3},{12,8},{13,12},{... | collective-permute-start | bytes 983048 | tf_op jit(solution)/shard_map/ppermute | solution.py:275
  9.5 2.6 %collective-permute-start.6 = (f32[5,8,32,128]{3,2,1,0:T(8,128)}, f32[5,8,32,128]{3,2,1,0:T(8,128)S(1)}, u32[]{:S(2)}, u32[]{:S(2)}) collective-permute-start(f32[5,8,32,128]{3,2,1,0:T(8,128)} %get-tuple-element.28), channel_id=1, source_target_pairs={{4,0},{5,4},{6,6},{7,2},{8,1},{9,5},{10,7},{11,3},{12,8},{13,12},{... | collective-permute-start | bytes 1966088 | tf_op jit(solution)/shard_map/ppermute | solution.py:275
  12.5 2.4 %collective-permute-start.3 = (f32[5,12,32,128]{3,2,1,0:T(8,128)}, f32[5,12,32,128]{3,2,1,0:T(8,128)S(1)}, u32[]{:S(2)}, u32[]{:S(2)}) collective-permute-start(f32[5,12,32,128]{3,2,1,0:T(8,128)} %get-tuple-element.25), channel_id=1, source_target_pairs={{0,0},{1,4},{2,6},{3,2},{4,1},{5,5},{6,7},{7,3},{8,8},{9,12},{10,1... | collective-permute-start | bytes 2949128 | tf_op jit(solution)/shard_map/ppermute | solution.py:275
  15.1 3.1 %collective-permute-start.2 = (f32[5,12,8,128]{3,2,1,0:T(8,128)S(1)}, f32[5,12,8,128]{3,2,1,0:T(8,128)S(1)}, u32[]{:S(2)}, u32[]{:S(2)}) collective-permute-start(f32[5,12,8,128]{3,2,1,0:T(8,128)S(1)} %pad_maximum_fusion), channel_id=1, source_target_pairs={{0,0},{1,4},{2,6},{3,2},{4,1},{5,5},{6,7},{7,3},{8,8},{9,12},{10,1... | collective-permute-start | bytes 737288 | tf_op jit(solution)/shard_map/ppermute | solution.py:275
  18.4 18.4 %collective-permute-done.2.refs_0_ = f32[5,12,8,128]{3,2,1,0:T(8,128)S(1)} collective-permute-done((f32[5,12,8,128]{3,2,1,0:T(8,128)S(1)}, f32[5,12,8,128]{3,2,1,0:T(8,128)S(1)}, u32[]{:S(2)}, u32[]{:S(2)}) %collective-permute-start.2) | collective-permute-done | bytes 245792 | tf_op jit(solution)/shard_map/ppermute | solution.py:275
  36.8 1.9 %collective-permute-start.5 = (f32[5,12,8,128]{3,2,1,0:T(8,128)S(1)}, f32[5,12,8,128]{3,2,1,0:T(8,128)S(1)}, u32[]{:S(2)}, u32[]{:S(2)}) collective-permute-start(f32[5,12,8,128]{3,2,1,0:T(8,128)S(1)} %pad_maximum_fusion.1), channel_id=1, source_target_pairs={{4,0},{5,4},{6,6},{7,2},{8,1},{9,5},{10,7},{11,3},{12,8},{13,12},{... | collective-permute-start | bytes 737288 | tf_op jit(solution)/shard_map/ppermute | solution.py:275
  40.7 4.0 %part.10 = (f32[5,4,32,128]{3,2,1,0:T(8,128)S(1)}, f32[4,6,2,48,128]{4,3,2,1,0:T(8,128)S(1)}) custom-call(f32[72]{0:T(128)S(1)} %concatenate.45.table, f32[5,12,8,128]{3,2,1,0:T(8,128)S(1)} %collective-permute-done.2.refs_0_, f32[5,12,32,128]{3,2,1,0:T(8,128)S(1)} %collective-permute-done.3.refs_1_), custom_call_target="tpu_custom_call" | custom-call | flops 153354240 | bytes 4000000 | tf_op jit(solution)/shard_map/part/pallas_call | solution.py:301
  45.7 4.5 %part.11 = (f32[5,8,32,128]{3,2,1,0:T(8,128)S(1)}, f32[4,6,2,48,128]{4,3,2,1,0:T(8,128)S(1)}) custom-call(f32[72]{0:T(128)S(1)} %concatenate.45.table, f32[4,6,2,48,128]{4,3,2,1,0:T(8,128)S(1)} %get-tuple-element.27.refs_0_, s32[4,8,32,128]{3,2,1,0:T(8,128)S(1)} %collective-permute-done.4.refs_1_, f32[5,12,8,128]{3,2,1,0:T(8,128)S(1)} %collective-permute-done.5.refs_2_, ...), custom_call_target="tpu_custom_call" | custom-call | flops 102236160 | bytes 4000000 | tf_op jit(solution)/shard_map/part/pallas_call | solution.py:301
  50.2 2.5 %part.12.refs_2_ = f32[5,4,32,128]{3,2,1,0:T(8,128)S(1)} custom-call(f32[72]{0:T(128)S(1)} %concatenate.45.table, f32[4,6,2,48,128]{4,3,2,1,0:T(8,128)S(1)} %get-tuple-element.30.refs_0_, s32[4,8,32,128]{3,2,1,0:T(8,128)S(1)} %collective-permute-done.4.refs_1_, f32[5,12,8,128]{3,2,1,0:T(8,128)S(1)} %collective-permute-done.5.refs_2_, ...), custom_call_target="tpu_custom_call" | custom-call | flops 51118080 | bytes 4000000 | tf_op jit(solution)/shard_map/part/pallas_call | solution.py:301
  53.1 3.0 %collective-permute-start.11 = (f32[5,4,32,128]{3,2,1,0:T(8,128)S(1)}, f32[5,4,32,128]{3,2,1,0:T(8,128)S(1)}, u32[]{:S(2)}, u32[]{:S(2)}) collective-permute-start(f32[5,4,32,128]{3,2,1,0:T(8,128)S(1)} %get-tuple-element.26), channel_id=1, source_target_pairs={{1,0},{5,4},{7,6},{3,2},{8,1},{12,5},{14,7},{10,3},{9,8},{13,12},{... | collective-permute-start | bytes 983048 | tf_op jit(solution)/shard_map/ppermute | solution.py:275
  56.1 1.9 %collective-permute-start.12 = (f32[5,8,32,128]{3,2,1,0:T(8,128)S(1)}, f32[5,8,32,128]{3,2,1,0:T(8,128)S(1)}, u32[]{:S(2)}, u32[]{:S(2)}) collective-permute-start(f32[5,8,32,128]{3,2,1,0:T(8,128)S(1)} %get-tuple-element.29.refs_1_), channel_id=1, source_target_pairs={{1,0},{5,4},{7,6},{3,2},{8,1},{12,5},{14,7},{10,3},{9,8},{13,12},{... | collective-permute-start | bytes 1966088 | tf_op jit(solution)/shard_map/ppermute | solution.py:275
  59.5 4.1 %collective-permute-done.8 = f32[5,16,4,128]{3,2,1,0:T(4,128)S(1)} collective-permute-done((f32[5,16,4,128]{3,2,1,0:T(4,128)S(1)}, f32[5,16,4,128]{3,2,1,0:T(4,128)S(1)}, u32[]{:S(2)}, u32[]{:S(2)}) %collective-permute-start.8) | collective-permute-done | bytes 163872 | tf_op jit(solution)/shard_map/ppermute | solution.py:283
  63.7 3.2 %collective-permute-start.10 = (f32[5,12,8,128]{3,2,1,0:T(8,128)S(1)}, f32[5,12,8,128]{3,2,1,0:T(8,128)S(1)}, u32[]{:S(2)}, u32[]{:S(2)}) collective-permute-start(f32[5,12,8,128]{3,2,1,0:T(8,128)S(1)} %pad_maximum_fusion.3), channel_id=1, source_target_pairs={{1,0},{5,4},{7,6},{3,2},{8,1},{12,5},{14,7},{10,3},{9,8},{13,12},{... | collective-permute-start | bytes 737288 | tf_op jit(solution)/shard_map/ppermute | solution.py:275
  67.0 4.0 %part.13 = (f32[5,4,32,128]{3,2,1,0:T(8,128)S(1)}, f32[4,6,2,48,128]{4,3,2,1,0:T(8,128)S(1)}) custom-call(f32[72]{0:T(128)S(1)} %concatenate.45.table, f32[5,12,8,128]{3,2,1,0:T(8,128)S(1)} %pad_maximum_fusion.2.refs_0_, f32[5,8,32,128]{3,2,1,0:T(8,128)S(1)} %get-tuple-element.29.refs_1_, f32[5,4,32,128]{3,2,1,0:T(8,128)S(1)} %part.12.refs_2_), custom_call_target="tpu_custom_call" | custom-call | flops 153354240 | bytes 4000000 | tf_op jit(solution)/shard_map/part/pallas_call | solution.py:301
  72.0 6.2 %part.14 = (f32[5,8,32,128]{3,2,1,0:T(8,128)S(1)}, f32[5,4,32,128]{3,2,1,0:T(8,128)S(1)}) custom-call(f32[72]{0:T(128)S(1)} %concatenate.45.table, f32[4,6,2,48,128]{4,3,2,1,0:T(8,128)S(1)} %get-tuple-element.33.refs_0_, s32[4,8,32,128]{3,2,1,0:T(8,128)S(1)} %collective-permute-done.4.refs_1_, f32[5,12,8,128]{3,2,1,0:T(8,128)S(1)} %collective-permute-done.10.refs_2_, ...), custom_call_target="tpu_custom_call" | custom-call | flops 153354240 | bytes 4000000 | tf_op jit(solution)/shard_map/part/pallas_call | solution.py:301
  81.8 2.4 %collective-permute-start.17 = (f32[5,8,32,128]{3,2,1,0:T(8,128)S(1)}, f32[5,8,32,128]{3,2,1,0:T(8,128)S(1)}, u32[]{:S(2)}, u32[]{:S(2)}) collective-permute-start(f32[5,8,32,128]{3,2,1,0:T(8,128)S(1)} %get-tuple-element.34.refs_1_), channel_id=1, source_target_pairs={{1,0},{5,4},{7,6},{3,2},{8,1},{12,5},{14,7},{10,3},{9,8},{13,12},{... | collective-permute-start | bytes 1966088 | tf_op jit(solution)/shard_map/ppermute | solution.py:275
  84.4 5.7 %collective-permute-done.13 = f32[5,16,4,128]{3,2,1,0:T(4,128)S(1)} collective-permute-done((f32[5,16,4,128]{3,2,1,0:T(4,128)S(1)}, f32[5,16,4,128]{3,2,1,0:T(4,128)S(1)}, u32[]{:S(2)}, u32[]{:S(2)}) %collective-permute-start.13) | collective-permute-done | bytes 163872 | tf_op jit(solution)/shard_map/ppermute | solution.py:283
  90.1 2.8 %collective-permute-start.15 = (f32[5,12,8,128]{3,2,1,0:T(8,128)S(1)}, f32[5,12,8,128]{3,2,1,0:T(8,128)S(1)}, u32[]{:S(2)}, u32[]{:S(2)}) collective-permute-start(f32[5,12,8,128]{3,2,1,0:T(8,128)S(1)} %pad_maximum_fusion.5), channel_id=1, source_target_pairs={{1,0},{5,4},{7,6},{3,2},{8,1},{12,5},{14,7},{10,3},{9,8},{13,12},{... | collective-permute-start | bytes 737288 | tf_op jit(solution)/shard_map/ppermute | solution.py:275
  93.0 4.0 %part.15 = (f32[5,4,32,128]{3,2,1,0:T(8,128)S(1)}, f32[4,6,2,48,128]{4,3,2,1,0:T(8,128)S(1)}) custom-call(f32[72]{0:T(128)S(1)} %concatenate.45.table, f32[5,12,8,128]{3,2,1,0:T(8,128)S(1)} %pad_maximum_fusion.4.refs_0_, f32[5,8,32,128]{3,2,1,0:T(8,128)S(1)} %get-tuple-element.34.refs_1_, f32[5,4,32,128]{3,2,1,0:T(8,128)S(1)} %get-tuple-element.35.refs_2_), custom_call_target="tpu_custom_call" | custom-call | flops 153354240 | bytes 4000000 | tf_op jit(solution)/shard_map/part/pallas_call | solution.py:301
  98.1 6.2 %part.16 = (f32[5,8,32,128]{3,2,1,0:T(8,128)S(1)}, f32[5,4,32,128]{3,2,1,0:T(8,128)S(1)}) custom-call(f32[72]{0:T(128)S(1)} %concatenate.45.table, f32[4,6,2,48,128]{4,3,2,1,0:T(8,128)S(1)} %get-tuple-element.37.refs_0_, s32[4,8,32,128]{3,2,1,0:T(8,128)S(1)} %collective-permute-done.4.refs_1_, f32[5,12,8,128]{3,2,1,0:T(8,128)S(1)} %collective-permute-done.15.refs_2_, ...), custom_call_target="tpu_custom_call" | custom-call | flops 153354240 | bytes 4000000 | tf_op jit(solution)/shard_map/part/pallas_call | solution.py:301
  105.2 1.9 %collective-permute-start.22 = (f32[5,4,32,128]{3,2,1,0:T(8,128)S(1)}, f32[5,4,32,128]{3,2,1,0:T(8,128)S(1)}, u32[]{:S(2)}, u32[]{:S(2)}) collective-permute-start(f32[5,4,32,128]{3,2,1,0:T(8,128)S(1)} %get-tuple-element.36), channel_id=1, source_target_pairs={{1,0},{5,4},{7,6},{3,2},{8,1},{12,5},{14,7},{10,3},{9,8},{13,12},{... | collective-permute-start | bytes 983048 | tf_op jit(solution)/shard_map/ppermute | solution.py:275
  107.2 3.0 %collective-permute-start.23 = (f32[5,8,32,128]{3,2,1,0:T(8,128)S(1)}, f32[5,8,32,128]{3,2,1,0:T(8,128)S(1)}, u32[]{:S(2)}, u32[]{:S(2)}) collective-permute-start(f32[5,8,32,128]{3,2,1,0:T(8,128)S(1)} %get-tuple-element.38.refs_1_), channel_id=1, source_target_pairs={{1,0},{5,4},{7,6},{3,2},{8,1},{12,5},{14,7},{10,3},{9,8},{13,12},{... | collective-permute-start | bytes 1966088 | tf_op jit(solution)/shard_map/ppermute | solution.py:275
  110.6 5.4 %collective-permute-done.18 = f32[5,16,4,128]{3,2,1,0:T(4,128)S(1)} collective-permute-done((f32[5,16,4,128]{3,2,1,0:T(4,128)S(1)}, f32[5,16,4,128]{3,2,1,0:T(4,128)S(1)}, u32[]{:S(2)}, u32[]{:S(2)}) %collective-permute-start.18) | collective-permute-done | bytes 163872 | tf_op jit(solution)/shard_map/ppermute | solution.py:283
  116.1 2.8 %collective-permute-start.21 = (f32[5,12,8,128]{3,2,1,0:T(8,128)S(1)}, f32[5,12,8,128]{3,2,1,0:T(8,128)S(1)}, u32[]{:S(2)}, u32[]{:S(2)}) collective-permute-start(f32[5,12,8,128]{3,2,1,0:T(8,128)S(1)} %pad_maximum_fusion.7), channel_id=1, source_target_pairs={{1,0},{5,4},{7,6},{3,2},{8,1},{12,5},{14,7},{10,3},{9,8},{13,12},{... | collective-permute-start | bytes 737288 | tf_op jit(solution)/shard_map/ppermute | solution.py:275
  118.9 4.0 %part.17 = (f32[5,4,32,128]{3,2,1,0:T(8,128)S(1)}, f32[4,6,2,48,128]{4,3,2,1,0:T(8,128)S(1)}) custom-call(f32[72]{0:T(128)S(1)} %concatenate.45.table, f32[5,12,8,128]{3,2,1,0:T(8,128)S(1)} %pad_maximum_fusion.6.refs_0_, f32[5,8,32,128]{3,2,1,0:T(8,128)S(1)} %get-tuple-element.38.refs_1_, f32[5,4,32,128]{3,2,1,0:T(8,128)S(1)} %get-tuple-element.39.refs_2_), custom_call_target="tpu_custom_call" | custom-call | flops 153354240 | bytes 4000000 | tf_op jit(solution)/shard_map/part/pallas_call | solution.py:301
  123.6 3.5 %part.18 = (f32[5,6,32,128]{3,2,1,0:T(8,128)S(1)}, f32[4,6,2,48,128]{4,3,2,1,0:T(8,128)S(1)}) custom-call(f32[72]{0:T(128)S(1)} %concatenate.45.table, f32[4,6,2,48,128]{4,3,2,1,0:T(8,128)S(1)} %get-tuple-element.41.refs_0_, f32[5,12,8,128]{3,2,1,0:T(8,128)S(1)} %collective-permute-done.21.refs_1_, f32[5,4,32,128]{3,2,1,0:T(8,128)S(1)} %collective-permute-done.22.refs_2_, ...), custom_call_target="tpu_custom_call" | custom-call | flops 76677120 | bytes 4000000 | tf_op jit(solution)/shard_map/part/pallas_call | solution.py:301
  127.1 1.9 %collective-permute-start.24 = (f32[5,6,32,128]{3,2,1,0:T(8,128)S(1)}, f32[5,6,32,128]{3,2,1,0:T(8,128)S(1)}, u32[]{:S(2)}, u32[]{:S(2)}) collective-permute-start(f32[5,6,32,128]{3,2,1,0:T(8,128)S(1)} %get-tuple-element.42), channel_id=1, source_target_pairs={{0,0},{4,1},{6,2},{2,3},{1,4},{5,5},{7,6},{3,7},{8,8},{12,9},{14,1... | collective-permute-start | bytes 1474568 | tf_op jit(solution)/shard_map/ppermute | solution.py:275
  129.1 3.4 %part.19 = f32[5,6,32,128]{3,2,1,0:T(8,128)S(1)} custom-call(f32[72]{0:T(128)S(1)} %concatenate.45.table, f32[4,6,2,48,128]{4,3,2,1,0:T(8,128)S(1)} %get-tuple-element.43.refs_0_, f32[5,12,8,128]{3,2,1,0:T(8,128)S(1)} %collective-permute-done.21.refs_1_, f32[5,6,32,128]{3,2,1,0:T(8,128)S(1)} %slice.167.refs_2_), custom_call_target="tpu_custom_call" | custom-call | flops 76677120 | bytes 4000000 | tf_op jit(solution)/shard_map/part/pallas_call | solution.py:301
  132.6 3.6 %collective-permute-start.25 = (f32[5,6,32,128]{3,2,1,0:T(8,128)S(1)}, f32[5,6,32,128]{3,2,1,0:T(8,128)S(1)}, u32[]{:S(2)}, u32[]{:S(2)}) collective-permute-start(f32[5,6,32,128]{3,2,1,0:T(8,128)S(1)} %part.19), channel_id=1, source_target_pairs={{0,0},{4,1},{6,2},{2,3},{1,4},{5,5},{7,6},{3,7},{8,8},{12,9},{14,1... | collective-permute-start | bytes 1474568 | tf_op jit(solution)/shard_map/ppermute | solution.py:275
  136.2 1.9 %collective-permute-start.20 = (f32[5,4,32,128]{3,2,1,0:T(8,128)S(1)}, f32[5,4,32,128]{3,2,1,0:T(8,128)S(1)}, u32[]{:S(2)}, u32[]{:S(2)}) collective-permute-start(f32[5,4,32,128]{3,2,1,0:T(8,128)S(1)} %get-tuple-element.40), channel_id=1, source_target_pairs={{0,0},{4,1},{6,2},{2,3},{1,4},{5,5},{7,6},{3,7},{8,8},{12,9},{14,1... | collective-permute-start | bytes 983048 | tf_op jit(solution)/shard_map/ppermute | solution.py:275
  138.1 8.1 %collective-permute-done.20.refs_0_ = f32[5,4,32,128]{3,2,1,0:T(8,128)S(1)} collective-permute-done((f32[5,4,32,128]{3,2,1,0:T(8,128)S(1)}, f32[5,4,32,128]{3,2,1,0:T(8,128)S(1)}, u32[]{:S(2)}, u32[]{:S(2)}) %collective-permute-start.20) | collective-permute-done | bytes 327712 | tf_op jit(solution)/shard_map/ppermute | solution.py:275
  (93 shorter events, 17.4 us)
Async XLA Ops:
  0.6 11.5 %copy-start.2 = (f32[4,3]{1,0:T(4,128)S(1)}, f32[4,3]{1,0:T(4,128)}, u32[]{:S(2)}) copy-start(f32[4,3]{1,0:T(4,128)} %param.12) | copy-start | bytes 148
  0.6 11.6 %copy-start.1 = (f32[4,2]{0,1:T(2,128)S(1)}, f32[4,2]{0,1:T(2,128)}, u32[]{:S(2)}) copy-start(f32[4,2]{0,1:T(2,128)} %param.13) | copy-start | bytes 100
  0.7 45.0 %collective-permute-start.4 = (s32[4,8,32,128]{3,2,1,0:T(8,128)}, s32[4,8,32,128]{3,2,1,0:T(8,128)S(1)}, u32[]{:S(2)}, u32[]{:S(2)}) collective-permute-start(s32[4,8,32,128]{3,2,1,0:T(8,128)} %index.1), channel_id=1, source_target_pairs={{24,25},{29,29},{30,31},{27,27}} | collective-permute-start | bytes 1572872 | tf_op jit(solution)/shard_map/ppermute | solution.py:323
  4.6 34.0 %copy-start.5 = (f32[2]{0:T(128)S(1)}, f32[2]{0:T(128)}, u32[]{:S(2)}) copy-start(f32[2]{0:T(128)} %param.15) | copy-start | bytes 28
  4.7 34.0 %copy-start.4 = (f32[4]{0:T(128)S(1)}, f32[4]{0:T(128)}, u32[]{:S(2)}) copy-start(f32[4]{0:T(128)} %param.14) | copy-start | bytes 52
  4.7 35.1 %copy-start.3 = (f32[16,2]{0,1:T(2,128)S(1)}, f32[16,2]{0,1:T(2,128)}, u32[]{:S(2)}) copy-start(f32[16,2]{0,1:T(2,128)} %param.16) | copy-start | bytes 388
  4.7 7.9 %collective-permute-start = (f32[5,16,4,128]{3,2,1,0:T(4,128)}, f32[5,16,4,128]{3,2,1,0:T(4,128)S(1)}, u32[]{:S(2)}, u32[]{:S(2)}) collective-permute-start(f32[5,16,4,128]{3,2,1,0:T(4,128)} %get-tuple-element.23), channel_id=1, source_target_pairs={{0,1},{1,2},{2,3},{3,0},{4,5},{5,6},{6,7},{7,4},{8,9},{9,10},{10,1... | collective-permute-start | bytes 491528 | tf_op jit(solution)/shard_map/ppermute | solution.py:283
  6.5 8.5 %collective-permute-start.1 = (f32[5,16,4,128]{3,2,1,0:T(4,128)}, f32[5,16,4,128]{3,2,1,0:T(4,128)S(1)}, u32[]{:S(2)}, u32[]{:S(2)}) collective-permute-start(f32[5,16,4,128]{3,2,1,0:T(4,128)} %get-tuple-element.24), channel_id=1, source_target_pairs={{1,0},{2,1},{3,2},{0,3},{5,4},{6,5},{7,6},{4,7},{9,8},{10,9},{11,1... | collective-permute-start | bytes 491528 | tf_op jit(solution)/shard_map/ppermute | solution.py:284
  6.5 43.6 %collective-permute-start.7 = (f32[5,4,32,128]{3,2,1,0:T(8,128)}, f32[5,4,32,128]{3,2,1,0:T(8,128)S(1)}, u32[]{:S(2)}, u32[]{:S(2)}) collective-permute-start(f32[5,4,32,128]{3,2,1,0:T(8,128)} %get-tuple-element.31), channel_id=1, source_target_pairs={{4,0},{5,4},{6,6},{7,2},{8,1},{9,5},{10,7},{11,3},{12,8},{13,12},{... | collective-permute-start | bytes 983048 | tf_op jit(solution)/shard_map/ppermute | solution.py:275
  9.5 36.1 %collective-permute-start.6 = (f32[5,8,32,128]{3,2,1,0:T(8,128)}, f32[5,8,32,128]{3,2,1,0:T(8,128)S(1)}, u32[]{:S(2)}, u32[]{:S(2)}) collective-permute-start(f32[5,8,32,128]{3,2,1,0:T(8,128)} %get-tuple-element.28), channel_id=1, source_target_pairs={{4,0},{5,4},{6,6},{7,2},{8,1},{9,5},{10,7},{11,3},{12,8},{13,12},{... | collective-permute-start | bytes 1966088 | tf_op jit(solution)/shard_map/ppermute | solution.py:275
  12.5 28.2 %collective-permute-start.3 = (f32[5,12,32,128]{3,2,1,0:T(8,128)}, f32[5,12,32,128]{3,2,1,0:T(8,128)S(1)}, u32[]{:S(2)}, u32[]{:S(2)}) collective-permute-start(f32[5,12,32,128]{3,2,1,0:T(8,128)} %get-tuple-element.25), channel_id=1, source_target_pairs={{0,0},{1,4},{2,6},{3,2},{4,1},{5,5},{6,7},{7,3},{8,8},{9,12},{10,1... | collective-permute-start | bytes 2949128 | tf_op jit(solution)/shard_map/ppermute | solution.py:275
  15.1 21.6 %collective-permute-start.2 = (f32[5,12,8,128]{3,2,1,0:T(8,128)S(1)}, f32[5,12,8,128]{3,2,1,0:T(8,128)S(1)}, u32[]{:S(2)}, u32[]{:S(2)}) collective-permute-start(f32[5,12,8,128]{3,2,1,0:T(8,128)S(1)} %pad_maximum_fusion), channel_id=1, source_target_pairs={{0,0},{1,4},{2,6},{3,2},{4,1},{5,5},{6,7},{7,3},{8,8},{9,12},{10,1... | collective-permute-start | bytes 737288 | tf_op jit(solution)/shard_map/ppermute | solution.py:275
  36.8 8.9 %collective-permute-start.5 = (f32[5,12,8,128]{3,2,1,0:T(8,128)S(1)}, f32[5,12,8,128]{3,2,1,0:T(8,128)S(1)}, u32[]{:S(2)}, u32[]{:S(2)}) collective-permute-start(f32[5,12,8,128]{3,2,1,0:T(8,128)S(1)} %pad_maximum_fusion.1), channel_id=1, source_target_pairs={{4,0},{5,4},{6,6},{7,2},{8,1},{9,5},{10,7},{11,3},{12,8},{13,12},{... | collective-permute-start | bytes 737288 | tf_op jit(solution)/shard_map/ppermute | solution.py:275
  52.8 6.6 %collective-permute-start.9 = (f32[5,16,4,128]{3,2,1,0:T(4,128)S(1)}, f32[5,16,4,128]{3,2,1,0:T(4,128)S(1)}, u32[]{:S(2)}, u32[]{:S(2)}) collective-permute-start(f32[5,16,4,128]{3,2,1,0:T(4,128)S(1)} %pad_maximum_fusion.9), channel_id=1, source_target_pairs={{4,0},{6,4},{2,6},{0,2},{5,1},{7,5},{3,7},{1,3},{12,8},{14,12},{10... | collective-permute-start | bytes 491528 | tf_op jit(solution)/shard_map/ppermute | solution.py:284
  53.1 18.0 %collective-permute-start.11 = (f32[5,4,32,128]{3,2,1,0:T(8,128)S(1)}, f32[5,4,32,128]{3,2,1,0:T(8,128)S(1)}, u32[]{:S(2)}, u32[]{:S(2)}) collective-permute-start(f32[5,4,32,128]{3,2,1,0:T(8,128)S(1)} %get-tuple-element.26), channel_id=1, source_target_pairs={{1,0},{5,4},{7,6},{3,2},{8,1},{12,5},{14,7},{10,3},{9,8},{13,12},{... | collective-permute-start | bytes 983048 | tf_op jit(solution)/shard_map/ppermute | solution.py:275
  56.1 15.9 %collective-permute-start.12 = (f32[5,8,32,128]{3,2,1,0:T(8,128)S(1)}, f32[5,8,32,128]{3,2,1,0:T(8,128)S(1)}, u32[]{:S(2)}, u32[]{:S(2)}) collective-permute-start(f32[5,8,32,128]{3,2,1,0:T(8,128)S(1)} %get-tuple-element.29.refs_1_), channel_id=1, source_target_pairs={{1,0},{5,4},{7,6},{3,2},{8,1},{12,5},{14,7},{10,3},{9,8},{13,12},{... | collective-permute-start | bytes 1966088 | tf_op jit(solution)/shard_map/ppermute | solution.py:275
  58.1 5.6 %collective-permute-start.8 = (f32[5,16,4,128]{3,2,1,0:T(4,128)S(1)}, f32[5,16,4,128]{3,2,1,0:T(4,128)S(1)}, u32[]{:S(2)}, u32[]{:S(2)}) collective-permute-start(f32[5,16,4,128]{3,2,1,0:T(4,128)S(1)} %pad_maximum_fusion.8), channel_id=1, source_target_pairs={{0,4},{4,6},{6,2},{2,0},{1,5},{5,7},{7,3},{3,1},{8,12},{12,14},{14... | collective-permute-start | bytes 491528 | tf_op jit(solution)/shard_map/ppermute | solution.py:283
  63.7 8.3 %collective-permute-start.10 = (f32[5,12,8,128]{3,2,1,0:T(8,128)S(1)}, f32[5,12,8,128]{3,2,1,0:T(8,128)S(1)}, u32[]{:S(2)}, u32[]{:S(2)}) collective-permute-start(f32[5,12,8,128]{3,2,1,0:T(8,128)S(1)} %pad_maximum_fusion.3), channel_id=1, source_target_pairs={{1,0},{5,4},{7,6},{3,2},{8,1},{12,5},{14,7},{10,3},{9,8},{13,12},{... | collective-permute-start | bytes 737288 | tf_op jit(solution)/shard_map/ppermute | solution.py:275
  78.3 6.0 %collective-permute-start.14 = (f32[5,16,4,128]{3,2,1,0:T(4,128)S(1)}, f32[5,16,4,128]{3,2,1,0:T(4,128)S(1)}, u32[]{:S(2)}, u32[]{:S(2)}) collective-permute-start(f32[5,16,4,128]{3,2,1,0:T(4,128)S(1)} %pad_maximum_fusion.11), channel_id=1, source_target_pairs={{4,0},{6,4},{2,6},{0,2},{5,1},{7,5},{3,7},{1,3},{12,8},{14,12},{10... | collective-permute-start | bytes 491528 | tf_op jit(solution)/shard_map/ppermute | solution.py:284
  79.9 17.2 %collective-permute-start.16 = (f32[5,4,32,128]{3,2,1,0:T(8,128)S(1)}, f32[5,4,32,128]{3,2,1,0:T(8,128)S(1)}, u32[]{:S(2)}, u32[]{:S(2)}) collective-permute-start(f32[5,4,32,128]{3,2,1,0:T(8,128)S(1)} %get-tuple-element.32), channel_id=1, source_target_pairs={{1,0},{5,4},{7,6},{3,2},{8,1},{12,5},{14,7},{10,3},{9,8},{13,12},{... | collective-permute-start | bytes 983048 | tf_op jit(solution)/shard_map/ppermute | solution.py:275
  81.8 16.3 %collective-permute-start.17 = (f32[5,8,32,128]{3,2,1,0:T(8,128)S(1)}, f32[5,8,32,128]{3,2,1,0:T(8,128)S(1)}, u32[]{:S(2)}, u32[]{:S(2)}) collective-permute-start(f32[5,8,32,128]{3,2,1,0:T(8,128)S(1)} %get-tuple-element.34.refs_1_), channel_id=1, source_target_pairs={{1,0},{5,4},{7,6},{3,2},{8,1},{12,5},{14,7},{10,3},{9,8},{13,12},{... | collective-permute-start | bytes 1966088 | tf_op jit(solution)/shard_map/ppermute | solution.py:275
  84.3 5.8 %collective-permute-start.13 = (f32[5,16,4,128]{3,2,1,0:T(4,128)S(1)}, f32[5,16,4,128]{3,2,1,0:T(4,128)S(1)}, u32[]{:S(2)}, u32[]{:S(2)}) collective-permute-start(f32[5,16,4,128]{3,2,1,0:T(4,128)S(1)} %pad_maximum_fusion.10), channel_id=1, source_target_pairs={{0,4},{4,6},{6,2},{2,0},{1,5},{5,7},{7,3},{3,1},{8,12},{12,14},{14... | collective-permute-start | bytes 491528 | tf_op jit(solution)/shard_map/ppermute | solution.py:283
  90.1 7.9 %collective-permute-start.15 = (f32[5,12,8,128]{3,2,1,0:T(8,128)S(1)}, f32[5,12,8,128]{3,2,1,0:T(8,128)S(1)}, u32[]{:S(2)}, u32[]{:S(2)}) collective-permute-start(f32[5,12,8,128]{3,2,1,0:T(8,128)S(1)} %pad_maximum_fusion.5), channel_id=1, source_target_pairs={{1,0},{5,4},{7,6},{3,2},{8,1},{12,5},{14,7},{10,3},{9,8},{13,12},{... | collective-permute-start | bytes 737288 | tf_op jit(solution)/shard_map/ppermute | solution.py:275
  104.4 6.1 %collective-permute-start.19 = (f32[5,16,4,128]{3,2,1,0:T(4,128)S(1)}, f32[5,16,4,128]{3,2,1,0:T(4,128)S(1)}, u32[]{:S(2)}, u32[]{:S(2)}) collective-permute-start(f32[5,16,4,128]{3,2,1,0:T(4,128)S(1)} %pad_maximum_fusion.13), channel_id=1, source_target_pairs={{4,0},{6,4},{2,6},{0,2},{5,1},{7,5},{3,7},{1,3},{12,8},{14,12},{10... | collective-permute-start | bytes 491528 | tf_op jit(solution)/shard_map/ppermute | solution.py:284
  105.2 17.7 %collective-permute-start.22 = (f32[5,4,32,128]{3,2,1,0:T(8,128)S(1)}, f32[5,4,32,128]{3,2,1,0:T(8,128)S(1)}, u32[]{:S(2)}, u32[]{:S(2)}) collective-permute-start(f32[5,4,32,128]{3,2,1,0:T(8,128)S(1)} %get-tuple-element.36), channel_id=1, source_target_pairs={{1,0},{5,4},{7,6},{3,2},{8,1},{12,5},{14,7},{10,3},{9,8},{13,12},{... | collective-permute-start | bytes 983048 | tf_op jit(solution)/shard_map/ppermute | solution.py:275
  107.2 15.8 %collective-permute-start.23 = (f32[5,8,32,128]{3,2,1,0:T(8,128)S(1)}, f32[5,8,32,128]{3,2,1,0:T(8,128)S(1)}, u32[]{:S(2)}, u32[]{:S(2)}) collective-permute-start(f32[5,8,32,128]{3,2,1,0:T(8,128)S(1)} %get-tuple-element.38.refs_1_), channel_id=1, source_target_pairs={{1,0},{5,4},{7,6},{3,2},{8,1},{12,5},{14,7},{10,3},{9,8},{13,12},{... | collective-permute-start | bytes 1966088 | tf_op jit(solution)/shard_map/ppermute | solution.py:275
  110.2 5.8 %collective-permute-start.18 = (f32[5,16,4,128]{3,2,1,0:T(4,128)S(1)}, f32[5,16,4,128]{3,2,1,0:T(4,128)S(1)}, u32[]{:S(2)}, u32[]{:S(2)}) collective-permute-start(f32[5,16,4,128]{3,2,1,0:T(4,128)S(1)} %pad_maximum_fusion.12), channel_id=1, source_target_pairs={{0,4},{4,6},{6,2},{2,0},{1,5},{5,7},{7,3},{3,1},{8,12},{12,14},{14... | collective-permute-start | bytes 491528 | tf_op jit(solution)/shard_map/ppermute | solution.py:283
  116.1 7.6 %collective-permute-start.21 = (f32[5,12,8,128]{3,2,1,0:T(8,128)S(1)}, f32[5,12,8,128]{3,2,1,0:T(8,128)S(1)}, u32[]{:S(2)}, u32[]{:S(2)}) collective-permute-start(f32[5,12,8,128]{3,2,1,0:T(8,128)S(1)} %pad_maximum_fusion.7), channel_id=1, source_target_pairs={{1,0},{5,4},{7,6},{3,2},{8,1},{12,5},{14,7},{10,3},{9,8},{13,12},{... | collective-permute-start | bytes 737288 | tf_op jit(solution)/shard_map/ppermute | solution.py:275
  127.1 19.1 %collective-permute-start.24 = (f32[5,6,32,128]{3,2,1,0:T(8,128)S(1)}, f32[5,6,32,128]{3,2,1,0:T(8,128)S(1)}, u32[]{:S(2)}, u32[]{:S(2)}) collective-permute-start(f32[5,6,32,128]{3,2,1,0:T(8,128)S(1)} %get-tuple-element.42), channel_id=1, source_target_pairs={{0,0},{4,1},{6,2},{2,3},{1,4},{5,5},{7,6},{3,7},{8,8},{12,9},{14,1... | collective-permute-start | bytes 1474568 | tf_op jit(solution)/shard_map/ppermute | solution.py:275
  129.1 17.1 %copy-start = (s32[4,8,32,128]{3,2,1,0:T(8,128)S(1)}, s32[4,8,32,128]{3,2,1,0:T(8,128)}, u32[]{:S(2)}) copy-start(s32[4,8,32,128]{3,2,1,0:T(8,128)} %index.1) | copy-start | bytes 1572868
  132.6 13.7 %collective-permute-start.25 = (f32[5,6,32,128]{3,2,1,0:T(8,128)S(1)}, f32[5,6,32,128]{3,2,1,0:T(8,128)S(1)}, u32[]{:S(2)}, u32[]{:S(2)}) collective-permute-start(f32[5,6,32,128]{3,2,1,0:T(8,128)S(1)} %part.19), channel_id=1, source_target_pairs={{0,0},{4,1},{6,2},{2,3},{1,4},{5,5},{7,6},{3,7},{8,8},{12,9},{14,1... | collective-permute-start | bytes 1474568 | tf_op jit(solution)/shard_map/ppermute | solution.py:275
  136.2 10.0 %collective-permute-start.20 = (f32[5,4,32,128]{3,2,1,0:T(8,128)S(1)}, f32[5,4,32,128]{3,2,1,0:T(8,128)S(1)}, u32[]{:S(2)}, u32[]{:S(2)}) collective-permute-start(f32[5,4,32,128]{3,2,1,0:T(8,128)S(1)} %get-tuple-element.40), channel_id=1, source_target_pairs={{0,0},{4,1},{6,2},{2,3},{1,4},{5,5},{7,6},{3,7},{8,8},{12,9},{14,1... | collective-permute-start | bytes 983048 | tf_op jit(solution)/shard_map/ppermute | solution.py:275
